TPU v7x, 32 devices: a whole 2x2x4 slice. The times are simulated.
32 devices in a mesh: dp: 8 (over z, y), expert: 4 (over x, core).
Axes of the slice: x: 2, y: 2, z: 4, core: 2. Of those that a mesh axis runs over, the one named last changes fastest.
Arguments:
- tokens: bfloat16 [8, 1024, 2048], P('dp', 'expert'), may hold values from -6 to 6
- cotangent: bfloat16 [8, 1024, 2048], P('dp', 'expert'), may hold values from -6 to 6
- attention_routes: int32 [8, 1024, 2], P('dp'), may hold values from 0 to 3, all different within a row; in each aligned block of 256 rows (0 to 255, 256 to 511, ..., all dimensions but the last counted through in order) at most 160 rows name the same one
- feedforward_routes: int32 [8, 1024, 2], P('dp'), may hold values from 0 to 3, all different within a row; in each aligned block of 256 rows (0 to 255, 256 to 511, ..., all dimensions but the last counted through in order) at most 160 rows name the same one
- prefix_length: int32 [8], P('dp'), may hold values from 102 to 512
- gain_attention: float32 [2048], replicated, may hold values from 0.25 to 1.75
- gain_feedforward: float32 [2048], replicated, may hold values from 0.25 to 1.75
- keyvalue_weight: bfloat16 [2048, 4096], P('dp'), may hold values from -0.125 to 0.125
- router_weight: bfloat16 [2048, 8], P('dp'), may hold values from -0.25 to 0.25
- query_weight: bfloat16 [4, 2048, 2048], P('expert', 'dp'), may hold values from -0.125 to 0.125
- output_weight: bfloat16 [4, 2048, 2048], P('expert', 'dp'), may hold values from -3 to 3
- gate_weight: bfloat16 [4, 5632, 2048], P('expert', 'dp'), may hold values from -0.125 to 0.125
- up_weight: bfloat16 [4, 5632, 2048], P('expert', 'dp'), may hold values from -0.125 to 0.125
- down_weight: bfloat16 [4, 5632, 2048], P('expert', 'dp'), may hold values from -0.15625 to 0.15625
Outputs:
- layer_output: bfloat16 [8, 1024, 2048], P('dp', 'expert')
- grad_tokens: float32 [8, 1024, 2048], P('dp', 'expert')
- grad_gain_attention: float32 [2048], P('dp')
- grad_gain_feedforward: float32 [2048], P('dp')
- grad_keyvalue: float32 [2048, 4096], P('dp')
- grad_router: float32 [2048, 8], P('dp')
- grad_query: float32 [4, 2048, 2048], P('expert', 'dp')
- grad_projection: float32 [4, 2048, 2048], P('expert', 'dp')
- grad_gate: float32 [4, 5632, 2048], P('expert', 'dp')
- grad_up: float32 [4, 5632, 2048], P('expert', 'dp')
- grad_down: float32 [4, 5632, 2048], P('expert', 'dp')
Inputs may be any that keep to these rules, and one draw needn't show every extreme that they name: `attention_routes`: the two ids of a token differ. Among the 256 tokens of one device (aligned blocks of each sequence) no expert is named more than 160 times, a bound that some block reaches. `feedforward_routes`: the two ids of a token differ. Among the 256 tokens of one device (aligned blocks of each sequence) no expert is named more than 160 times, a bound that some block reaches.
All inputs are finite; a program needn't handle non-finite values.
Results may differ from a plain program's by a relative error of at most 0.025.
Values may be sent and summed in bfloat16 or wider, within the bound.
A program may use at most 448 MiB of HBM per device.

v0:
```python
import jax
import jax.numpy as jnp
from jax import lax
from jax.sharding import PartitionSpec as P

HEADS = 16
HEAD_DIM = 128


EPS = 1e-06
NEG = -1e30
HIGH = lax.Precision.HIGHEST
ACROSS = (((1,), (1,)), ((), ()))
DOWNWARD = (((0,), (0,)), ((), ()))


def norm_parts(vector, gain_vector):
    factor = lax.rsqrt(jnp.mean(vector * vector, axis=-1, keepdims=True) + EPS)
    normed = vector * factor
    return (normed * gain_vector, normed, factor)


def norm_back(incoming, gain_vector, normed, factor):
    dnormed = incoming * gain_vector
    return factor * (dnormed - normed * jnp.mean(dnormed * normed, axis=-1, keepdims=True))


def route_plan(sequence_ids, my_index, group_size, tok_rows, slot_count):
    expert_range = jnp.arange(group_size, dtype=jnp.int32)
    matches_all = (sequence_ids[:, :, None] == expert_range[None, None, :]).astype(jnp.int32)
    chosen = jnp.sum(matches_all, axis=1).reshape(group_size, tok_rows, group_size)
    ranking = jnp.cumsum(chosen, axis=1) - chosen
    slot_ids = jnp.arange(slot_count, dtype=jnp.int32)[None, :, None]
    block_pick = (expert_range == my_index).astype(jnp.int32)
    my_chosen = jnp.sum(chosen * block_pick[:, None, None], axis=0).T
    my_ranking = jnp.sum(ranking * block_pick[:, None, None], axis=0).T
    send_table = (
        my_chosen[:, None, :] * (my_ranking[:, None, :] == slot_ids).astype(jnp.int32)
    ).astype(jnp.float32)
    column_chosen = jnp.sum(chosen * block_pick[None, None, :], axis=2)
    column_ranking = jnp.sum(ranking * block_pick[None, None, :], axis=2)
    taken = column_chosen[:, None, :] * (column_ranking[:, None, :] == slot_ids).astype(jnp.int32)
    positions = (
        expert_range[:, None, None] * tok_rows
        + jnp.arange(tok_rows, dtype=jnp.int32)[None, None, :]
    )
    arrival_places = jnp.sum(taken * positions, axis=2).reshape(-1)
    my_ids = lax.dynamic_slice_in_dim(sequence_ids, my_index * tok_rows, tok_rows, 0)
    matches = (my_ids[:, :, None] == expert_range[None, None, :]).astype(jnp.float32)
    return (send_table, arrival_places, matches)


def pair_gates(logits, matches):
    selected = jnp.sum(matches * logits[:, None, :], axis=2)
    largest = jnp.max(selected, axis=1, keepdims=True)
    exponent = jnp.exp(selected - largest)
    weights = exponent / jnp.sum(exponent, axis=1, keepdims=True)
    return (weights, jnp.sum(weights[:, :, None] * matches, axis=1))


def gates_back(dgate, weights, matches):
    dweights = jnp.sum(dgate[:, None, :] * matches, axis=2)
    dselected = weights * (dweights - jnp.sum(weights * dweights, axis=1, keepdims=True))
    return jnp.sum(dselected[:, :, None] * matches, axis=1)


def merge_back(send_table, gate_table, returned):
    weighted = send_table * gate_table.T[:, None, :]
    return jnp.einsum("ect,ecd->td", weighted, returned.astype(jnp.float32), precision=HIGH)


def branch_cotangent(send_table, gate_table, returned, incoming):
    spread_grad = jnp.einsum("ect,td->ecd", send_table, incoming, precision=HIGH)
    slot_gate = jnp.sum(send_table * gate_table.T[:, None, :], axis=2)
    cotangent_rows = (spread_grad * slot_gate[:, :, None]).astype(jnp.bfloat16)
    slot_dgate = jnp.sum(spread_grad * returned.astype(jnp.float32), axis=2)
    dgate = jnp.einsum("ect,ec->te", send_table, slot_dgate, precision=HIGH)
    return (cotangent_rows, dgate)


def dispatch(rows):
    return lax.all_to_all(rows, "expert", split_axis=0, concat_axis=0, tiled=True)


def collect(rows):
    return lax.all_to_all(rows, "expert", split_axis=0, concat_axis=0, tiled=True)


def spread_rows(rows):
    return lax.all_gather(rows, "dp", axis=0, tiled=True)


def sum_rows(terms):
    return lax.psum_scatter(
        terms.astype(jnp.bfloat16), "dp", scatter_dimension=0, tiled=True
    ).astype(jnp.float32)


def send_rows(send_table, rows):
    return jnp.einsum(
        "ect,td->ecd", send_table.astype(jnp.bfloat16), rows, preferred_element_type=jnp.float32
    ).astype(jnp.bfloat16)


def per_device(
    tokens,
    cotangent,
    attention_routes,
    feedforward_routes,
    prefix_length,
    gain_attention,
    gain_feedforward,
    keyvalue_weight,
    router_weight,
    query_weight,
    output_weight,
    gate_weight,
    up_weight,
    down_weight,
):
    my_index = lax.axis_index("expert")
    group_size = lax.axis_size("expert")
    inputs = tokens[0].astype(jnp.float32)
    tok_rows = inputs.shape[0]
    model_width = inputs.shape[1]
    seq_total = tok_rows * group_size
    slot_count = 5 * 2 * tok_rows // (4 * group_size)
    query_width = HEADS * HEAD_DIM
    scaling = HEAD_DIM ** (-0.5)
    keyvalue_full, router_full, query_full, output_full = (
        lax.all_gather(keyvalue_weight, "dp", axis=0, tiled=True),
        lax.all_gather(router_weight, "dp", axis=0, tiled=True),
        lax.all_gather(query_weight[0], "dp", axis=0, tiled=True),
        lax.all_gather(output_weight[0], "dp", axis=0, tiled=True),
    )
    attention_cols = router_full[:, :group_size]
    feedforward_cols = router_full[:, group_size:]
    normed_attention, unit_attention, factor_attention = norm_parts(inputs, gain_attention)
    attention_in = normed_attention.astype(jnp.bfloat16)
    keyvalue_rows = jnp.dot(attention_in, keyvalue_full, preferred_element_type=jnp.float32).astype(
        jnp.bfloat16
    )
    keyvalue_seq = lax.all_gather(keyvalue_rows, "expert", axis=0, tiled=True)
    key_rows = keyvalue_seq[:, :query_width].reshape(seq_total, HEADS, HEAD_DIM)
    value_rows = keyvalue_seq[:, query_width:].reshape(seq_total, HEADS, HEAD_DIM)
    attend_table, attend_places, attend_matches = route_plan(
        attention_routes[0], my_index, group_size, tok_rows, slot_count
    )
    attend_logits = jnp.dot(attention_in, attention_cols, preferred_element_type=jnp.float32)
    attend_weights, attend_gate = pair_gates(attend_logits, attend_matches)
    arrived = dispatch(send_rows(attend_table, attention_in)).reshape(-1, model_width)
    queries = jnp.dot(arrived, query_full, preferred_element_type=jnp.float32).astype(jnp.bfloat16)
    queries = queries.reshape(-1, HEADS, HEAD_DIM)
    key_places = jnp.arange(seq_total, dtype=jnp.int32)
    allowed = (key_places[None, :] <= attend_places[:, None]) | (
        key_places[None, :] < prefix_length[0]
    )
    scores = (
        jnp.einsum("rhd,khd->hrk", queries, key_rows, preferred_element_type=jnp.float32) * scaling
    )
    scores = jnp.where(allowed[None], scores, NEG)
    row_max = jnp.max(scores, axis=2, keepdims=True)
    exponent = jnp.exp(scores - row_max)
    row_total = jnp.sum(exponent, axis=2, keepdims=True)
    log_total = row_max + jnp.log(row_total)
    attention_low = (exponent / row_total).astype(jnp.bfloat16)
    mixture = jnp.einsum(
        "hrk,khd->rhd", attention_low, value_rows, preferred_element_type=jnp.float32
    )
    mixture = mixture.astype(jnp.bfloat16).reshape(-1, query_width)
    attend_branch = jnp.dot(mixture, output_full, preferred_element_type=jnp.float32).astype(
        jnp.bfloat16
    )
    attend_returned = collect(attend_branch.reshape(group_size, slot_count, model_width))
    hidden = inputs + merge_back(attend_table, attend_gate, attend_returned)
    normed_feed, unit_feed, factor_feed = norm_parts(hidden, gain_feedforward)
    feed_in = normed_feed.astype(jnp.bfloat16)
    feed_table, _, feed_matches = route_plan(
        feedforward_routes[0], my_index, group_size, tok_rows, slot_count
    )
    feed_logits = jnp.dot(feed_in, feedforward_cols, preferred_element_type=jnp.float32)
    feed_weights, feed_gate = pair_gates(feed_logits, feed_matches)
    feed_rows = dispatch(send_rows(feed_table, feed_in)).reshape(-1, model_width)
    everyone = spread_rows(feed_rows)
    pre_gate = lax.dot_general(everyone, gate_weight[0], ACROSS, preferred_element_type=jnp.float32)
    pre_up = lax.dot_general(everyone, up_weight[0], ACROSS, preferred_element_type=jnp.float32)
    act_low = (pre_gate * jax.nn.sigmoid(pre_gate) * pre_up).astype(jnp.bfloat16)
    feed_branch = sum_rows(
        jnp.dot(act_low, down_weight[0], preferred_element_type=jnp.float32)
    ).astype(jnp.bfloat16)
    feed_returned = collect(feed_branch.reshape(group_size, slot_count, model_width))
    layer_output = hidden + merge_back(feed_table, feed_gate, feed_returned)
    gradient = cotangent[0].astype(jnp.float32)
    feed_cot, feed_dgate = branch_cotangent(feed_table, feed_gate, feed_returned, gradient)
    feed_dlogits = gates_back(feed_dgate, feed_weights, feed_matches)
    feed_cot_rows = dispatch(feed_cot).reshape(-1, model_width)
    cot_everyone = spread_rows(feed_cot_rows)
    sigmoid_gate = jax.nn.sigmoid(pre_gate)
    act_grad = lax.dot_general(
        cot_everyone, down_weight[0], ACROSS, preferred_element_type=jnp.float32
    )
    dgate_low = (act_grad * pre_up * sigmoid_gate * (1.0 + pre_gate * (1.0 - sigmoid_gate))).astype(
        jnp.bfloat16
    )
    dup_low = (act_grad * pre_gate * sigmoid_gate).astype(jnp.bfloat16)
    grad_gate = lax.dot_general(dgate_low, everyone, DOWNWARD, preferred_element_type=jnp.float32)
    grad_up = lax.dot_general(dup_low, everyone, DOWNWARD, preferred_element_type=jnp.float32)
    grad_down = lax.dot_general(act_low, cot_everyone, DOWNWARD, preferred_element_type=jnp.float32)
    feed_dx = sum_rows(
        jnp.dot(dgate_low, gate_weight[0], preferred_element_type=jnp.float32)
        + jnp.dot(dup_low, up_weight[0], preferred_element_type=jnp.float32)
    )
    feed_home = lax.all_to_all(
        feed_dx.reshape(group_size, slot_count, model_width).astype(jnp.bfloat16),
        "expert",
        split_axis=0,
        concat_axis=0,
        tiled=True,
    ).astype(jnp.float32)
    feed_dnorm = jnp.einsum("ect,ecd->td", feed_table, feed_home, precision=HIGH) + jnp.dot(
        feed_dlogits, feedforward_cols.astype(jnp.float32).T, precision=HIGH
    )
    grad_gain_feed = jnp.sum(feed_dnorm * unit_feed, axis=0)
    hidden_grad = gradient + norm_back(feed_dnorm, gain_feedforward, unit_feed, factor_feed)
    attend_cot, attend_dgate = branch_cotangent(
        attend_table, attend_gate, attend_returned, hidden_grad
    )
    attend_dlogits = gates_back(attend_dgate, attend_weights, attend_matches)
    attend_cot_rows = dispatch(attend_cot).reshape(-1, model_width)
    dmixture = lax.dot_general(
        attend_cot_rows, output_full, ACROSS, preferred_element_type=jnp.float32
    )
    dmixture = dmixture.astype(jnp.bfloat16).reshape(-1, HEADS, HEAD_DIM)
    grad_projection = lax.dot_general(
        mixture, attend_cot_rows, DOWNWARD, preferred_element_type=jnp.float32
    )
    scores_again = (
        jnp.einsum("rhd,khd->hrk", queries, key_rows, preferred_element_type=jnp.float32) * scaling
    )
    attention = jnp.where(allowed[None], jnp.exp(scores_again - log_total), 0.0)
    attention_again = attention.astype(jnp.bfloat16)
    dattention = jnp.einsum(
        "rhd,khd->hrk", dmixture, value_rows, preferred_element_type=jnp.float32
    )
    row_dot = jnp.sum(attention * dattention, axis=2, keepdims=True)
    dscores = (attention * (dattention - row_dot)).astype(jnp.bfloat16)
    dqueries = (
        jnp.einsum("hrk,khd->rhd", dscores, key_rows, preferred_element_type=jnp.float32) * scaling
    )
    dqueries = dqueries.astype(jnp.bfloat16).reshape(-1, query_width)
    dkeys = (
        jnp.einsum("hrk,rhd->khd", dscores, queries, preferred_element_type=jnp.float32) * scaling
    )
    dvalues = jnp.einsum(
        "hrk,rhd->khd", attention_again, dmixture, preferred_element_type=jnp.float32
    )
    grad_query = lax.dot_general(arrived, dqueries, DOWNWARD, preferred_element_type=jnp.float32)
    attend_dx = lax.dot_general(dqueries, query_full, ACROSS, preferred_element_type=jnp.float32)
    keyvalue_terms = jnp.concatenate(
        [dkeys.reshape(seq_total, query_width), dvalues.reshape(seq_total, query_width)], axis=1
    ).reshape(group_size, tok_rows, 2 * query_width)
    attend_home, keyvalue_home = (
        lax.all_to_all(
            attend_dx.reshape(group_size, slot_count, model_width).astype(jnp.bfloat16),
            "expert",
            split_axis=0,
            concat_axis=0,
            tiled=True,
        ).astype(jnp.float32),
        lax.all_to_all(
            keyvalue_terms.astype(jnp.bfloat16), "expert", split_axis=0, concat_axis=0, tiled=True
        ).astype(keyvalue_terms.dtype),
    )
    dkeyvalue = jnp.sum(keyvalue_home, axis=0).astype(jnp.bfloat16)
    attend_dnorm = (
        jnp.einsum("ect,ecd->td", attend_table, attend_home, precision=HIGH)
        + lax.dot_general(dkeyvalue, keyvalue_full, ACROSS, preferred_element_type=jnp.float32)
        + jnp.dot(attend_dlogits, attention_cols.astype(jnp.float32).T, precision=HIGH)
    )
    grad_keyvalue = lax.dot_general(
        attention_in, dkeyvalue, DOWNWARD, preferred_element_type=jnp.float32
    )
    grad_router = jnp.concatenate(
        [
            jnp.dot(attention_in.astype(jnp.float32).T, attend_dlogits, precision=HIGH),
            jnp.dot(feed_in.astype(jnp.float32).T, feed_dlogits, precision=HIGH),
        ],
        axis=1,
    )
    grad_gain_attend = jnp.sum(attend_dnorm * unit_attention, axis=0)
    grad_tokens = hidden_grad + norm_back(
        attend_dnorm, gain_attention, unit_attention, factor_attention
    )
    reduced = (
        lax.psum_scatter(
            grad_keyvalue.astype(jnp.bfloat16), "dp", scatter_dimension=0, tiled=True
        ).astype(jnp.float32),
        lax.psum_scatter(
            grad_router.astype(jnp.bfloat16), "dp", scatter_dimension=0, tiled=True
        ).astype(jnp.float32),
        lax.psum_scatter(
            grad_query.astype(jnp.bfloat16), "dp", scatter_dimension=0, tiled=True
        ).astype(jnp.float32),
        lax.psum_scatter(
            grad_projection.astype(jnp.bfloat16), "dp", scatter_dimension=0, tiled=True
        ).astype(jnp.float32),
        lax.psum_scatter(
            grad_gain_attend.astype(jnp.bfloat16), "dp", scatter_dimension=0, tiled=True
        ).astype(jnp.float32),
        lax.psum_scatter(
            grad_gain_feed.astype(jnp.bfloat16), "dp", scatter_dimension=0, tiled=True
        ).astype(jnp.float32),
    )
    shared = (
        lax.psum(reduced[0].astype(jnp.bfloat16), "expert").astype(jnp.float32),
        lax.psum(reduced[1].astype(jnp.bfloat16), "expert").astype(jnp.float32),
        lax.psum(reduced[4].astype(jnp.bfloat16), "expert").astype(jnp.float32),
        lax.psum(reduced[5].astype(jnp.bfloat16), "expert").astype(jnp.float32),
    )
    return (
        layer_output.astype(jnp.bfloat16)[None],
        grad_tokens[None],
        shared[2],
        shared[3],
        shared[0],
        shared[1],
        reduced[2][None],
        reduced[3][None],
        grad_gate[None],
        grad_up[None],
        grad_down[None],
    )


def solution(mesh):
    in_specs = (
        P("dp", "expert", None),
        P("dp", "expert", None),
        P("dp", None, None),
        P("dp", None, None),
        P("dp"),
        P(),
        P(),
        P("dp", None),
        P("dp", None),
        P("expert", "dp", None),
        P("expert", "dp", None),
        P("expert", "dp", None),
        P("expert", "dp", None),
        P("expert", "dp", None),
    )
    out_specs = (
        P("dp", "expert", None),
        P("dp", "expert", None),
        P("dp"),
        P("dp"),
        P("dp", None),
        P("dp", None),
        P("expert", "dp", None),
        P("expert", "dp", None),
        P("expert", "dp", None),
        P("expert", "dp", None),
        P("expert", "dp", None),
    )
    return jax.shard_map(
        per_device, mesh=mesh, in_specs=in_specs, out_specs=out_specs, check_vma=False
    )
```

profile of v0, /device:TPU:2, one launch (start us, length us, event | category | flops | bytes accessed | tf_op | source)
XLA Modules:
  0.0 3379.9 jit_solution(1048255030446471202)
XLA Ops:
  10.3 228.7 %all-gather.9.cloned.1.call-done = bf16[2048,4096]{1,0:T(8,128)(2,1)} async-done(((bf16[256,4096]{1,0:T(8,128)(2,1)}), bf16[2048,4096]{1,0:T(8,128)(2,1)}) %all-gather.9.cloned.1.call-update) | async-done | bytes 16777232 | tf_op jit(solution)/shard_map/all_gather | solution.py:131
  300.5 63.7 %all-gather.17.cloned.1.call-done = bf16[1,2048,2048]{2,1,0:T(8,128)(2,1)} async-done(((bf16[1,256,2048]{2,1,0:T(8,128)(2,1)}), bf16[1,2048,2048]{2,1,0:T(8,128)(2,1)}) %all-gather.17.cloned.1.call-update) | async-done | bytes 8388624 | tf_op jit(solution)/shard_map/all_gather | solution.py:133
  379.5 42.3 %all-gather.11.cloned.1.call-done = bf16[1024,4096]{1,0:T(8,128)(2,1)} async-done(((bf16[256,4096]{1,0:T(8,128)(2,1)}), bf16[1024,4096]{1,0:T(8,128)(2,1)}) %all-gather.11.cloned.1.call-update) | async-done | bytes 8388624 | tf_op jit(solution)/shard_map/all_gather | solution.py:143
  496.4 53.5 %all-gather.19.cloned.1.call-done = bf16[1,2048,2048]{2,1,0:T(8,128)(2,1)} async-done(((bf16[1,256,2048]{2,1,0:T(8,128)(2,1)}), bf16[1,2048,2048]{2,1,0:T(8,128)(2,1)}) %all-gather.19.cloned.1.call-update) | async-done | bytes 8388624 | tf_op jit(solution)/shard_map/all_gather | solution.py:134
  565.1 30.4 all_gather.21
  605.4 33.1 all_to_all.45
  638.5 400.1 %all-gather.13.cloned.1.call-done = bf16[5120,2048]{1,0:T(8,128)(2,1)} async-done(((bf16[640,2048]{1,0:T(8,128)(2,1)}), bf16[5120,2048]{1,0:T(8,128)(2,1)}) %all-gather.13.cloned.1.call-update) | async-done | bytes 20971536 | tf_op jit(solution)/shard_map/all_gather | solution.py:90
  1061.0 29.8 multiply_convert_fusion.3
  1114.2 343.6 %reduce-scatter.7.cloned.1.call-done = bf16[640,2048]{1,0:T(8,128)(2,1)} async-done(((bf16[5120,2048]{1,0:T(8,128)(2,1)}), bf16[640,2048]{1,0:T(8,128)(2,1)}) %reduce-scatter.7.cloned.1.call-update) | async-done | bytes 2621456 | tf_op jit(solution)/shard_map/reduce_scatter | solution.py:94
  1465.1 27.5 all-to-all-done.3
  1503.2 34.6 %all_to_all.46 = bf16[4,160,2048]{2,1,0:T(8,128)(2,1)} all-to-all(bf16[4,160,2048]{2,1,0:T(8,128)(2,1)S(1)} %multiply_convert_fusion.7), channel_id=1, replica_groups=mesh['dp'=8,'expert'=4] {'expert'}, dimensions={0} | all-to-all | bytes 5242880 | tf_op jit(solution)/shard_map/all_to_all | solution.py:82
  1537.9 401.2 %all-gather.15.cloned.1.call-done = bf16[5120,2048]{1,0:T(8,128)(2,1)} async-done(((bf16[640,2048]{1,0:T(8,128)(2,1)}), bf16[5120,2048]{1,0:T(8,128)(2,1)}) %all-gather.15.cloned.1.call-update) | async-done | bytes 20971536 | tf_op jit(solution)/shard_map/all_gather | solution.py:90
  1939.1 42.0 %multiply_convert_fusion.1 = (bf16[5120,704]{0,1:T(8,128)(2,1)}, bf16[5120,704]{0,1:T(8,128)(2,1)}) fusion(f32[5120,704]{0,1:T(8,128)} %fusion.44, f32[5120,704]{0,1:T(8,128)} %get-tuple-element.45, bf16[5120,2048]{1,0:T(8,128)(2,1)} %all-gather.15.cloned.1.call-done, bf16[1,704,2048]{2,1,0:T(8,128)(2,1)S(1)} %copy-done), kind=kOutput, calls=%fused_computation.14 | convolution fusion | flops 14810808320 | bytes 67108864 | tf_op jit(solution)/shard_map/dot_general | solution.py:199
  2008.2 28.7 add_convert_fusion
  2036.9 343.6 %reduce-scatter.9.cloned.1.call-done = bf16[640,2048]{1,0:T(8,128)(2,1)} async-done(((bf16[5120,2048]{1,0:T(8,128)(2,1)}), bf16[640,2048]{1,0:T(8,128)(2,1)}) %reduce-scatter.9.cloned.1.call-update) | async-done | bytes 2621456 | tf_op jit(solution)/shard_map/reduce_scatter | solution.py:94
  2386.1 29.5 all-to-all-done.5
  2437.3 29.6 all-to-all-done.6
  2499.9 35.8 %multiply_reduce_fusion = (f32[16,640]{1,0:T(8,128)S(1)}, f32[16,640,1024]{2,1,0:T(8,128)}) fusion(f32[16,640,1024]{2,1,0:T(8,128)} %get-tuple-element.41, f32[16,640]{1,0:T(8,128)S(1)} %log_add_fusion, pred[640,1024]{1,0:T(8,128)(4,1)S(1)} %copy-done.7, bf16[640,16,128]{0,2,1:T(8,128)(2,1)S(1)} %bitcast.245, bf16[128,16,8,128]{3,2,1,0:T(8,128)(2,1)} %get-tuple-element.36), kind=kOutput, calls=%fused_computation.1 | convolution fusion | flops 2736773120 | bytes 91439104 | tf_op jit(solution)/shard_map/rhd,khd->hrk/dot_general | solution.py:242
  2548.3 34.3 %multiply_convert_fusion = bf16[16,640,1024]{2,1,0:T(8,128)(2,1)} fusion(f32[16,640,1024]{2,1,0:T(8,128)} %get-tuple-element.50, f32[16,640,1024]{2,1,0:T(8,128)} %get-tuple-element.41, f32[16,640]{1,0:T(8,128)S(1)} %get-tuple-element.49, f32[16,640]{1,0:T(8,128)S(1)} %log_add_fusion, pred[640,1024]{1,0:T(8,128)(4,1)S(1)} %copy-done.7), kind=kLoop, calls=%fused_computation | loop fusion | flops 62914560 | bytes 105594880 | tf_op jit(solution)/shard_map/convert_element_type | solution.py:246
  2624.9 89.0 %all-to-all-done.8 = bf16[4,256,4096]{1,2,0:T(8,128)(2,1)} async-done(((bf16[4,256,4096]{1,2,0:T(8,128)(2,1)}), bf16[4,256,4096]{1,2,0:T(8,128)(2,1)}, u32[]{:S(2)}, u32[]{:S(2)}) %all-to-all-start.8) | async-done | bytes 8388640 | tf_op jit(solution)/shard_map/all_to_all | solution.py:270
  2927.7 85.7 %reduce-scatter.11.cloned.1.call-done = bf16[256,4096]{1,0:T(8,128)(2,1)} async-done(((bf16[2048,4096]{1,0:T(8,128)(2,1)}), bf16[256,4096]{1,0:T(8,128)(2,1)}) %reduce-scatter.11.cloned.1.call-update) | async-done | bytes 2097168 | tf_op jit(solution)/shard_map/reduce_scatter | solution.py:295
  3013.5 152.2 %reduce-scatter.17.cloned.1.call-done = bf16[256,2048]{1,0:T(8,128)(2,1)} async-done(((bf16[2048,2048]{1,0:T(8,128)(2,1)}), bf16[256,2048]{1,0:T(8,128)(2,1)}) %reduce-scatter.17.cloned.1.call-update) | async-done | bytes 1048592 | tf_op jit(solution)/shard_map/reduce_scatter | solution.py:304
  3168.6 148.6 %reduce-scatter.15.cloned.1.call-done = bf16[256,2048]{1,0:T(8,128)(2,1)} async-done(((bf16[2048,2048]{1,0:T(8,128)(2,1)}), bf16[256,2048]{1,0:T(8,128)(2,1)}) %reduce-scatter.15.cloned.1.call-update) | async-done | bytes 1048592 | tf_op jit(solution)/shard_map/reduce_scatter | solution.py:301
  3320.0 49.0 %all-reduce.6.cloned.1.call-done = bf16[256,4096]{1,0:T(8,128)(2,1)} async-done(((bf16[256,4096]{1,0:T(8,128)(2,1)}), bf16[256,4096]{1,0:T(8,128)(2,1)}) %all-reduce.6.cloned.1.call-update) | async-done | bytes 2097168 | tf_op jit(solution)/shard_map/psum | solution.py:315
  (314 shorter events, 607.1 us)
Async XLA Ops:
  7.2 1083.7 %copy-start = (bf16[1,704,2048]{2,1,0:T(8,128)(2,1)S(1)}, bf16[1,704,2048]{2,1,0:T(8,128)(2,1)}, u32[]{:S(2)}) copy-start(bf16[1,704,2048]{2,1,0:T(8,128)(2,1)} %param.27) | copy-start | bytes 8650756
  7.2 231.8 %all-gather.9.cloned.1.call-start = ((), (), s32[]{:S(2)}) async-start(), calls=%async_computation.15 | async-start | bytes 18874368 | tf_op jit(solution)/shard_map/all_gather | solution.py:131
  7.9 356.3 %all-gather.17.cloned.1.call-start = ((), (), s32[]{:S(2)}) async-start(), calls=%async_computation.26 | async-start | bytes 9437184 | tf_op jit(solution)/shard_map/all_gather | solution.py:133
  8.7 413.1 %all-gather.11.cloned.1.call-start = ((), (), s32[]{:S(2)}) async-start(), calls=%async_computation.16 | async-start | bytes 10485760 | tf_op jit(solution)/shard_map/all_gather | solution.py:143
  261.9 2153.7 %copy-start.23 = (s32[256,4]{0,1:T(4,128)}, s32[256,4]{0,1:T(4,128)S(1)}, u32[]{:S(2)}) copy-start(s32[256,4]{0,1:T(4,128)S(1)} %get-tuple-element.17) | copy-start | bytes 12292
  261.9 2153.7 %copy-start.25 = (s32[256,4]{0,1:T(4,128)}, s32[256,4]{0,1:T(4,128)S(1)}, u32[]{:S(2)}) copy-start(s32[256,4]{0,1:T(4,128)S(1)} %get-tuple-element.18) | copy-start | bytes 12292
  265.7 34.8 %all-to-all-start = ((bf16[4,160,2048]{2,1,0:T(8,128)(2,1)}), bf16[4,160,2048]{2,1,0:T(8,128)(2,1)}, u32[]{:S(2)}, u32[]{:S(2)}) async-start(bf16[4,160,2048]{2,1,0:T(8,128)(2,1)} %convolution_convert_fusion.6), calls=%async_computation | async-start | bytes 5242880 | tf_op jit(solution)/shard_map/all_to_all | solution.py:82
  270.8 279.1 %all-gather.19.cloned.1.call-start = ((), (), s32[]{:S(2)}) async-start(), calls=%async_computation.27 | async-start | bytes 9437184 | tf_op jit(solution)/shard_map/all_gather | solution.py:134
  559.8 38.2 %all-to-all-start.1 = ((bf16[4,160,2048]{2,1,0:T(8,128)(2,1)}), bf16[4,160,2048]{2,1,0:T(8,128)(2,1)}, u32[]{:S(2)}, u32[]{:S(2)}) async-start(bf16[4,160,2048]{2,1,0:T(8,128)(2,1)} %bitcast.250), calls=%async_computation.1 | async-start | bytes 5242880 | tf_op jit(solution)/shard_map/all_to_all | solution.py:86
  565.1 473.5 %all-gather.13.cloned.1.call-start = ((), (), s32[]{:S(2)}) async-start(), calls=%async_computation.17 | async-start | bytes 23592960 | tf_op jit(solution)/shard_map/all_gather | solution.py:90
  595.5 1824.6 %copy-start.17 = (bf16[2048,8]{0,1:T(8,128)(2,1)}, bf16[2048,8]{0,1:T(8,128)(2,1)S(1)}, u32[]{:S(2)}) copy-start(bf16[2048,8]{0,1:T(8,128)(2,1)S(1)} %all_gather.21) | copy-start | bytes 98308
  638.5 819.3 %reduce-scatter.7.cloned.1.call-start = ((), (), s32[]{:S(2)}) async-start(), calls=%async_computation.18 | async-start | bytes 23592960 | tf_op jit(solution)/shard_map/reduce_scatter | solution.py:94
  1457.7 34.8 %all-to-all-start.3 = ((bf16[4,160,2048]{2,1,0:T(8,128)(2,1)}), bf16[4,160,2048]{2,1,0:T(8,128)(2,1)}, u32[]{:S(2)}, u32[]{:S(2)}) async-start(bf16[4,160,2048]{2,1,0:T(8,128)(2,1)} %bitcast.251), calls=%async_computation.4 | async-start | bytes 5242880 | tf_op jit(solution)/shard_map/all_to_all | solution.py:86
  1462.8 476.3 %all-gather.15.cloned.1.call-start = ((), (), s32[]{:S(2)}) async-start(), calls=%async_computation.19 | async-start | bytes 23592960 | tf_op jit(solution)/shard_map/all_gather | solution.py:90
  1537.8 842.6 %reduce-scatter.9.cloned.1.call-start = ((), (), s32[]{:S(2)}) async-start(), calls=%async_computation.20 | async-start | bytes 23592960 | tf_op jit(solution)/shard_map/reduce_scatter | solution.py:94
  2380.5 35.2 %all-to-all-start.5 = ((bf16[4,160,2048]{2,1,0:T(8,128)(2,1)}), bf16[4,160,2048]{2,1,0:T(8,128)(2,1)}, u32[]{:S(2)}, u32[]{:S(2)}) async-start(bf16[4,160,2048]{2,1,0:T(8,128)(2,1)} %bitcast.252), calls=%async_computation.7 | async-start | bytes 5242880 | tf_op jit(solution)/shard_map/all_to_all | solution.py:213
  2431.4 35.5 %all-to-all-start.6 = ((bf16[4,160,2048]{2,1,0:T(8,128)(2,1)}), bf16[4,160,2048]{2,1,0:T(8,128)(2,1)S(1)}, u32[]{:S(2)}, u32[]{:S(2)}) async-start(bf16[4,160,2048]{2,1,0:T(8,128)(2,1)} %get-tuple-element.39), calls=%async_computation.8 | async-start | bytes 5242880 | tf_op jit(solution)/shard_map/all_to_all | solution.py:82
  2614.9 98.9 %all-to-all-start.8 = ((bf16[4,256,4096]{1,2,0:T(8,128)(2,1)}), bf16[4,256,4096]{1,2,0:T(8,128)(2,1)}, u32[]{:S(2)}, u32[]{:S(2)}) async-start(bf16[4,256,4096]{1,2,0:T(8,128)(2,1)} %pad_maximum_fusion), calls=%async_computation.10 | async-start | bytes 16777216 | tf_op jit(solution)/shard_map/all_to_all | solution.py:270
  2622.3 292.5 %reduce-scatter.13.cloned.1.call-start = ((), (), s32[]{:S(2)}) async-start(), calls=%async_computation.23 | async-start | bytes 36864 | tf_op jit(solution)/shard_map/reduce_scatter | solution.py:298
  2624.8 388.7 %reduce-scatter.11.cloned.1.call-start = ((), (), s32[]{:S(2)}) async-start(), calls=%async_computation.21 | async-start | bytes 18874368 | tf_op jit(solution)/shard_map/reduce_scatter | solution.py:295
  2730.3 435.3 %reduce-scatter.17.cloned.1.call-start = ((), (), s32[]{:S(2)}) async-start(), calls=%async_computation.25 | async-start | bytes 9437184 | tf_op jit(solution)/shard_map/reduce_scatter | solution.py:304
  2743.0 574.2 %reduce-scatter.15.cloned.1.call-start = ((), (), s32[]{:S(2)}) async-start(), calls=%async_computation.24 | async-start | bytes 9437184 | tf_op jit(solution)/shard_map/reduce_scatter | solution.py:301
  2835.2 36.1 %all-to-all-start.7 = ((bf16[4,160,2048]{2,1,0:T(8,128)(2,1)}), bf16[4,160,2048]{2,1,0:T(8,128)(2,1)}, u32[]{:S(2)}, u32[]{:S(2)}) async-start(bf16[4,160,2048]{2,1,0:T(8,128)(2,1)} %fusion.26), calls=%async_computation.9 | async-start | bytes 5242880 | tf_op jit(solution)/shard_map/all_to_all | solution.py:263
  2841.5 527.5 %all-reduce.6.cloned.1.call-start = ((), (), s32[]{:S(2)}) async-start(), calls=%async_computation.22 | async-start | bytes 4194304 | tf_op jit(solution)/shard_map/psum | solution.py:315
  (73 other events, 3550.2 us)
Sparse Core Ops, SparseCore 0:
  10.2 228.8 all-gather.8
  241.2 123.0 all-gather.16
  366.4 55.2 all-gather.10
  423.7 126.0 all-gather.18
  638.6 399.9 all-gather.12
  1114.3 343.3 reduce-scatter.6
  1537.9 401.1 all-gather.14
  2037.0 343.4 reduce-scatter.8
  2626.2 52.7 reduce-scatter.12
  2730.5 282.9 reduce-scatter.10
  3017.5 148.0 reduce-scatter.16
  3169.1 148.0 reduce-scatter.14
  3319.7 49.2 all-reduce.5
where the time goes:
time: 3390 us; the launch traced here: 3380 us
  waiting for transfers between devices  2520 us (74%)
  matrix products  507 us (15%)
  blocking collectives  124 us (4%)
  other arithmetic  101 us (3%)
  local copies, waits for them, and re-layouts  66.5 us (2%)
  starting transfers between devices  41.2 us (1%)
    all_gather x2, waiting for transfers between devices, spread_rows(): return lax.all_gather(rows, 'dp', axis=0, tiled=True)  801 us
    reduce_scatter x2, waiting for transfers between devices, sum_rows(): lax.psum_scatter(terms.astype(jnp.bfloat16), 'dp', scatter_dimension=0, t...  687 us
    all_gather x1, waiting for transfers between devices, per_device(): lax.all_gather(keyvalue_weight, 'dp', axis=0, tiled=True)  229 us
    reduce_scatter x1, waiting for transfers between devices, per_device(): lax.psum_scatter(grad_projection.astype(jnp.bfloat16), 'dp', scatter_dime...  152 us
    reduce_scatter x1, waiting for transfers between devices, per_device(): lax.psum_scatter(grad_query.astype(jnp.bfloat16), 'dp', scatter_dimension...  149 us
    all_to_all x1, waiting for transfers between devices, per_device(): lax.all_to_all(keyvalue_terms.astype(jnp.bfloat16), 'expert', split_axis=...  89 us
    reduce_scatter x1, waiting for transfers between devices, per_device(): lax.psum_scatter(grad_keyvalue.astype(jnp.bfloat16), 'dp', scatter_dimens...  85.7 us
  transfers between devices with their start and end apart: 20, of which 18 were waited for; matrix products, arithmetic and copies ran while one was open for 9% of the time, Pallas kernels for 0%

commit v1 on v0

--- a/solution.py
+++ b/solution.py
@@ -1,6 +1,10 @@
+import functools
+
 import jax
 import jax.numpy as jnp
 from jax import lax
+from jax.experimental import pallas as pl
+from jax.experimental.pallas import tpu as pltpu
 from jax.sharding import PartitionSpec as P
 
 HEADS = 16
@@ -76,6 +80,60 @@
     slot_dgate = jnp.sum(spread_grad * returned.astype(jnp.float32), axis=2)
     dgate = jnp.einsum("ect,ec->te", send_table, slot_dgate, precision=HIGH)
     return (cotangent_rows, dgate)
+
+
+def expert_matches(ids, group_size):
+    expert_range = jnp.arange(group_size, dtype=jnp.int32)
+    return (ids[:, :, None] == expert_range[None, None, :]).astype(jnp.float32)
+
+
+def expert_table(ids, my_index, group_size, tok_rows, slot_count):
+    blocks = ids.reshape(-1, tok_rows, 2)
+    chosen = jnp.sum((blocks == my_index).astype(jnp.float32), axis=2)
+    before = jnp.triu(jnp.ones((tok_rows, tok_rows), jnp.float32), 1)
+    ranking = jnp.dot(chosen, before)
+    slot_ids = jnp.arange(slot_count, dtype=jnp.float32)[None, :, None]
+    taken = chosen[:, None, :] * (ranking[:, None, :] == slot_ids).astype(jnp.float32)
+    other = jnp.sum(blocks, axis=2) - my_index
+    slot_other = jnp.sum(taken * other[:, None, :].astype(jnp.float32), axis=2)
+    return (taken.astype(jnp.bfloat16), slot_other.reshape(-1).astype(jnp.int32))
+
+
+def own_gate(logits, other, my_index):
+    expert_range = jnp.arange(logits.shape[1], dtype=jnp.int32)[None]
+    mine = jnp.sum(jnp.where(expert_range == my_index, logits, 0.0), axis=1, keepdims=True)
+    theirs = jnp.sum(jnp.where(expert_range == other[:, None], logits, 0.0), axis=1, keepdims=True)
+    return jax.nn.sigmoid(mine - theirs)
+
+
+def pick_rows(taken, rows):
+    blocks, slots, tokens = taken.shape
+    picked = jnp.einsum(
+        "bct,btd->bcd",
+        taken,
+        rows.reshape(blocks, tokens, -1),
+        preferred_element_type=jnp.float32,
+    )
+    return picked.astype(jnp.bfloat16).reshape(blocks * slots, -1)
+
+
+def return_rows(taken, rows):
+    blocks, slots, tokens = taken.shape
+    placed = jnp.einsum(
+        "bct,bcd->btd",
+        taken,
+        rows.reshape(blocks, slots, -1),
+        preferred_element_type=jnp.float32,
+    )
+    return placed.astype(jnp.bfloat16).reshape(blocks * tokens, -1)
+
+
+def gather_all(rows):
+    return lax.all_gather(rows, ("dp", "expert"), axis=0, tiled=True)
+
+
+def scatter_all(rows):
+    return lax.psum_scatter(rows, ("dp", "expert"), scatter_dimension=0, tiled=True)
 
 
 def dispatch(rows):
@@ -133,6 +191,8 @@
         lax.all_gather(query_weight[0], "dp", axis=0, tiled=True),
         lax.all_gather(output_weight[0], "dp", axis=0, tiled=True),
     )
+    every_route = lax.all_gather(feedforward_routes[0], "dp", axis=0, tiled=True)
+    cot_everyone = gather_all(cotangent[0])
     attention_cols = router_full[:, :group_size]
     feedforward_cols = router_full[:, group_size:]
     normed_attention, unit_attention, factor_attention = norm_parts(inputs, gain_attention)
@@ -175,49 +235,56 @@
     hidden = inputs + merge_back(attend_table, attend_gate, attend_returned)
     normed_feed, unit_feed, factor_feed = norm_parts(hidden, gain_feedforward)
     feed_in = normed_feed.astype(jnp.bfloat16)
-    feed_table, _, feed_matches = route_plan(
-        feedforward_routes[0], my_index, group_size, tok_rows, slot_count
-    )
+    feed_ids = lax.dynamic_slice_in_dim(
+        feedforward_routes[0], my_index * tok_rows, tok_rows, 0
+    )
+    feed_matches = expert_matches(feed_ids, group_size)
     feed_logits = jnp.dot(feed_in, feedforward_cols, preferred_element_type=jnp.float32)
     feed_weights, feed_gate = pair_gates(feed_logits, feed_matches)
-    feed_rows = dispatch(send_rows(feed_table, feed_in)).reshape(-1, model_width)
-    everyone = spread_rows(feed_rows)
-    pre_gate = lax.dot_general(everyone, gate_weight[0], ACROSS, preferred_element_type=jnp.float32)
-    pre_up = lax.dot_general(everyone, up_weight[0], ACROSS, preferred_element_type=jnp.float32)
-    act_low = (pre_gate * jax.nn.sigmoid(pre_gate) * pre_up).astype(jnp.bfloat16)
-    feed_branch = sum_rows(
-        jnp.dot(act_low, down_weight[0], preferred_element_type=jnp.float32)
-    ).astype(jnp.bfloat16)
-    feed_returned = collect(feed_branch.reshape(group_size, slot_count, model_width))
-    layer_output = hidden + merge_back(feed_table, feed_gate, feed_returned)
-    gradient = cotangent[0].astype(jnp.float32)
-    feed_cot, feed_dgate = branch_cotangent(feed_table, feed_gate, feed_returned, gradient)
-    feed_dlogits = gates_back(feed_dgate, feed_weights, feed_matches)
-    feed_cot_rows = dispatch(feed_cot).reshape(-1, model_width)
-    cot_everyone = spread_rows(feed_cot_rows)
+    everyone = gather_all(feed_in)
+    feed_taken, feed_pairs = expert_table(every_route, my_index, group_size, tok_rows, slot_count)
+    pick = functools.partial(pick_rows, feed_taken)
+    feed_rows = pick(everyone)
+    cot_rows = pick(cot_everyone)
+    row_logits = jnp.dot(feed_rows, feedforward_cols, preferred_element_type=jnp.float32)
+    row_gate = own_gate(row_logits, feed_pairs, my_index)
+    pre_gate = lax.dot_general(feed_rows, gate_weight[0], ACROSS, preferred_element_type=jnp.float32)
+    pre_up = lax.dot_general(feed_rows, up_weight[0], ACROSS, preferred_element_type=jnp.float32)
     sigmoid_gate = jax.nn.sigmoid(pre_gate)
-    act_grad = lax.dot_general(
-        cot_everyone, down_weight[0], ACROSS, preferred_element_type=jnp.float32
-    )
+    act = pre_gate * sigmoid_gate * pre_up
+    act_low = act.astype(jnp.bfloat16)
+    act_scaled = (act * row_gate).astype(jnp.bfloat16)
+    act_grad = lax.dot_general(cot_rows, down_weight[0], ACROSS, preferred_element_type=jnp.float32)
+    slot_dgate = jnp.sum(act_low.astype(jnp.float32) * act_grad, axis=1)
+    act_grad = act_grad * row_gate
     dgate_low = (act_grad * pre_up * sigmoid_gate * (1.0 + pre_gate * (1.0 - sigmoid_gate))).astype(
         jnp.bfloat16
     )
     dup_low = (act_grad * pre_gate * sigmoid_gate).astype(jnp.bfloat16)
-    grad_gate = lax.dot_general(dgate_low, everyone, DOWNWARD, preferred_element_type=jnp.float32)
-    grad_up = lax.dot_general(dup_low, everyone, DOWNWARD, preferred_element_type=jnp.float32)
-    grad_down = lax.dot_general(act_low, cot_everyone, DOWNWARD, preferred_element_type=jnp.float32)
-    feed_dx = sum_rows(
+    feed_dx = (
         jnp.dot(dgate_low, gate_weight[0], preferred_element_type=jnp.float32)
         + jnp.dot(dup_low, up_weight[0], preferred_element_type=jnp.float32)
-    )
-    feed_home = lax.all_to_all(
-        feed_dx.reshape(group_size, slot_count, model_width).astype(jnp.bfloat16),
-        "expert",
-        split_axis=0,
-        concat_axis=0,
-        tiled=True,
-    ).astype(jnp.float32)
-    feed_dnorm = jnp.einsum("ect,ecd->td", feed_table, feed_home, precision=HIGH) + jnp.dot(
+    ).astype(jnp.bfloat16)
+    feed_branch = jnp.dot(act_scaled, down_weight[0], preferred_element_type=jnp.float32).astype(
+        jnp.bfloat16
+    )
+    grad_gate = lax.dot_general(dgate_low, feed_rows, DOWNWARD, preferred_element_type=jnp.float32)
+    grad_up = lax.dot_general(dup_low, feed_rows, DOWNWARD, preferred_element_type=jnp.float32)
+    grad_down = lax.dot_general(act_scaled, cot_rows, DOWNWARD, preferred_element_type=jnp.float32)
+    token_dgate = jnp.einsum(
+        "bct,bc->bt",
+        feed_taken.astype(jnp.float32),
+        slot_dgate.reshape(-1, slot_count),
+        precision=HIGH,
+    ).reshape(-1, 1)
+    own_column = (jnp.arange(group_size) == my_index).astype(jnp.float32)[None]
+    feed_dgate = scatter_all(token_dgate * own_column)
+    feed_home = scatter_all(return_rows(feed_taken, feed_dx)).astype(jnp.float32)
+    feed_sum = scatter_all(return_rows(feed_taken, feed_branch)).astype(jnp.float32)
+    layer_output = hidden + feed_sum
+    gradient = cotangent[0].astype(jnp.float32)
+    feed_dlogits = gates_back(feed_dgate, feed_weights, feed_matches)
+    feed_dnorm = feed_home + jnp.dot(
         feed_dlogits, feedforward_cols.astype(jnp.float32).T, precision=HIGH
     )
     grad_gain_feed = jnp.sum(feed_dnorm * unit_feed, axis=0)
@@ -332,6 +399,792 @@
     )
 
 
+MESH = pl.DeviceIdType.MESH
+CHIPS_Z = 4
+TURNS = ((3, 2, 1, 0), (3, 0, 2, 1), (0, 3, 1, 2), (0, 1, 2, 3))
+
+
+class Place:
+    def __init__(self):
+        self.dp, self.expert = lax.axis_index("dp"), lax.axis_index("expert")
+        self.at = {
+            "z": self.dp // 2,
+            "y": self.dp % 2,
+            "x": self.expert // 2,
+            "c": self.expert % 2,
+        }
+
+    def across(self, axis):
+        back = 1 - 2 * self.at[axis]
+        if axis == "c":
+            return (self.dp, self.expert + back)
+        if axis == "x":
+            return (self.dp, self.expert + 2 * back)
+        return (self.dp + back, self.expert)
+
+    def along(self, step):
+        return (self.dp + 2 * step, self.expert)
+
+    def block(self, whose, z, flips):
+        at = {a: self.at[a] + flips.get(a, 0) * (1 - 2 * self.at[a]) for a in "xyc"}
+        dp, expert = z * 2 + at["y"], at["x"] * 2 + at["c"]
+        return {"all": dp * 4 + expert, "dp": dp, "expert": expert}[whose]
+
+
+def enter(place, axes):
+    barrier, count = pltpu.get_barrier_semaphore(), 0
+    for axis in axes:
+        if axis != "z":
+            pl.semaphore_signal(
+                barrier, inc=1, device_id=place.across(axis), device_id_type=MESH
+            )
+            count += 1
+    if "z" in axes:
+        z = place.at["z"]
+        for step, there in ((-1, z > 0), (1, z < CHIPS_Z - 1)):
+
+            @pl.when(there)
+            def _(step=step):
+                pl.semaphore_signal(
+                    barrier, inc=1, device_id=place.along(step), device_id_type=MESH
+                )
+
+            count = count + there.astype(jnp.int32)
+    pl.semaphore_wait(barrier, count)
+
+
+def on(condition, action):
+    if condition is None:
+        action()
+    else:
+        pl.when(condition)(action)
+
+
+def both(a, b):
+    return b if a is None else a if b is None else a & b
+
+
+class Post:
+    def __init__(self, sems, place):
+        self.sems, self.place, self.sent = sems, place, []
+
+    def send(self, source, target, arrival, device, condition=None):
+        number = len(self.sent)
+
+        def copy():
+            return pltpu.make_async_remote_copy(
+                src_ref=source,
+                dst_ref=target,
+                send_sem=self.sems.at[number],
+                recv_sem=arrival,
+                device_id=device,
+                device_id_type=MESH,
+            )
+
+        self.sent.append((condition, copy))
+        on(condition, lambda: copy().start())
+
+    def arrived(self, target, arrival):
+        pltpu.make_async_remote_copy(
+            src_ref=target,
+            dst_ref=target,
+            send_sem=self.sems.at[0],
+            recv_sem=arrival,
+            device_id=self.place.across("c"),
+            device_id_type=MESH,
+        ).wait_recv()
+
+    def close(self):
+        for condition, copy in self.sent:
+            on(condition, lambda copy=copy: copy().wait_send())
+
+
+FLIPS = {"x": 4, "y": 2, "c": 1}
+
+
+def gather_kernel(jobs, axes, *refs):
+    count = len(jobs)
+    sources, targets = refs[:count], refs[count : 2 * count]
+    send_sems, arrive_sems, own_sems = refs[2 * count :]
+    place = Place()
+    enter(place, axes)
+    post = Post(send_sems, place)
+    z_here = place.at["z"]
+    line = 0
+    waves, owns = {}, []
+    for j, (whose, rows, pieces) in enumerate(jobs):
+        own = pltpu.make_async_copy(
+            sources[j],
+            targets[j].at[pl.ds(place.block(whose, z_here, {}) * rows, rows)],
+            own_sems.at[j],
+        )
+        own.start()
+        owns.append(own)
+        for first, length, order in pieces:
+
+            def part(z, flips, j=j, whose=whose, rows=rows, first=first, length=length):
+                at = place.block(whose, z, flips) * rows + first
+                return targets[j].at[pl.ds(at, length)]
+
+            def mark(z, flips, line=line):
+                return arrive_sems.at[line, z * 8 + sum(FLIPS[a] * v for a, v in flips.items())]
+
+            def hand_on(source, z, flips, depth, side, wave, condition, order=order, part=part, mark=mark):
+                for axis in order[max(depth, 0) :]:
+                    if axis == "z" and (depth < 0 or order[depth] != "z"):
+                        for step in (1, -1):
+                            there = (z_here < CHIPS_Z - 1) if step > 0 else (z_here > 0)
+                            post.send(source, part(z, flips), mark(z, flips), place.along(step), both(condition, there))
+                    elif axis == "z":
+                        there = (z_here < CHIPS_Z - 1) if side > 0 else (z_here > 0)
+                        post.send(source, part(z, flips), mark(z, flips), place.along(side), both(condition, there))
+                    elif depth < 0 or axis != order[depth]:
+                        seen = dict(flips)
+                        seen[axis] = 1
+                        post.send(source, part(z, flips), mark(z, seen), place.across(axis), condition)
+
+            def come(z, flips, depth, side, hops, wave, condition, order=order, part=part, mark=mark, hand_on=hand_on):
+                def act():
+                    on(condition, lambda: post.arrived(part(z, flips), mark(z, flips)))
+                    hand_on(part(z, flips), z, flips, depth, side, wave, condition)
+
+                waves.setdefault(wave, []).append(act)
+                spread(z, flips, depth, side, hops, wave, condition, order, come)
+
+            hand_on(sources[j].at[pl.ds(first, length)], z_here, {}, -1, 0, 0, None)
+            spread(z_here, {}, -1, 0, 0, 0, None, order, come)
+            line += 1
+    for wave in sorted(waves):
+        for act in waves[wave]:
+            act()
+    for own in owns:
+        own.wait()
+    post.close()
+
+
+def spread(z, flips, depth, side, hops, wave, condition, order, come):
+    z_here = lax.axis_index("dp") // 2
+    for later in range(max(depth, 0), len(order)):
+        axis = order[later]
+        if axis == "z":
+            if depth >= 0 and order[depth] == "z":
+                if hops < CHIPS_Z - 1:
+                    far = hops + 1
+                    there = (z_here >= far) if side > 0 else (z_here + far < CHIPS_Z)
+                    come(z_here - side * far, flips, later, side, far, wave + 1, there)
+            else:
+                for step in (1, -1):
+                    there = (z_here >= 1) if step > 0 else (z_here + 1 < CHIPS_Z)
+                    come(z_here - step, flips, later, step, 1, wave + 1, both(condition, there))
+        elif later > depth:
+            seen = dict(flips)
+            seen[axis] = 1
+            come(z, seen, later, 0, 0, wave + 1, condition)
+
+
+def gather(jobs, collective_id, name):
+    arrays = [rows for rows, _, _ in jobs]
+    sizes = {"all": 32, "dp": 8, "expert": 4}
+    plan = tuple((whose, rows.shape[0], pieces) for rows, whose, pieces in jobs)
+    axes = "".join(a for a in "cxyz" if any(a in order for _, _, ps in plan for _, _, order in ps))
+    lines = sum(len(ps) for _, _, ps in plan)
+    any_spec = pl.BlockSpec(memory_space=pltpu.HBM)
+    return pl.pallas_call(
+        functools.partial(gather_kernel, plan, axes),
+        out_shape=[
+            jax.ShapeDtypeStruct((sizes[whose] * r.shape[0], r.shape[1]), r.dtype)
+            for r, whose, _ in jobs
+        ],
+        in_specs=[any_spec] * len(jobs),
+        out_specs=[any_spec] * len(jobs),
+        scratch_shapes=[
+            pltpu.SemaphoreType.DMA((110 * lines,)),
+            pltpu.SemaphoreType.DMA((lines, 32)),
+            pltpu.SemaphoreType.DMA((len(jobs),)),
+        ],
+        compiler_params=pltpu.CompilerParams(
+            collective_id=collective_id, has_side_effects=True
+        ),
+        name=name,
+    )(*arrays)
+
+
+def scatter_kernel(whose, rows, pieces, source, result, acc, *refs):
+    place = Place()
+    orders = [order for _, _, order in pieces]
+    flat = [order.replace("z", "") for order in orders]
+    steps = len(flat[0])
+    lined = "z" in orders[0]
+    turns = CHIPS_Z if lined else 1
+    bins = refs[:steps]
+    line = refs[steps] if lined else None
+    send_sems, load_sems, bin_sems, line_sems = refs[-4:]
+    z_here = place.at["z"]
+    if lined:
+        turn = [
+            sum((z_here == z).astype(jnp.int32) * seq[k] for z, seq in enumerate(TURNS))
+            for k in range(CHIPS_Z)
+        ]
+    else:
+        turn = [z_here]
+    slot_z = lambda k: turn[k] if lined else 0
+    post = Post(send_sems, place)
+
+    def flips_of(p, stage, code):
+        later = flat[p][stage + 1 :]
+        flips = {a: (code >> i) & 1 for i, a in enumerate(later)}
+        if stage < steps:
+            flips[flat[p][stage]] = 1
+        return flips
+
+    def kept(p, flips):
+        names = sorted(flat[p][1:])
+        return sum(flips.get(a, 0) << i for i, a in enumerate(names))
+
+    def code_after(p, stage, flips):
+        return sum(flips.get(a, 0) << i for i, a in enumerate(flat[p][stage + 1 :]))
+
+    keep = 2 ** (steps - 1)
+    names = sorted(flat[0][1:])
+    loads = {}
+    for k in range(turns):
+        for n in reversed(range(keep)):
+            flips = {a: (n >> i) & 1 for i, a in enumerate(names)}
+            at = slot_z(k) * keep + n
+            loads[k, n] = pltpu.make_async_copy(
+                source.at[pl.ds(place.block(whose, turn[k], flips) * rows, rows)],
+                acc.at[at],
+                load_sems.at[at],
+            )
+            loads[k, n].start()
+    enter(place, "".join(flat[0]) + ("z" if lined else ""))
+    loaded = set()
+
+    def add(target, terms, length):
+        @pl.loop(0, length // 16)
+        def _(r):
+            at = pl.ds(pl.multiple_of(r * 16, 16), 16)
+            total = target[at, :].astype(jnp.float32)
+            for term in terms:
+                total = total + term[at, :].astype(jnp.float32)
+            target[at, :] = total.astype(jnp.bfloat16)
+
+    def mine(p, ref):
+        first, length, _ = pieces[p]
+        return ref.at[pl.ds(first, length)]
+
+    def gathered(p, k, stage, flips):
+        n = kept(p, flips)
+        at = slot_z(k) * keep + n
+        if (k, n) not in loaded:
+            loads[k, n].wait()
+            loaded.add((k, n))
+        terms = []
+        for before in range(stage):
+            code = code_after(p, before, flips)
+            width = 2 ** (steps - 1 - before)
+            ref = mine(p, bins[before].at[slot_z(k) * width + code])
+            post.arrived(ref, bin_sems.at[p, before, slot_z(k) * width + code])
+            terms.append(ref)
+        block = mine(p, acc.at[at])
+        add(block, terms, pieces[p][1])
+        return block
+
+    def leave(p, k, stage, code, block, flips):
+        axis = flat[p][stage]
+        width = 2 ** (steps - 1 - stage)
+        at = slot_z(k) * width + code
+        post.send(block, mine(p, bins[stage].at[at]), bin_sems.at[p, stage, at], place.across(axis))
+
+    def work(k, stage):
+        if stage < steps:
+            for code in reversed(range(2 ** (steps - 1 - stage))):
+                for p in range(len(pieces)):
+                    flips = flips_of(p, stage, code)
+                    if stage == 0:
+                        first, length, _ = pieces[p]
+                        at = place.block(whose, turn[k], flips) * rows + first
+                        leave(p, k, stage, code, source.at[pl.ds(at, length)], flips)
+                    else:
+                        leave(p, k, stage, code, gathered(p, k, stage, flips), flips)
+            return
+        for p in range(len(pieces)):
+            block = gathered(p, k, steps, {})
+            if not lined or k == turns - 1:
+                continue
+            t = turn[k]
+            right = t > z_here
+
+            def pass_on(p=p, t=t, block=block):
+                ref = mine(p, line.at[t])
+                post.arrived(ref, line_sems.at[p, t])
+                add(block, [ref], pieces[p][1])
+
+            pl.when((right & (z_here > 0)) | (~right & (z_here < CHIPS_Z - 1)))(pass_on)
+            slot = jnp.where(t == z_here - 1, CHIPS_Z, t)
+            post.send(
+                block,
+                mine(p, line.at[slot]),
+                line_sems.at[p, slot],
+                place.along(jnp.where(right, 1, -1)),
+            )
+
+    for k in range(turns):
+        work(k, 0)
+    for time in range(turns + steps):
+        for stage in range(1, steps + 1):
+            k = time - stage + 1
+            if 0 <= k < turns:
+                work(k, stage)
+    for p in range(len(pieces)):
+        first, length, _ = pieces[p]
+        block = mine(p, acc.at[z_here * keep if lined else 0])
+        if lined:
+            for slot, there in ((z_here, z_here > 0), (CHIPS_Z, z_here < CHIPS_Z - 1)):
+
+                def last(p=p, slot=slot, block=block):
+                    ref = mine(p, line.at[slot])
+                    post.arrived(ref, line_sems.at[p, slot])
+                    add(block, [ref], pieces[p][1])
+
+                pl.when(there)(last)
+
+        @pl.loop(0, length // 16)
+        def _(r, first=first, block=block):
+            at = pl.ds(pl.multiple_of(r * 16, 16), 16)
+            result[pl.ds(pl.multiple_of(first + r * 16, 16), 16), :] = block[at, :].astype(
+                result.dtype
+            )
+
+    post.close()
+
+
+def scatter(array, whose, pieces, collective_id, name, dtype=jnp.float32):
+    size = {"all": 32, "dp": 8, "expert": 4}[whose]
+    rows, width = array.shape[0] // size, array.shape[1]
+    flat = pieces[0][2].replace("z", "")
+    steps, lined = len(flat), "z" in pieces[0][2]
+    turns = CHIPS_Z if lined else 1
+    room = lambda blocks: pltpu.VMEM((blocks, rows, width), jnp.bfloat16)
+    scratch = [room(turns * 2 ** (steps - 1))]
+    scratch += [room(turns * 2 ** (steps - 1 - stage)) for stage in range(steps)]
+    if lined:
+        scratch.append(room(CHIPS_Z + 1))
+    count = len(pieces)
+    scratch += [
+        pltpu.SemaphoreType.DMA((count * (turns * 2**steps + 4),)),
+        pltpu.SemaphoreType.DMA((turns * 2 ** (steps - 1),)),
+        pltpu.SemaphoreType.DMA((count, steps, turns * 2 ** (steps - 1))),
+        pltpu.SemaphoreType.DMA((count, CHIPS_Z + 1)),
+    ]
+    return pl.pallas_call(
+        functools.partial(scatter_kernel, whose, rows, pieces),
+        out_shape=jax.ShapeDtypeStruct((rows, width), dtype),
+        in_specs=[pl.BlockSpec(memory_space=pltpu.HBM)],
+        out_specs=pl.BlockSpec(memory_space=pltpu.VMEM),
+        scratch_shapes=scratch,
+        compiler_params=pltpu.CompilerParams(
+            collective_id=collective_id, has_side_effects=True, vmem_limit_bytes=62 * 2**20
+        ),
+        name=name,
+    )(array)
+
+
+def attention_bias(bias, block, rows, width, prefix):
+    query = block * rows + lax.broadcasted_iota(jnp.int32, (rows, width), 0)
+    key = lax.broadcasted_iota(jnp.int32, (rows, width), 1)
+    bias[:, :width] = jnp.where((key <= query) | (key < prefix), 0.0, NEG)
+
+
+def pick_expert(ref, lane, experts, span, chosen):
+    total = None
+    for e in range(experts):
+        cols = ref[:, pl.ds(pl.multiple_of(e * span + lane, HEAD_DIM), HEAD_DIM)]
+        term = jnp.where(chosen == e, cols.astype(jnp.float32), 0.0)
+        total = term if total is None else total + term
+    return total.astype(jnp.bfloat16)
+
+
+def key_limits(blocks, rows):
+    return [max((i + 1) * rows, blocks * rows // 2) for i in range(blocks)]
+
+
+def for_each_limit(blocks, rows, body):
+    block = pl.program_id(0)
+    limits = key_limits(blocks, rows)
+    for width in sorted(set(limits)):
+        members = [i for i, limit in enumerate(limits) if limit == width]
+        pl.when((block >= members[0]) & (block <= members[-1]))(lambda width=width: body(width))
+
+
+def attention_kernel(experts, prefix, q, k, v, side, mixed, log_total, bias):
+    rows, span = q.shape[0], k.shape[1]
+    heads = span // HEAD_DIM
+    block = pl.program_id(0)
+    chosen = [side[:, 0:1], side[:, 1:2]]
+    gates = [side[:, 2:3], side[:, 3:4]]
+
+    def body(width):
+        attention_bias(bias, block, rows, width, prefix[0])
+
+        @pl.loop(0, heads)
+        def _(head):
+            lane = head * HEAD_DIM
+            lanes = pl.ds(pl.multiple_of(lane, HEAD_DIM), HEAD_DIM)
+            weighted = []
+            for j in range(2):
+                query = pick_expert(q, lane, experts, span, chosen[j])
+                scores = lax.dot_general(
+                    query, k[:width, lanes], ACROSS, preferred_element_type=jnp.float32
+                )
+                scores = scores * (HEAD_DIM**-0.5) + bias[:, :width]
+                largest = jnp.max(scores, axis=1, keepdims=True)
+                exponent = jnp.exp(scores - largest)
+                total = jnp.sum(exponent, axis=1, keepdims=True)
+                low = (exponent * (1.0 / total)).astype(jnp.bfloat16)
+                out = jnp.dot(low, v[:width, lanes], preferred_element_type=jnp.float32)
+                weighted.append(out * gates[j])
+                at = pl.ds(pl.multiple_of((2 * head + j) * HEAD_DIM, HEAD_DIM), HEAD_DIM)
+                log_total[:, at] = jnp.broadcast_to(
+                    largest + jnp.log(total), (rows, HEAD_DIM)
+                )
+            for e in range(experts):
+                cols = jnp.where(chosen[0] == e, weighted[0], 0.0) + jnp.where(
+                    chosen[1] == e, weighted[1], 0.0
+                )
+                at = pl.ds(pl.multiple_of(e * span + lane, HEAD_DIM), HEAD_DIM)
+                mixed[:, at] = cols.astype(jnp.bfloat16)
+
+    for_each_limit(k.shape[0] // rows, rows, body)
+
+
+def attention(projected, side, prefix, experts, rows):
+    length = projected.shape[0]
+    span = projected.shape[1] // (experts + 2)
+    wide = experts * span
+    return pl.pallas_call(
+        functools.partial(attention_kernel, experts),
+        grid=(length // rows,),
+        in_specs=[
+            pl.BlockSpec(memory_space=pltpu.SMEM),
+            pl.BlockSpec((rows, wide), lambda i: (i, 0)),
+            pl.BlockSpec((length, span), lambda i: (0, experts)),
+            pl.BlockSpec((length, span), lambda i: (0, experts + 1)),
+            pl.BlockSpec((rows, 128), lambda i: (i, 0)),
+        ],
+        out_specs=[
+            pl.BlockSpec((rows, wide), lambda i: (i, 0)),
+            pl.BlockSpec((rows, 2 * span), lambda i: (i, 0)),
+        ],
+        out_shape=[
+            jax.ShapeDtypeStruct((length, wide), jnp.bfloat16),
+            jax.ShapeDtypeStruct((length, 2 * span), jnp.float32),
+        ],
+        scratch_shapes=[pltpu.VMEM((rows, length), jnp.float32)],
+        compiler_params=pltpu.CompilerParams(vmem_limit_bytes=48 * 2**20),
+        name="attention",
+    )(prefix, projected, projected, projected, side)
+
+
+def attention_back_kernel(
+    experts, prefix, q, k, v, side, log_total, dmix, dprojected, dgate, bias, dk, dv
+):
+    rows, span = q.shape[0], k.shape[1]
+    length = k.shape[0]
+    heads = span // HEAD_DIM
+    block = pl.program_id(0)
+    scaling = HEAD_DIM**-0.5
+    chosen = [side[:, 0:1], side[:, 1:2]]
+    gates = [side[:, 2:3], side[:, 3:4]]
+    row_at = pl.ds(pl.multiple_of(block * rows, rows), rows)
+    column = lax.broadcasted_iota(jnp.int32, (rows, 128), 1)
+
+    @pl.when(block == 0)
+    def _():
+        dk[...] = jnp.zeros_like(dk)
+        dv[...] = jnp.zeros_like(dv)
+
+    dgate[...] = jnp.zeros_like(dgate)
+
+    def body(width):
+        attention_bias(bias, block, rows, width, prefix[0])
+
+        @pl.loop(0, heads)
+        def _(head):
+            lane = head * HEAD_DIM
+            lanes = pl.ds(pl.multiple_of(lane, HEAD_DIM), HEAD_DIM)
+            keys, values = k[:width, lanes], v[:width, lanes]
+            dqueries = []
+            for j in range(2):
+                query = pick_expert(q, lane, experts, span, chosen[j])
+                dm = pick_expert(dmix, lane, experts, span, chosen[j])
+                at = pl.ds(pl.multiple_of((2 * head + j) * HEAD_DIM, HEAD_DIM), HEAD_DIM)
+                logs = jnp.tile(log_total[:, at], (1, width // HEAD_DIM))
+                scores = lax.dot_general(query, keys, ACROSS, preferred_element_type=jnp.float32)
+                probs = jnp.exp(scores * scaling + bias[:, :width] - logs)
+                dprobs = lax.dot_general(dm, values, ACROSS, preferred_element_type=jnp.float32)
+                inner = jnp.sum(probs * dprobs, axis=1, keepdims=True)
+                dgate[...] += jnp.where(column == j, inner, 0.0)
+                probs = probs * gates[j]
+                dscores = (probs * (dprobs - inner)).astype(jnp.bfloat16)
+                low = probs.astype(jnp.bfloat16)
+                dquery = jnp.dot(dscores, keys, preferred_element_type=jnp.float32) * scaling
+                dqueries.append(dquery)
+                dk[:width, lanes] += lax.dot_general(
+                    dscores, query, DOWNWARD, preferred_element_type=jnp.float32
+                )
+                dv[:width, lanes] += lax.dot_general(
+                    low, dm, DOWNWARD, preferred_element_type=jnp.float32
+                )
+            for e in range(experts):
+                cols = jnp.where(chosen[0] == e, dqueries[0], 0.0) + jnp.where(
+                    chosen[1] == e, dqueries[1], 0.0
+                )
+                at = pl.ds(pl.multiple_of(e * span + lane, HEAD_DIM), HEAD_DIM)
+                dprojected[row_at, at] = cols.astype(jnp.bfloat16)
+
+    for_each_limit(length // rows, rows, body)
+
+    @pl.when(block == pl.num_programs(0) - 1)
+    def _():
+        dprojected[:, experts * span : (experts + 1) * span] = (dk[...] * scaling).astype(
+            jnp.bfloat16
+        )
+        dprojected[:, (experts + 1) * span :] = dv[...].astype(jnp.bfloat16)
+
+
+def attention_back(projected, side, prefix, log_total, dmix, experts, rows):
+    length, total = projected.shape
+    span = total // (experts + 2)
+    wide = experts * span
+    return pl.pallas_call(
+        functools.partial(attention_back_kernel, experts),
+        grid=(length // rows,),
+        in_specs=[
+            pl.BlockSpec(memory_space=pltpu.SMEM),
+            pl.BlockSpec((rows, wide), lambda i: (i, 0)),
+            pl.BlockSpec((length, span), lambda i: (0, experts)),
+            pl.BlockSpec((length, span), lambda i: (0, experts + 1)),
+            pl.BlockSpec((rows, 128), lambda i: (i, 0)),
+            pl.BlockSpec((rows, 2 * span), lambda i: (i, 0)),
+            pl.BlockSpec((rows, wide), lambda i: (i, 0)),
+        ],
+        out_specs=[
+            pl.BlockSpec((length, total), lambda i: (0, 0)),
+            pl.BlockSpec((rows, 128), lambda i: (i, 0)),
+        ],
+        out_shape=[
+            jax.ShapeDtypeStruct((length, total), jnp.bfloat16),
+            jax.ShapeDtypeStruct((length, 128), jnp.float32),
+        ],
+        scratch_shapes=[
+            pltpu.VMEM((rows, length), jnp.float32),
+            pltpu.VMEM((length, span), jnp.float32),
+            pltpu.VMEM((length, span), jnp.float32),
+        ],
+        compiler_params=pltpu.CompilerParams(vmem_limit_bytes=56 * 2**20),
+        name="attention_back",
+    )(prefix, projected, projected, projected, side, log_total, dmix)
+
+
+def per_device_torus(
+    tokens,
+    cotangent,
+    attention_routes,
+    feedforward_routes,
+    prefix_length,
+    gain_attention,
+    gain_feedforward,
+    keyvalue_weight,
+    router_weight,
+    query_weight,
+    output_weight,
+    gate_weight,
+    up_weight,
+    down_weight,
+):
+    my_index = lax.axis_index("expert")
+    group_size = lax.axis_size("expert")
+    dp_size = lax.axis_size("dp")
+    inputs = tokens[0].astype(jnp.float32)
+    tok_rows, model_width = inputs.shape
+    slot_count = 5 * 2 * tok_rows // (4 * group_size)
+    query_width = HEADS * HEAD_DIM
+    span = query_width // group_size
+    low = jnp.bfloat16
+    f32 = jnp.float32
+
+    half = dp_size // group_size
+    swap = [
+        ((z * half + y) * group_size + e, (e * half + y) * group_size + z)
+        for z in range(group_size)
+        for y in range(half)
+        for e in range(group_size)
+    ]
+    cot_everyone = lax.all_gather(cotangent[0], ("dp", "expert"), axis=0, tiled=True)
+    router_full = lax.all_gather(router_weight, "dp", axis=0, tiled=True)
+    every_route = lax.all_gather(feedforward_routes[0], "dp", axis=0, tiled=True)
+    query_cols = lax.all_to_all(query_weight[0], "expert", split_axis=1, concat_axis=1, tiled=True)
+    key_cols = lax.dynamic_slice_in_dim(keyvalue_weight, my_index * span, span, 1)
+    value_cols = lax.dynamic_slice_in_dim(keyvalue_weight, query_width + my_index * span, span, 1)
+    in_shard = jnp.concatenate([query_cols, key_cols, value_cols], axis=1)
+    out_shard = lax.ppermute(output_weight[0], ("dp", "expert"), swap)
+
+    normed_attention, unit_attention, factor_attention = norm_parts(inputs, gain_attention)
+    attention_in = normed_attention.astype(low)
+    quarters = lambda order: tuple(
+        (i * tok_rows // 4, tok_rows // 4, order) for i in range(4)
+    )
+    rows_in = in_shard.shape[0]
+    sequence_in, in_weight, out_weight = gather(
+        [
+            (attention_in, "expert", quarters("xc")),
+            (in_shard, "dp", ((0, rows_in, "zy"),)),
+            (out_shard, "dp", ((0, rows_in, "zy"),)),
+        ],
+        1,
+        "gather_weights",
+    )
+    attention_cols = router_full[:, :group_size]
+    feedforward_cols = router_full[:, group_size:]
+    projected = jnp.dot(sequence_in, in_weight, preferred_element_type=f32).astype(low)
+    attend_matches_all = expert_matches(attention_routes[0], group_size)
+    attend_logits = jnp.dot(sequence_in, attention_cols, preferred_element_type=f32)
+    attend_weights_all, _ = pair_gates(attend_logits, attend_matches_all)
+    side = jnp.concatenate([attention_routes[0].astype(f32), attend_weights_all], axis=1)
+    side = jnp.pad(side, ((0, 0), (0, 128 - side.shape[1])))
+    mixed, log_total = attention(projected, side, prefix_length, group_size, tok_rows)
+    attend_part = jnp.dot(mixed, out_weight, preferred_element_type=f32).astype(low)
+    attended = scatter(attend_part, "expert", quarters("cx"), 2, "sum_attention")
+    hidden = inputs + attended
+    normed_feed, unit_feed, factor_feed = norm_parts(hidden, gain_feedforward)
+    feed_in = normed_feed.astype(low)
+    everywhere = lambda a, b: ((0, tok_rows // 2, a), (tok_rows // 2, tok_rows // 2, b))
+    (everyone,) = gather([(feed_in, "all", everywhere("zxyc", "zyxc"))], 3, "gather_rows")
+
+    mine = lambda a: lax.dynamic_slice_in_dim(a, my_index * tok_rows, tok_rows, 0)
+    feed_matches = expert_matches(mine(feedforward_routes[0]), group_size)
+    feed_logits = jnp.dot(feed_in, feedforward_cols, preferred_element_type=f32)
+    feed_weights, _ = pair_gates(feed_logits, feed_matches)
+    feed_taken, feed_pairs = expert_table(every_route, my_index, group_size, tok_rows, slot_count)
+    feed_rows = pick_rows(feed_taken, everyone)
+    cot_rows = pick_rows(feed_taken, cot_everyone)
+    row_logits = jnp.dot(feed_rows, feedforward_cols, preferred_element_type=f32)
+    row_gate = own_gate(row_logits, feed_pairs, my_index)
+    pre_gate = lax.dot_general(feed_rows, gate_weight[0], ACROSS, preferred_element_type=f32)
+    pre_up = lax.dot_general(feed_rows, up_weight[0], ACROSS, preferred_element_type=f32)
+    sigmoid_gate = jax.nn.sigmoid(pre_gate)
+    act = pre_gate * sigmoid_gate * pre_up
+    act_low = act.astype(low)
+    act_scaled = (act * row_gate).astype(low)
+    act_grad = lax.dot_general(cot_rows, down_weight[0], ACROSS, preferred_element_type=f32)
+    slot_dgate = jnp.sum(act_low.astype(f32) * act_grad, axis=1)
+    act_grad = act_grad * row_gate
+    dgate_low = (act_grad * pre_up * sigmoid_gate * (1.0 + pre_gate * (1.0 - sigmoid_gate))).astype(
+        low
+    )
+    dup_low = (act_grad * pre_gate * sigmoid_gate).astype(low)
+    feed_dx = (
+        jnp.dot(dgate_low, gate_weight[0], preferred_element_type=f32)
+        + jnp.dot(dup_low, up_weight[0], preferred_element_type=f32)
+    ).astype(low)
+    feed_branch = jnp.dot(act_scaled, down_weight[0], preferred_element_type=f32).astype(low)
+    grad_gate = lax.dot_general(dgate_low, feed_rows, DOWNWARD, preferred_element_type=f32)
+    grad_up = lax.dot_general(dup_low, feed_rows, DOWNWARD, preferred_element_type=f32)
+    grad_down = lax.dot_general(act_scaled, cot_rows, DOWNWARD, preferred_element_type=f32)
+    token_dgate = jnp.einsum(
+        "bct,bc->bt", feed_taken.astype(f32), slot_dgate.reshape(-1, slot_count), precision=HIGH
+    )
+    own_row = (jnp.arange(group_size) == my_index).astype(f32)[None, :, None]
+    feed_dgate = lax.psum_scatter(
+        (token_dgate[:, None, :] * own_row).reshape(-1, tok_rows),
+        ("dp", "expert"),
+        scatter_dimension=0,
+        tiled=True,
+    ).T
+    feed_home = scatter(
+        return_rows(feed_taken, feed_dx), "all", everywhere("cxyz", "cyxz"), 4, "sum_rows"
+    )
+    feed_sum = scatter(
+        return_rows(feed_taken, feed_branch), "all", everywhere("cxyz", "cyxz"), 4, "sum_rows"
+    )
+    layer_output = hidden + feed_sum
+    gradient = cotangent[0].astype(f32)
+    feed_dlogits = gates_back(feed_dgate, feed_weights, feed_matches)
+    feed_dnorm = feed_home + jnp.dot(feed_dlogits, feedforward_cols.astype(f32).T, precision=HIGH)
+    grad_gain_feed = jnp.sum(feed_dnorm * unit_feed, axis=0)
+    hidden_grad = gradient + norm_back(feed_dnorm, gain_feedforward, unit_feed, factor_feed)
+
+    (sequence_grad,) = gather(
+        [(hidden_grad.astype(low), "expert", quarters("xc"))], 5, "gather_cotangents"
+    )
+    dmix = lax.dot_general(sequence_grad, out_weight, ACROSS, preferred_element_type=f32).astype(low)
+    grad_out = lax.dot_general(mixed, sequence_grad, DOWNWARD, preferred_element_type=f32)
+    dprojected, gate_parts = attention_back(
+        projected, side, prefix_length, log_total, dmix, group_size, tok_rows
+    )
+    attend_dx = lax.dot_general(dprojected, in_weight, ACROSS, preferred_element_type=f32)
+    grad_in = lax.dot_general(sequence_in, dprojected, DOWNWARD, preferred_element_type=f32)
+    attend_home = scatter(attend_dx.astype(low), "expert", quarters("cx"), 2, "sum_attention")
+    pair_dgate = lax.psum_scatter(
+        gate_parts[:, :2].reshape(group_size, tok_rows, 2).transpose(0, 2, 1).reshape(-1, tok_rows),
+        "expert",
+        scatter_dimension=0,
+        tiled=True,
+    ).T
+    matches = mine(attend_matches_all)
+    weights = mine(attend_weights_all)
+    dselected = weights * (pair_dgate - jnp.sum(weights * pair_dgate, axis=1, keepdims=True))
+    attend_dlogits = jnp.sum(dselected[:, :, None] * matches, axis=1)
+    attend_dnorm = attend_home + jnp.dot(
+        attend_dlogits, attention_cols.astype(f32).T, precision=HIGH
+    )
+    grad_gain_attend = jnp.sum(attend_dnorm * unit_attention, axis=0)
+    grad_tokens = hidden_grad + norm_back(
+        attend_dnorm, gain_attention, unit_attention, factor_attention
+    )
+    small = jnp.concatenate(
+        [
+            lax.dot_general(attend_dlogits, attention_in.astype(f32), DOWNWARD, precision=HIGH),
+            lax.dot_general(feed_dlogits, feed_in.astype(f32), DOWNWARD, precision=HIGH),
+            grad_gain_attend[None],
+            grad_gain_feed[None],
+        ],
+        axis=0,
+    )
+    small = lax.psum(small.astype(f32), ("dp", "expert"))
+    small = lax.dynamic_slice_in_dim(small, lax.axis_index("dp") * rows_in, rows_in, 1)
+
+    down_dp = ((0, rows_in, "yz"),)
+    out_rows = scatter(grad_out.astype(low), "dp", down_dp, 6, "sum_output_weight")
+    in_rows = scatter(grad_in.astype(low), "dp", down_dp, 7, "sum_input_weight").astype(low)
+    grad_projection = lax.ppermute(out_rows.astype(low), ("dp", "expert"), swap).astype(f32)
+    wide = group_size * span
+    grad_query = lax.all_to_all(
+        in_rows[:, :wide], "expert", split_axis=1, concat_axis=1, tiled=True
+    ).astype(f32)
+    grad_keyvalue = lax.all_gather(in_rows[:, wide:], "expert", axis=0, tiled=False)
+    grad_keyvalue = (
+        grad_keyvalue.reshape(group_size, rows_in, 2, span)
+        .transpose(1, 2, 0, 3)
+        .reshape(rows_in, 2 * query_width)
+        .astype(f32)
+    )
+    return (
+        layer_output.astype(low)[None],
+        grad_tokens[None],
+        small[2 * group_size],
+        small[2 * group_size + 1],
+        grad_keyvalue,
+        small[: 2 * group_size].T,
+        grad_query[None],
+        grad_projection[None],
+        grad_gate[None],
+        grad_up[None],
+        grad_down[None],
+    )
+
+
 def solution(mesh):
     in_specs = (
         P("dp", "expert", None),
@@ -362,6 +1215,8 @@
         P("expert", "dp", None),
         P("expert", "dp", None),
     )
+    torus = (mesh.shape["dp"], mesh.shape["expert"]) == (8, 4)
+    body = per_device_torus if torus else per_device
     return jax.shard_map(
-        per_device, mesh=mesh, in_specs=in_specs, out_specs=out_specs, check_vma=False
-    )
+        body, mesh=mesh, in_specs=in_specs, out_specs=out_specs, check_vma=False
+    )

time: 3390 us -> 1900 us (0.56)
  waiting for transfers between devices: 2520 us -> 19.4 us
  Pallas kernels: 0 us -> 1150 us
  other arithmetic: 101 us -> 27.4 us
  matrix products: 507 us -> 463 us
    all_gather x6 -> x2, waiting for transfers between devices: 1190 us -> 0.01 us  [the longest x1 0.01 us: per_device_torus(): lax.all_gather(cotangent[0], ('dp', 'expert'), axis=0, tiled=True)]
    pallas_call x0 -> x11, Pallas kernels: none -> 1150 us  [the longest x6 608 us: scatter(): pl.pallas_call(functools.partial(scatter_kernel, whose, rows, pieces), ou...]
    reduce_scatter x6 -> x0, waiting for transfers between devices: 1070 us -> none  [the longest x2 687 us: sum_rows(): lax.psum_scatter(terms.astype(jnp.bfloat16), 'dp', scatter_dimension=0, t...]
    all_to_all x7 -> x2, waiting for transfers between devices: 210 us -> 17.2 us  [the longest x1 17.2 us: per_device_torus(): lax.all_to_all(in_rows[:, :wide], 'expert', split_axis=1, concat_axis=1,...]
    all_gather x1 -> x2, blocking collectives: 30.4 us -> 129 us  [the longest x1 98.3 us: per_device_torus(): lax.all_gather(feedforward_routes[0], 'dp', axis=0, tiled=True)]
    all_to_all x2 -> x0, blocking collectives: 67.7 us -> none  [dispatch(): lax.all_to_all(rows, 'expert', split_axis=0, concat_axis=0, tiled=True)]
    psum x1, waiting for transfers between devices: 49 us -> 0.01 us  [per_device_torus(): small = lax.psum(small.astype(f32), ('dp', 'expert'))]
    dot_general x40 -> x28, matrix products: 507 us -> 463 us  [the longest x2 53.4 us: pick_rows(): jnp.einsum('bct,btd->bcd', taken, rows.reshape(blocks, tokens, -1), prefe...]
  transfers between devices with their start and end apart: 20 -> 8, of which waited for: 18 -> 2; matrix products, arithmetic and copies ran while one was open for 9% -> 18% of each run, Pallas kernels for 0% -> 55%
where the time goes in v1:
time: 1900 us; the launch traced here: 1890 us
  Pallas kernels  1150 us (61%)
  matrix products  463 us (24%)
  blocking collectives  141 us (7%)
  local copies, waits for them, and re-layouts  50.4 us (3%)
  other arithmetic  27.4 us (1%)
  starting transfers between devices  24.1 us (1%)
  waiting for transfers between devices  19.4 us (1%)
    pallas_call x6, Pallas kernels, scatter(): pl.pallas_call(functools.partial(scatter_kernel, whose, rows, pieces), ou...  608 us
    pallas_call x3, Pallas kernels, gather(): pl.pallas_call(functools.partial(gather_kernel, plan, axes), out_shape=[j...  471 us
    all_gather x1, blocking collectives, per_device_torus(): lax.all_gather(feedforward_routes[0], 'dp', axis=0, tiled=True)  98.3 us
    dot_general x2, matrix products, pick_rows(): jnp.einsum('bct,btd->bcd', taken, rows.reshape(blocks, tokens, -1), prefe...  53.4 us
    dot_general x2, matrix products, return_rows(): jnp.einsum('bct,bcd->btd', taken, rows.reshape(blocks, slots, -1), prefer...  48.5 us
    pallas_call x1, Pallas kernels, attention_back(): pl.pallas_call(functools.partial(attention_back_kernel, experts), grid=(l...  40.1 us
  transfers between devices with their start and end apart: 8, of which 2 were waited for; matrix products, arithmetic and copies ran while one was open for 18% of the time, Pallas kernels for 55%

profile of v1, /device:TPU:2, one launch (start us, length us, event | category | flops | bytes accessed | tf_op | source)
XLA Modules:
  0.0 1888.9 jit_solution(12013078811816144316)
XLA Ops:
  19.6 98.3 %all-gather = s32[1,8192,2]{1,2,0:T(2,128)S(1)} all-gather(s32[1,1024,2]{1,2,0:T(2,128)S(1)} %copy-done.30), channel_id=2, replica_groups=mesh['dp'=8,'expert'=4] {'dp'}, dimensions={1}, use_global_device_ids=true | all-gather | bytes 73728 | tf_op jit(solution)/shard_map/all_gather | solution.py:1026
  124.1 30.8 %all_gather.15 = bf16[2048,8]{0,1:T(8,128)(2,1)S(1)} all-gather(bf16[256,8]{0,1:T(8,128)(2,1)S(1)} %copy-done.32), channel_id=1, replica_groups=mesh['dp'=8,'expert'=4] {'dp'}, dimensions={0}, use_global_device_ids=true | all-gather | bytes 36864 | tf_op jit(solution)/shard_map/all_gather | solution.py:1025
  160.0 286.1 %gather_weights.1 = (bf16[1024,2048]{1,0:T(8,128)(2,1)}, bf16[2048,3072]{1,0:T(8,128)(2,1)}, bf16[2048,2048]{1,0:T(8,128)(2,1)}) custom-call(bf16[256,2048]{1,0:T(8,128)(2,1)} %fusion.31.refs_0_, bf16[256,3072]{1,0:T(8,128)(2,1)} %pad_maximum_fusion.refs_1_, bf16[256,2048]{1,0:T(8,128)(2,1)} %collective-permute-done.refs_2_), custom_call_target="tpu_custom_call" | custom-call | tf_op jit(solution)/shard_map/gather_weights/pallas_call | solution.py:592
  469.5 28.9 %attention.1 = (bf16[1024,2048]{1,0:T(8,128)(2,1)S(1)}, f32[1024,1024]{1,0:T(8,128)}) custom-call(s32[1]{0:T(128)S(6)} %copy.109.prefix, bf16[1024,3072]{1,0:T(8,128)(2,1)} %convolution_convert_fusion.7.q.k.v, bf16[1024,3072]{1,0:T(8,128)(2,1)} %convolution_convert_fusion.7.q.k.v, bf16[1024,3072]{1,0:T(8,128)(2,1)} %convolution_convert_fusion.7.q.k.v, ...), custom_call_target="tpu_custom_call" | custom-call | tf_op jit(solution)/shard_map/attention/pallas_call | solution.py:865
  510.6 27.9 %sum_attention.2 = f32[256,2048]{1,0:T(8,128)} custom-call(bf16[1024,2048]{1,0:T(8,128)(2,1)} %convolution_convert_fusion.10.source), custom_call_target="tpu_custom_call" | custom-call | tf_op jit(solution)/shard_map/sum_attention/pallas_call | solution.py:780
  543.0 144.6 %gather_rows.1 = bf16[8192,2048]{1,0:T(8,128)(2,1)} custom-call(bf16[256,2048]{1,0:T(8,128)(2,1)} %multiply_convert_fusion.5.refs_0_), custom_call_target="tpu_custom_call" | custom-call | tf_op jit(solution)/shard_map/gather_rows/pallas_call | solution.py:592
  687.6 26.7 %convolution_convert_fusion.4 = bf16[32,160,2048]{2,1,0:T(8,128)(2,1)} fusion(bf16[32,256,2048]{2,1,0:T(8,128)(2,1)} %bitcast.132, f32[32,256]{1,0:T(8,128)S(1)} %reduce_sum.195, f32[32,256]{1,0:T(8,128)S(1)} %fusion.40), kind=kOutput, calls=%fused_computation.11 | convolution fusion | flops 5381816320 | bytes 54591488 | tf_op jit(solution)/shard_map/bct,btd->bcd/dot_general | solution.py:111
  727.3 31.1 %fusion.10 = f32[5120,704]{0,1:T(8,128)} fusion(bf16[5120,2048]{1,0:T(8,128)(2,1)S(1)} %bitcast.136, bf16[1,704,2048]{2,1,0:T(8,128)(2,1)} %param.26), kind=kOutput, calls=%fused_computation.37 | convolution fusion | flops 14763950080 | bytes 38273024 | tf_op jit(solution)/shard_map/dot_general | solution.py:1075
  758.4 31.4 %fusion.14 = f32[5120,704]{0,1:T(8,128)} fusion(bf16[5120,2048]{1,0:T(8,128)(2,1)S(1)} %bitcast.137, bf16[1,704,2048]{2,1,0:T(8,128)(2,1)} %param.25), kind=kOutput, calls=%fused_computation.41 | convolution fusion | flops 14763950080 | bytes 38273024 | tf_op jit(solution)/shard_map/dot_general | solution.py:1074
  789.8 23.7 %convolution_convert_fusion.2 = bf16[5120,2048]{1,0:T(8,128)(2,1)} fusion(bf16[1,704,2048]{2,1,0:T(8,128)(2,1)S(1)} %copy-done.34, f32[5120]{0:T(1024)S(1)} %add_divide_fusion.1, f32[5120,704]{0,1:T(8,128)} %fusion.10, f32[5120,704]{0,1:T(8,128)} %fusion.14), kind=kOutput, calls=%fused_computation.3 | convolution fusion | flops 14799667200 | bytes 52711424 | tf_op jit(solution)/shard_map/dot_general | solution.py:1091
  813.6 24.3 %convolution_convert_fusion.1 = bf16[32,256,2048]{2,1,0:T(8,128)(2,1)} fusion(bf16[32,160,2048]{2,1,0:T(8,128)(2,1)} %bitcast.142, f32[32,256]{1,0:T(8,128)S(1)} %reduce_sum.195, f32[32,256]{1,0:T(8,128)S(1)} %fusion.40), kind=kOutput, calls=%fused_computation.2 | convolution fusion | flops 5388107776 | bytes 54591488 | tf_op jit(solution)/shard_map/bct,bcd->btd/dot_general | solution.py:122
  837.8 155.7 %sum_rows.2 = f32[256,2048]{1,0:T(8,128)} custom-call(bf16[8192,2048]{1,0:T(8,128)(2,1)} %bitcast.131), custom_call_target="tpu_custom_call" | custom-call | tf_op jit(solution)/shard_map/sum_rows/pallas_call | solution.py:780
  994.6 26.7 %convolution_convert_fusion.3 = bf16[32,160,2048]{2,1,0:T(8,128)(2,1)} fusion(bf16[32,256,2048]{2,1,0:T(8,128)(2,1)} %bitcast.138, f32[32,256]{1,0:T(8,128)S(1)} %reduce_sum.195, f32[32,256]{1,0:T(8,128)S(1)} %fusion.40), kind=kOutput, calls=%fused_computation.10 | convolution fusion | flops 5381816320 | bytes 54591488 | tf_op jit(solution)/shard_map/bct,btd->bcd/dot_general | solution.py:111
  1021.3 27.6 %convolution_bitcast_fusion = f32[1,704,2048]{2,1,0:T(8,128)} fusion(bf16[5120,2048]{1,0:T(8,128)(2,1)} %bitcast.139, f32[5120]{0:T(1024)S(1)} %add_divide_fusion.1, f32[5120,704]{0,1:T(8,128)} %fusion.10, f32[5120,704]{0,1:T(8,128)} %fusion.14), kind=kOutput, calls=%fused_computation.23 | convolution fusion | flops 14789181440 | bytes 55595008 | tf_op jit(solution)/shard_map/dot_general | solution.py:1094
  1048.8 29.8 %multiply_reduce_fusion = (f32[5120]{0:T(1024)S(1)}, bf16[5120,704]{0,1:T(8,128)(2,1)S(1)}, bf16[5120,704]{0,1:T(8,128)(2,1)}) fusion(f32[5120,704]{0,1:T(8,128)} %fusion.10, f32[5120,704]{0,1:T(8,128)} %fusion.14, f32[5120]{0:T(1024)S(1)} %add_divide_fusion.1, bf16[5120,2048]{1,0:T(8,128)(2,1)} %bitcast.140, bf16[1,704,2048]{2,1,0:T(8,128)(2,1)} %param.27), kind=kOutput, calls=%fused_computation.4 | convolution fusion | flops 14836034560 | bytes 67149824 | tf_op jit(solution)/shard_map/dot_general | solution.py:1080
  1100.9 24.2 %fusion.12 = f32[5120,2048]{1,0:T(8,128)} fusion(bf16[5120,704]{0,1:T(8,128)(2,1)} %copy-done.38, bf16[1,704,2048]{2,1,0:T(8,128)(2,1)S(1)} %copy-done.35), kind=kOutput, calls=%fused_computation.39 | convolution fusion | flops 14763950080 | bytes 52035584 | tf_op jit(solution)/shard_map/dot_general | solution.py:1088
  1149.0 28.8 %add_convert_fusion = bf16[5120,2048]{1,0:T(8,128)(2,1)} fusion(f32[5120,2048]{1,0:T(8,128)} %fusion.12, bf16[5120,704]{0,1:T(8,128)(2,1)} %get-tuple-element.74, bf16[1,704,2048]{2,1,0:T(8,128)(2,1)S(1)} %copy-done.36), kind=kOutput, calls=%fused_computation | convolution fusion | flops 14784921600 | bytes 73007104 | tf_op jit(solution)/shard_map/dot_general | solution.py:1089
  1177.9 24.3 %convolution_convert_fusion = bf16[32,256,2048]{2,1,0:T(8,128)(2,1)} fusion(bf16[32,160,2048]{2,1,0:T(8,128)(2,1)} %bitcast.141, f32[32,256]{1,0:T(8,128)S(1)} %copy-done.13, f32[32,256]{1,0:T(8,128)S(1)} %copy-done.15), kind=kOutput, calls=%fused_computation.1 | convolution fusion | flops 5388107776 | bytes 54591488 | tf_op jit(solution)/shard_map/bct,bcd->btd/dot_general | solution.py:122
  1202.2 155.2 %sum_rows.3 = f32[256,2048]{1,0:T(8,128)} custom-call(bf16[8192,2048]{1,0:T(8,128)(2,1)} %bitcast.130), custom_call_target="tpu_custom_call" | custom-call | tf_op jit(solution)/shard_map/sum_rows/pallas_call | solution.py:780
  1365.8 39.9 %gather_cotangents.1 = bf16[1024,2048]{1,0:T(8,128)(2,1)} custom-call(bf16[256,2048]{1,0:T(8,128)(2,1)} %fusion.64.refs_0_), custom_call_target="tpu_custom_call" | custom-call | tf_op jit(solution)/shard_map/gather_cotangents/pallas_call | solution.py:592
  1419.6 40.1 %attention_back.1 = (bf16[1024,3072]{1,0:T(8,128)(2,1)}, f32[1024,128]{1,0:T(8,128)}) custom-call(s32[1]{0:T(128)S(6)} %copy.109.prefix, bf16[1024,3072]{1,0:T(8,128)(2,1)} %convolution_convert_fusion.7.q.k.v, bf16[1024,3072]{1,0:T(8,128)(2,1)} %convolution_convert_fusion.7.q.k.v, bf16[1024,3072]{1,0:T(8,128)(2,1)} %convolution_convert_fusion.7.q.k.v, ...), custom_call_target="tpu_custom_call" | custom-call | tf_op jit(solution)/shard_map/attention_back/pallas_call | solution.py:960
  1479.6 29.5 %sum_attention.3 = f32[256,2048]{1,0:T(8,128)} custom-call(bf16[1024,2048]{1,0:T(8,128)(2,1)} %convolution_convert_fusion.8.source), custom_call_target="tpu_custom_call" | custom-call | tf_op jit(solution)/shard_map/sum_attention/pallas_call | solution.py:780
  1550.0 145.8 %sum_input_weight.1 = f32[256,3072]{1,0:T(8,128)} custom-call(bf16[2048,3072]{1,0:T(8,128)(2,1)} %convolution_convert_fusion.5.source), custom_call_target="tpu_custom_call" | custom-call | tf_op jit(solution)/shard_map/sum_input_weight/pallas_call | solution.py:780
  1713.9 94.0 %sum_output_weight.1 = f32[256,2048]{1,0:T(8,128)} custom-call(bf16[2048,2048]{1,0:T(8,128)(2,1)} %convolution_convert_fusion.6.source), custom_call_target="tpu_custom_call" | custom-call | tf_op jit(solution)/shard_map/sum_output_weight/pallas_call | solution.py:780
  (195 shorter events, 297.3 us)
Async XLA Ops:
  7.2 111.0 %copy-start.31 = (s32[1,1024,2]{1,2,0:T(2,128)S(1)}, s32[1,1024,2]{1,2,0:T(2,128)}, u32[]{:S(2)}) copy-start(s32[1,1024,2]{1,2,0:T(2,128)} %param.16) | copy-start | bytes 24580
  7.2 112.0 %copy-start.6 = (bf16[1,256,2048]{2,1,0:T(8,128)(2,1)S(1)}, bf16[1,256,2048]{2,1,0:T(8,128)(2,1)}, u32[]{:S(2)}) copy-start(bf16[1,256,2048]{2,1,0:T(8,128)(2,1)} %param.14) | copy-start | bytes 3145732
  7.2 987.4 %all-gather.6.cloned.1.call-start = ((), (), s32[]{:S(2)}) async-start(), calls=%async_computation.3 | async-start | bytes 34603008 | tf_op jit(solution)/shard_map/all_gather | solution.py:1024
  7.9 114.2 %copy-start.37 = (u32[32]{0:T(128)S(1)}, u32[32]{0:T(128)}, u32[]{:S(2)}) copy-start(u32[32]{0:T(128)} %constant.65) | copy-start | bytes 388
  8.0 116.2 %copy-start.32 = (bf16[256,8]{0,1:T(8,128)(2,1)S(1)}, bf16[256,8]{0,1:T(8,128)(2,1)}, u32[]{:S(2)}) copy-start(bf16[256,8]{0,1:T(8,128)(2,1)} %param.22) | copy-start | bytes 12292
  9.5 146.6 %copy-start.22 = (f32[2048]{0:T(1024)S(1)}, f32[2048]{0:T(1024)}, u32[]{:S(2)}) copy-start(f32[2048]{0:T(1024)} %param.19) | copy-start | bytes 24580
  10.8 146.5 %all-to-all-start = ((bf16[256,4,512]{2,0,1:T(8,128)(2,1)}), bf16[256,4,512]{2,0,1:T(8,128)(2,1)}, u32[]{:S(2)}, u32[]{:S(2)}) async-start(bf16[256,4,512]{2,0,1:T(8,128)(2,1)} %copy.82), calls=%async_computation | async-start | bytes 2097152 | tf_op jit(solution)/shard_map/all_to_all | solution.py:1027
  15.0 1342.4 %all-reduce.8.cloned.1.call-start = ((), (), s32[]{:S(2)}) async-start(), calls=%async_computation.5 | async-start | bytes 262144
  15.1 144.9 %collective-permute-start = (bf16[256,2048]{1,0:T(8,128)(2,1)}, bf16[256,2048]{1,0:T(8,128)(2,1)}, u32[]{:S(2)}, u32[]{:S(2)}) collective-permute-start(bf16[256,2048]{1,0:T(8,128)(2,1)} %bitcast.158), channel_id=1, source_target_pairs={{0,0},{1,8},{2,16},{3,24},{4,4},{5,12},{6,20},{7,28},{8,1},{9,9},{... | collective-permute-start | bytes 3145736 | tf_op jit(solution)/shard_map/ppermute | solution.py:1031
  118.1 876.5 %copy-start.12 = (f32[32,256]{1,0:T(8,128)}, f32[32,256]{1,0:T(8,128)S(1)}, u32[]{:S(2)}) copy-start(f32[32,256]{1,0:T(8,128)S(1)} %reduce_sum.195) | copy-start | bytes 98308
  119.5 326.6 %copy-start.28 = (f32[256]{0:T(256)}, f32[256]{0:T(256)S(1)}, u32[]{:S(2)}) copy-start(f32[256]{0:T(256)S(1)} %add_rsqrt_fusion.1) | copy-start | bytes 3076
  120.2 874.3 %copy-start.14 = (f32[32,256]{1,0:T(8,128)}, f32[32,256]{1,0:T(8,128)S(1)}, u32[]{:S(2)}) copy-start(f32[32,256]{1,0:T(8,128)S(1)} %fusion.40) | copy-start | bytes 98308
  154.9 838.6 %copy-start.18 = (bf16[2048,8]{0,1:T(8,128)(2,1)}, bf16[2048,8]{0,1:T(8,128)(2,1)S(1)}, u32[]{:S(2)}) copy-start(bf16[2048,8]{0,1:T(8,128)(2,1)S(1)} %all_gather.15) | copy-start | bytes 98308
  837.8 155.8 %copy-start.9 = (bf16[256,2048]{1,0:T(8,128)(2,1)S(1)}, bf16[256,2048]{1,0:T(8,128)(2,1)}, u32[]{:S(2)}) copy-start(bf16[256,2048]{1,0:T(8,128)(2,1)} %multiply_convert_fusion.5.refs_0_) | copy-start | bytes 3145732
  1127.4 707.6 %all-reduce.6.cloned.1.call-start = ((), (), s32[]{:S(2)}) async-start(), calls=%async_computation.2 | async-start | bytes 262144 | tf_op jit(solution)/shard_map/psum | solution.py:1155
  1202.1 156.1 %copy-start.26 = (s32[256,2]{0,1:T(2,128)S(1)}, s32[256,2]{0,1:T(2,128)}, u32[]{:S(2)}) copy-start(s32[256,2]{0,1:T(2,128)} %dynamic-slice_bitcast_fusion.3) | copy-start | bytes 6148
  1202.1 156.1 %copy-start.27 = (f32[256,4]{0,1:T(4,128)S(1)}, f32[256,4]{0,1:T(4,128)}, u32[]{:S(2)}) copy-start(f32[256,4]{0,1:T(4,128)} %fusion.50) | copy-start | bytes 12292
  1202.2 156.2 %copy-start.10 = (bf16[256,2048]{1,0:T(8,128)(2,1)S(1)}, bf16[256,2048]{1,0:T(8,128)(2,1)}, u32[]{:S(2)}) copy-start(bf16[256,2048]{1,0:T(8,128)(2,1)} %multiply_convert_fusion.5.refs_0_) | copy-start | bytes 3145732
  1202.2 156.8 %copy-start.19 = (bf16[2048,8]{0,1:T(8,128)(2,1)S(1)}, bf16[2048,8]{0,1:T(8,128)(2,1)}, u32[]{:S(2)}) copy-start(bf16[2048,8]{0,1:T(8,128)(2,1)} %copy-done.18) | copy-start | bytes 98308
  1202.2 156.8 %copy-start.21 = (f32[2048]{0:T(1024)S(1)}, f32[2048]{0:T(1024)}, u32[]{:S(2)}) copy-start(f32[2048]{0:T(1024)} %param.20) | copy-start | bytes 24580
  1202.2 156.8 %copy-start.25 = (f32[256]{0:T(256)S(1)}, f32[256]{0:T(256)}, u32[]{:S(2)}) copy-start(f32[256]{0:T(256)} %copy-done.24) | copy-start | bytes 3076
  1530.3 332.4 %all-gather.8.cloned.1.call-start = ((), (), s32[]{:S(2)}) async-start(), calls=%async_computation.4 | async-start | bytes 2621440 | tf_op jit(solution)/shard_map/all_gather | solution.py:1166
  1810.9 49.1 %collective-permute-start.1 = (bf16[256,2048]{1,0:T(8,128)(2,1)}, bf16[256,2048]{1,0:T(8,128)(2,1)}, u32[]{:S(2)}, u32[]{:S(2)}) collective-permute-start(bf16[256,2048]{1,0:T(8,128)(2,1)} %convert_element_type.194), channel_id=1, source_target_pairs={{0,0},{1,8},{2,16},{3,24},{4,4},{5,12},{6,20},{7,28},{8,1},{9,9},{... | collective-permute-start | bytes 3145736 | tf_op jit(solution)/shard_map/ppermute | solution.py:1161
  1817.9 37.0 %all-to-all-start.1 = ((bf16[256,4,512]{2,0,1:T(8,128)(2,1)}), bf16[256,4,512]{2,0,1:T(8,128)(2,1)}, u32[]{:S(2)}, u32[]{:S(2)}) async-start(bf16[256,4,512]{2,0,1:T(8,128)(2,1)} %bitcast.146), calls=%async_computation.1 | async-start | bytes 2097152 | tf_op jit(solution)/shard_map/all_to_all | solution.py:1163
  (25 other events, 539.2 us)
Sparse Core Ops, SparseCore 0:
  10.9 290.3 all-gather.5
  1127.5 123.6 all-reduce.7
  1530.5 127.1 all-reduce.5
  1698.9 21.2 all-gather.7

commit v2 on v1

--- a/solution.py
+++ b/solution.py
@@ -987,6 +987,352 @@
     )(prefix, projected, projected, projected, side, log_total, dmix)
 
 
+NEAREST = ((0, 1, 2, 3), (1, 2, 0, 3), (2, 1, 3, 0), (3, 2, 1, 0))
+
+
+def expert_slots(ids, my_index, tok_rows):
+    blocks = ids.reshape(-1, tok_rows, 2)
+    chosen = jnp.sum((blocks == my_index).astype(jnp.float32), axis=2)
+    before = jnp.triu(jnp.ones((tok_rows, tok_rows), jnp.float32), 1)
+    slots = jnp.where(chosen > 0, jnp.dot(chosen, before), -1.0).astype(jnp.int32)
+    return slots, jnp.sum(blocks, axis=2) - my_index
+
+
+def feed_kernel(
+    tok,
+    slot_count,
+    own_rows,
+    cots,
+    gate_weight,
+    up_weight,
+    down_weight,
+    router_rows,
+    slots,
+    others,
+    everyone,
+    dx_part,
+    out_part,
+    x_kept,
+    g_kept,
+    d_kept,
+    a_kept,
+    dgate,
+    w_in,
+    w_down,
+    rows_buf,
+    cots_buf,
+    xs,
+    gs,
+    pre,
+    back,
+    ds,
+    acts,
+    dx_buf,
+    out_buf,
+    send_sems,
+    arrive_sems,
+    own_sem,
+    weight_sems,
+    load_sems,
+    keep_sems,
+):
+    place = Place()
+    z_here = place.at["z"]
+    hidden = gate_weight.shape[0]
+    padded = w_down.shape[0]
+    width = own_rows.shape[1]
+    half = tok // 2
+    chips = 4 * CHIPS_Z
+    pair = 2 * slot_count
+    f32, low = jnp.float32, jnp.bfloat16
+
+    loads = [
+        pltpu.make_async_copy(gate_weight, w_in.at[pl.ds(0, hidden)], weight_sems.at[0]),
+        pltpu.make_async_copy(
+            router_rows, w_in.at[pl.ds(hidden, padded - hidden)], weight_sems.at[1]
+        ),
+        pltpu.make_async_copy(up_weight, w_in.at[pl.ds(padded, hidden)], weight_sems.at[2]),
+        pltpu.make_async_copy(down_weight, w_down.at[pl.ds(0, hidden)], weight_sems.at[3]),
+        pltpu.make_async_copy(
+            own_rows, everyone.at[pl.ds(place.block("all", z_here, {}) * tok, tok)], own_sem
+        ),
+    ]
+    for load in loads:
+        load.start()
+    w_in[padded + hidden :, :] = jnp.zeros((padded - hidden, width), low)
+    w_down[hidden:, :] = jnp.zeros((padded - hidden, width), low)
+    enter(place, "cxyz")
+
+    def chip(u):
+        k, xr, yr = u // 4, u % 2, (u // 2) % 2
+        z = sum(
+            ((z_here == at) & (k == i)).astype(jnp.int32) * seq[i]
+            for at, seq in enumerate(NEAREST)
+            for i in range(CHIPS_Z)
+        )
+        return z, xr, yr
+
+    def first_block(u):
+        z, xr, yr = chip(u)
+        x = place.at["x"] + xr * (1 - 2 * place.at["x"])
+        y = place.at["y"] + yr * (1 - 2 * place.at["y"])
+        return (z * 2 + y) * 4 + x * 2
+
+    def part(p, u, core):
+        return everyone.at[pl.ds((first_block(u) + core) * tok + p * half, half)]
+
+    def remote(source, target, number, mark, device):
+        return pltpu.make_async_remote_copy(
+            src_ref=source,
+            dst_ref=target,
+            send_sem=send_sems.at[number],
+            recv_sem=arrive_sems.at[mark],
+            device_id=device,
+            device_id_type=MESH,
+        )
+
+    def routes(u, p):
+        z, xr, yr = chip(u)
+        plain = (xr + yr) == 0
+        mark = (p * CHIPS_Z + z) * 8
+        here = xr * 4 + yr * 2
+        base = (u * 2 + p) * 5
+        own = z == z_here
+        right = plain & (z <= z_here) & (z_here < CHIPS_Z - 1)
+        left = plain & (z >= z_here) & (z_here > 0)
+        over_x = plain if p == 0 else xr == 0
+        over_y = yr == 0 if p == 0 else plain
+        return [
+            (right, base, mark, place.along(1)),
+            (left, base + 1, mark, place.along(-1)),
+            (over_x, base + 2, mark + 4 + yr * 2, place.across("x")),
+            (over_y, base + 3, mark + xr * 4 + 2, place.across("y")),
+            (None, base + 4, mark + here + 1, place.across("c")),
+        ]
+
+    def hand_on(u, sources):
+        for p in range(2):
+            for condition, number, mark, device in routes(u, p):
+                target = part(p, u, place.at["c"])
+                source = target if sources is None else sources[p]
+                on(
+                    condition,
+                    lambda source=source, target=target, number=number, mark=mark, device=device: remote(
+                        source, target, number, mark, device
+                    ).start(),
+                )
+
+    def sibling_came(u):
+        z, xr, yr = chip(u)
+        for p in range(2):
+            ref = part(p, u, 1 - place.at["c"])
+            mark = (p * CHIPS_Z + z) * 8 + xr * 4 + yr * 2 + 1
+            remote(ref, ref, 0, mark, place.across("c")).wait_recv()
+
+    def take_in(u):
+        z, xr, yr = chip(u)
+        for p in range(2):
+            ref = part(p, u, place.at["c"])
+            mark = (p * CHIPS_Z + z) * 8 + xr * 4 + yr * 2
+            remote(ref, ref, 0, mark, place.across("c")).wait_recv()
+        hand_on(u, None)
+        sibling_came(u)
+
+    def fetch(u):
+        at = pl.ds(first_block(u) * tok, 2 * tok)
+        return [
+            pltpu.make_async_copy(everyone.at[at], rows_buf.at[u % 2], load_sems.at[u % 2, 0]),
+            pltpu.make_async_copy(cots.at[at], cots_buf.at[u % 2], load_sems.at[u % 2, 1]),
+        ]
+
+    def keep(u):
+        rows = pl.ds(u * pair, pair)
+        blocks = pl.ds(first_block(u) * tok, 2 * tok)
+        s = u % 2
+        return [
+            pltpu.make_async_copy(xs.at[s], x_kept.at[rows], keep_sems.at[s, 0]),
+            pltpu.make_async_copy(gs.at[s], g_kept.at[rows], keep_sems.at[s, 1]),
+            pltpu.make_async_copy(ds.at[s], d_kept.at[rows], keep_sems.at[s, 2]),
+            pltpu.make_async_copy(acts.at[s], a_kept.at[rows], keep_sems.at[s, 3]),
+            pltpu.make_async_copy(dx_buf.at[s], dx_part.at[blocks], keep_sems.at[s, 4]),
+            pltpu.make_async_copy(out_buf.at[s], out_part.at[blocks], keep_sems.at[s, 5]),
+        ]
+
+    hand_on(0, [own_rows.at[pl.ds(0, half)], own_rows.at[pl.ds(half, half)]])
+    loads[4].wait()
+    sibling_came(0)
+    for copy in fetch(0):
+        copy.start()
+    take_in(1)
+    for load in loads[:4]:
+        load.wait()
+
+    def compute(u):
+        s = u % 2
+        block = first_block(u)
+        spread = []
+        for b in range(2):
+            row = slots[pl.ds(block + b, 1), :]
+            table = lax.broadcasted_iota(jnp.int32, (slot_count, tok), 0) == row
+            table = table.astype(f32)
+            spread.append(table)
+            at = pl.ds(b * slot_count, slot_count)
+            from_rows = pl.ds(b * tok, tok)
+            xs[s, at, :] = jnp.dot(
+                table.astype(low), rows_buf[s, from_rows, :], preferred_element_type=f32
+            ).astype(low)
+            gs[s, at, :] = jnp.dot(
+                table.astype(low), cots_buf[s, from_rows, :], preferred_element_type=f32
+            ).astype(low)
+
+        @pl.loop(0, 2 * padded // 256)
+        def _(n):
+            at = pl.ds(pl.multiple_of(n * 256, 256), 256)
+            pre[:, at] = lax.dot_general(xs[s], w_in[at, :], ACROSS, preferred_element_type=f32)
+
+        @pl.loop(0, padded // 256)
+        def _(n):
+            at = pl.ds(pl.multiple_of(n * 256, 256), 256)
+            back[:, at] = lax.dot_general(gs[s], w_down[at, :], ACROSS, preferred_element_type=f32)
+
+        for b in range(2):
+            at = pl.ds(b * slot_count, slot_count)
+            last = pre[at, padded - 128 : padded]
+            column = lax.broadcasted_iota(jnp.int32, (slot_count, 128), 1) - (
+                hidden - (padded - 128)
+            )
+            other = jnp.sum(
+                spread[b] * others[pl.ds(block + b, 1), :].astype(f32), axis=1, keepdims=True
+            )
+            mine = jnp.sum(jnp.where(column == place.expert, last, 0.0), axis=1, keepdims=True)
+            theirs = jnp.sum(
+                jnp.where(column == other.astype(jnp.int32), last, 0.0), axis=1, keepdims=True
+            )
+            gate = 1.0 / (1.0 + jnp.exp(theirs - mine))
+            inner = jnp.zeros((slot_count, 1), f32)
+            for n in range(padded // 256):
+                cols = pl.ds(n * 256, 256)
+                pre_gate, pre_up = pre[at, cols], pre[at, pl.ds(padded + n * 256, 256)]
+                dact = back[at, cols]
+                sig = 1.0 / (1.0 + jnp.exp(-pre_gate))
+                silu = pre_gate * sig
+                act = silu * pre_up
+                acts[s, at, cols] = (act * gate).astype(low)
+                inner += jnp.sum(act * dact, axis=1, keepdims=True)
+                dact = dact * gate
+                ds[s, at, cols] = (dact * pre_up * sig * (1.0 + pre_gate * (1.0 - sig))).astype(low)
+                ds[s, at, pl.ds(padded + n * 256, 256)] = (dact * silu).astype(low)
+            dgate[pl.ds(block + b, 1), :] = jnp.sum(spread[b] * inner, axis=0, keepdims=True)
+
+        @pl.loop(0, width // 256)
+        def _(n):
+            cols = pl.ds(pl.multiple_of(n * 256, 256), 256)
+            dx = jnp.dot(ds[s], w_in[:, cols], preferred_element_type=f32).astype(low)
+            out = jnp.dot(acts[s], w_down[:, cols], preferred_element_type=f32).astype(low)
+            for b in range(2):
+                at = slice(b * slot_count, (b + 1) * slot_count)
+                table = spread[b].astype(low)
+                to = pl.ds(b * tok, tok)
+                dx_buf[s, to, cols] = lax.dot_general(
+                    table, dx[at], DOWNWARD, preferred_element_type=f32
+                ).astype(low)
+                out_buf[s, to, cols] = lax.dot_general(
+                    table, out[at], DOWNWARD, preferred_element_type=f32
+                ).astype(low)
+
+    @pl.loop(0, chips)
+    def _(u):
+        @pl.when(u + 2 < chips)
+        def _():
+            take_in(u + 2)
+
+        @pl.when(u + 1 < chips)
+        def _():
+            for copy in fetch(u + 1):
+                copy.start()
+
+        for copy in fetch(u):
+            copy.wait()
+
+        @pl.when(u >= 2)
+        def _():
+            for copy in keep(u - 2):
+                copy.wait()
+
+        compute(u)
+        for copy in keep(u):
+            copy.start()
+
+    for u in (chips - 2, chips - 1):
+        for copy in keep(jnp.int32(u)):
+            copy.wait()
+
+    @pl.loop(0, chips)
+    def _(u):
+        for p in range(2):
+            for condition, number, mark, device in routes(u, p):
+                ref = part(p, u, place.at["c"])
+                on(
+                    condition,
+                    lambda ref=ref, number=number, mark=mark, device=device: remote(
+                        ref, ref, number, mark, device
+                    ).wait_send(),
+                )
+
+
+def feed(own_rows, cots, gate_weight, up_weight, down_weight, router_rows, slots, others, slot_count):
+    tok, width = own_rows.shape
+    hidden = gate_weight.shape[0]
+    padded = hidden + router_rows.shape[0]
+    total = cots.shape[0]
+    kept = total // tok * slot_count
+    low = jnp.bfloat16
+    hbm = pl.BlockSpec(memory_space=pltpu.HBM)
+    vmem = pl.BlockSpec(memory_space=pltpu.VMEM)
+    shape = jax.ShapeDtypeStruct
+    pair = 2 * slot_count
+    chips = 4 * CHIPS_Z
+    return pl.pallas_call(
+        functools.partial(feed_kernel, tok, slot_count),
+        in_specs=[hbm] * 6 + [vmem] * 2,
+        out_specs=[hbm] * 7 + [vmem],
+        out_shape=[
+            shape((total, width), low),
+            shape((total, width), low),
+            shape((total, width), low),
+            shape((kept, width), low),
+            shape((kept, width), low),
+            shape((kept, 2 * padded), low),
+            shape((kept, padded), low),
+            shape(slots.shape, jnp.float32),
+        ],
+        scratch_shapes=[
+            pltpu.VMEM((2 * padded, width), low),
+            pltpu.VMEM((padded, width), low),
+            pltpu.VMEM((2, 2 * tok, width), low),
+            pltpu.VMEM((2, 2 * tok, width), low),
+            pltpu.VMEM((2, pair, width), low),
+            pltpu.VMEM((2, pair, width), low),
+            pltpu.VMEM((pair, 2 * padded), jnp.float32),
+            pltpu.VMEM((pair, padded), jnp.float32),
+            pltpu.VMEM((2, pair, 2 * padded), low),
+            pltpu.VMEM((2, pair, padded), low),
+            pltpu.VMEM((2, 2 * tok, width), low),
+            pltpu.VMEM((2, 2 * tok, width), low),
+            pltpu.SemaphoreType.DMA((10 * chips,)),
+            pltpu.SemaphoreType.DMA((16 * CHIPS_Z,)),
+            pltpu.SemaphoreType.DMA,
+            pltpu.SemaphoreType.DMA((4,)),
+            pltpu.SemaphoreType.DMA((2, 2)),
+            pltpu.SemaphoreType.DMA((2, 6)),
+        ],
+        compiler_params=pltpu.CompilerParams(
+            collective_id=3, has_side_effects=True, vmem_limit_bytes=60 * 2**20
+        ),
+        name="feed_forward",
+    )(own_rows, cots, gate_weight, up_weight, down_weight, router_rows, slots, others)
+
+
 def per_device_torus(
     tokens,
     cotangent,
@@ -1021,9 +1367,6 @@
         for y in range(half)
         for e in range(group_size)
     ]
-    cot_everyone = lax.all_gather(cotangent[0], ("dp", "expert"), axis=0, tiled=True)
-    router_full = lax.all_gather(router_weight, "dp", axis=0, tiled=True)
-    every_route = lax.all_gather(feedforward_routes[0], "dp", axis=0, tiled=True)
     query_cols = lax.all_to_all(query_weight[0], "expert", split_axis=1, concat_axis=1, tiled=True)
     key_cols = lax.dynamic_slice_in_dim(keyvalue_weight, my_index * span, span, 1)
     value_cols = lax.dynamic_slice_in_dim(keyvalue_weight, query_width + my_index * span, span, 1)
@@ -1036,14 +1379,28 @@
         (i * tok_rows // 4, tok_rows // 4, order) for i in range(4)
     )
     rows_in = in_shard.shape[0]
-    sequence_in, in_weight, out_weight = gather(
+    route_shard = feedforward_routes[0].astype(low).reshape(-1, 128)
+    router_shard = router_weight.T.reshape(-1, 128)
+    whole = lambda a: ((0, a.shape[0], "zy"),)
+    out_weight = lax.all_gather(out_shard, "dp", axis=0, tiled=True)
+    cut = rows_in * 13 // 16
+    sequence_in, in_weight, every_route, router_full = gather(
         [
             (attention_in, "expert", quarters("xc")),
-            (in_shard, "dp", ((0, rows_in, "zy"),)),
-            (out_shard, "dp", ((0, rows_in, "zy"),)),
+            (in_shard, "dp", ((0, cut, "zy"), (cut, rows_in - cut, "yz"))),
+            (route_shard, "dp", whole(route_shard)),
+            (router_shard, "dp", whole(router_shard)),
         ],
         1,
         "gather_weights",
+    )
+    cot_late, sequence_in = lax.optimization_barrier((cotangent[0], sequence_in))
+    cot_everyone = lax.all_gather(cot_late, ("dp", "expert"), axis=0, tiled=True)
+    every_route = every_route.reshape(-1, 2).astype(jnp.int32)
+    router_full = (
+        router_full.reshape(dp_size, 2 * group_size, rows_in)
+        .transpose(0, 2, 1)
+        .reshape(-1, 2 * group_size)
     )
     attention_cols = router_full[:, :group_size]
     feedforward_cols = router_full[:, group_size:]
@@ -1060,40 +1417,32 @@
     normed_feed, unit_feed, factor_feed = norm_parts(hidden, gain_feedforward)
     feed_in = normed_feed.astype(low)
     everywhere = lambda a, b: ((0, tok_rows // 2, a), (tok_rows // 2, tok_rows // 2, b))
-    (everyone,) = gather([(feed_in, "all", everywhere("zxyc", "zyxc"))], 3, "gather_rows")
-
     mine = lambda a: lax.dynamic_slice_in_dim(a, my_index * tok_rows, tok_rows, 0)
     feed_matches = expert_matches(mine(feedforward_routes[0]), group_size)
     feed_logits = jnp.dot(feed_in, feedforward_cols, preferred_element_type=f32)
     feed_weights, _ = pair_gates(feed_logits, feed_matches)
-    feed_taken, feed_pairs = expert_table(every_route, my_index, group_size, tok_rows, slot_count)
-    feed_rows = pick_rows(feed_taken, everyone)
-    cot_rows = pick_rows(feed_taken, cot_everyone)
-    row_logits = jnp.dot(feed_rows, feedforward_cols, preferred_element_type=f32)
-    row_gate = own_gate(row_logits, feed_pairs, my_index)
-    pre_gate = lax.dot_general(feed_rows, gate_weight[0], ACROSS, preferred_element_type=f32)
-    pre_up = lax.dot_general(feed_rows, up_weight[0], ACROSS, preferred_element_type=f32)
-    sigmoid_gate = jax.nn.sigmoid(pre_gate)
-    act = pre_gate * sigmoid_gate * pre_up
-    act_low = act.astype(low)
-    act_scaled = (act * row_gate).astype(low)
-    act_grad = lax.dot_general(cot_rows, down_weight[0], ACROSS, preferred_element_type=f32)
-    slot_dgate = jnp.sum(act_low.astype(f32) * act_grad, axis=1)
-    act_grad = act_grad * row_gate
-    dgate_low = (act_grad * pre_up * sigmoid_gate * (1.0 + pre_gate * (1.0 - sigmoid_gate))).astype(
-        low
-    )
-    dup_low = (act_grad * pre_gate * sigmoid_gate).astype(low)
-    feed_dx = (
-        jnp.dot(dgate_low, gate_weight[0], preferred_element_type=f32)
-        + jnp.dot(dup_low, up_weight[0], preferred_element_type=f32)
-    ).astype(low)
-    feed_branch = jnp.dot(act_scaled, down_weight[0], preferred_element_type=f32).astype(low)
-    grad_gate = lax.dot_general(dgate_low, feed_rows, DOWNWARD, preferred_element_type=f32)
-    grad_up = lax.dot_general(dup_low, feed_rows, DOWNWARD, preferred_element_type=f32)
-    grad_down = lax.dot_general(act_scaled, cot_rows, DOWNWARD, preferred_element_type=f32)
-    token_dgate = jnp.einsum(
-        "bct,bc->bt", feed_taken.astype(f32), slot_dgate.reshape(-1, slot_count), precision=HIGH
+    slots, others = expert_slots(every_route, my_index, tok_rows)
+    hidden_rows = gate_weight.shape[1]
+    padded = -(-hidden_rows // 256) * 256
+    router_rows = jnp.pad(
+        feedforward_cols.T, ((0, padded - hidden_rows - group_size), (0, 0))
+    )
+    _, dx_part, out_part, kept_rows, kept_cots, kept_back, kept_act, token_dgate = feed(
+        feed_in,
+        cot_everyone,
+        gate_weight[0],
+        up_weight[0],
+        down_weight[0],
+        router_rows,
+        slots,
+        others,
+        slot_count,
+    )
+    grad_in_feed = lax.dot_general(kept_back, kept_rows, DOWNWARD, preferred_element_type=f32)
+    grad_gate = grad_in_feed[:hidden_rows]
+    grad_up = grad_in_feed[padded : padded + hidden_rows]
+    grad_down = lax.dot_general(
+        kept_act[:, :hidden_rows], kept_cots, DOWNWARD, preferred_element_type=f32
     )
     own_row = (jnp.arange(group_size) == my_index).astype(f32)[None, :, None]
     feed_dgate = lax.psum_scatter(
@@ -1102,12 +1451,13 @@
         scatter_dimension=0,
         tiled=True,
     ).T
-    feed_home = scatter(
-        return_rows(feed_taken, feed_dx), "all", everywhere("cxyz", "cyxz"), 4, "sum_rows"
-    )
-    feed_sum = scatter(
-        return_rows(feed_taken, feed_branch), "all", everywhere("cxyz", "cyxz"), 4, "sum_rows"
-    )
+    feed_home = scatter(dx_part, "all", everywhere("cxyz", "cyxz"), 4, "sum_rows")
+    feed_sum = lax.psum_scatter(
+        out_part,
+        ("dp", "expert"),
+        scatter_dimension=0,
+        tiled=True,
+    ).astype(f32)
     layer_output = hidden + feed_sum
     gradient = cotangent[0].astype(f32)
     feed_dlogits = gates_back(feed_dgate, feed_weights, feed_matches)

time: 1900 us -> 1830 us (0.963)
  matrix products: 463 us -> 179 us
  waiting for transfers between devices: 19.4 us -> 215 us
  blocking collectives: 141 us -> 11.6 us
  Pallas kernels: 1150 us -> 1260 us
    pallas_call x0 -> x1, Pallas kernels: none -> 368 us  [feed(): pl.pallas_call(functools.partial(feed_kernel, tok, slot_count), in_specs=...]
    dot_general x16 -> x3, matrix products: 351 us -> 65.1 us  [the longest x1 42.2 us: per_device_torus(): lax.dot_general(kept_back, kept_rows, DOWNWARD, preferred_element_type=f32)]
    pallas_call x3 -> x2, Pallas kernels: 471 us -> 272 us  [gather(): pl.pallas_call(functools.partial(gather_kernel, plan, axes), out_shape=[j...]
    all_gather x2 -> x0, blocking collectives: 129 us -> none  [the longest x1 98.3 us: per_device_torus(): lax.all_gather(feedforward_routes[0], 'dp', axis=0, tiled=True)]
    all_gather x1 -> x2, waiting for transfers between devices: 0.01 us -> 71.1 us  [the longest x1 71.1 us: per_device_torus(): lax.all_gather(cot_late, ('dp', 'expert'), axis=0, tiled=True)]
    reduce_scatter x0 -> x1, waiting for transfers between devices: none -> 63.3 us  [per_device_torus(): lax.psum_scatter(out_part, ('dp', 'expert'), scatter_dimension=0, tiled=T...]
    pallas_call x6 -> x5, Pallas kernels: 608 us -> 552 us  [scatter(): pl.pallas_call(functools.partial(scatter_kernel, whose, rows, pieces), ou...]
    ppermute x1, waiting for transfers between devices: 0.01 us -> 47.5 us  [per_device_torus(): out_shard = lax.ppermute(output_weight[0], ('dp', 'expert'), swap)]
  transfers between devices with their start and end apart: 8 -> 10, of which waited for: 2 -> 5; matrix products, arithmetic and copies ran while one was open for 18% -> 12% of each run, Pallas kernels for 55% -> 43%
where the time goes in v2:
time: 1830 us; the launch traced here: 1810 us
  Pallas kernels  1260 us (69%)
  waiting for transfers between devices  215 us (12%)
  matrix products  179 us (10%)
  local copies, waits for them, and re-layouts  62.8 us (3%)
  starting transfers between devices  36.1 us (2%)
  other arithmetic  32.7 us (2%)
    pallas_call x5, Pallas kernels, scatter(): pl.pallas_call(functools.partial(scatter_kernel, whose, rows, pieces), ou...  552 us
    pallas_call x1, Pallas kernels, feed(): pl.pallas_call(functools.partial(feed_kernel, tok, slot_count), in_specs=...  368 us
    pallas_call x2, Pallas kernels, gather(): pl.pallas_call(functools.partial(gather_kernel, plan, axes), out_shape=[j...  272 us
    all_gather x1, waiting for transfers between devices, per_device_torus(): lax.all_gather(cot_late, ('dp', 'expert'), axis=0, tiled=True)  71.1 us
    reduce_scatter x1, waiting for transfers between devices, per_device_torus(): lax.psum_scatter(out_part, ('dp', 'expert'), scatter_dimension=0, tiled=T...  63.3 us
    ppermute x1, waiting for transfers between devices, per_device_torus(): out_shard = lax.ppermute(output_weight[0], ('dp', 'expert'), swap)  47.5 us
    dot_general x1, matrix products, per_device_torus(): lax.dot_general(kept_back, kept_rows, DOWNWARD, preferred_element_type=f32)  42.2 us
    pallas_call x1, Pallas kernels, attention_back(): pl.pallas_call(functools.partial(attention_back_kernel, experts), grid=(l...  40 us
  transfers between devices with their start and end apart: 10, of which 5 were waited for; matrix products, arithmetic and copies ran while one was open for 12% of the time, Pallas kernels for 43%

profile of v2, /device:TPU:2, one launch (start us, length us, event | category | flops | bytes accessed | tf_op | source)
XLA Modules:
  0.0 1814.0 jit_solution(4523543258307252632)
XLA Ops:
  11.7 47.5 %collective-permute-done = bf16[256,2048]{1,0:T(8,128)(2,1)S(1)} collective-permute-done((bf16[256,2048]{1,0:T(8,128)(2,1)}, bf16[256,2048]{1,0:T(8,128)(2,1)S(1)}, u32[]{:S(2)}, u32[]{:S(2)}) %collective-permute-start) | collective-permute-done | bytes 1048608 | tf_op jit(solution)/shard_map/ppermute | solution.py:1374
  80.6 233.0 %gather_weights.1 = (bf16[1024,2048]{1,0:T(8,128)(2,1)}, bf16[2048,3072]{1,0:T(8,128)(2,1)}, bf16[128,128]{1,0:T(8,128)(2,1)}, bf16[128,128]{1,0:T(8,128)(2,1)}) custom-call(bf16[256,2048]{1,0:T(8,128)(2,1)} %fusion.9.refs_0_, bf16[256,3072]{1,0:T(8,128)(2,1)} %pad_maximum_fusion.refs_1_, bf16[16,128]{1,0:T(8,128)(2,1)} %convert_element_type.120.refs_2_, ...), custom_call_target="tpu_custom_call" | custom-call | tf_op jit(solution)/shard_map/gather_weights/pallas_call | solution.py:592
  331.8 18.6 %convolution_convert_fusion.2.q.k.v = bf16[1024,3072]{1,0:T(8,128)(2,1)} fusion(bf16[1024,2048]{1,0:T(8,128)(2,1)} %get-tuple-element.29, bf16[2048,3072]{1,0:T(8,128)(2,1)} %get-tuple-element.30), kind=kOutput, calls=%fused_computation.6 | convolution fusion | flops 12888047616 | bytes 23068672 | tf_op jit(solution)/shard_map/dot_general | solution.py:1407
  350.4 29.0 %attention.1 = (bf16[1024,2048]{1,0:T(8,128)(2,1)S(1)}, f32[1024,1024]{1,0:T(8,128)}) custom-call(s32[1]{0:T(128)S(6)} %copy.112.prefix, bf16[1024,3072]{1,0:T(8,128)(2,1)} %convolution_convert_fusion.2.q.k.v, bf16[1024,3072]{1,0:T(8,128)(2,1)} %convolution_convert_fusion.2.q.k.v, bf16[1024,3072]{1,0:T(8,128)(2,1)} %convolution_convert_fusion.2.q.k.v, ...), custom_call_target="tpu_custom_call" | custom-call | tf_op jit(solution)/shard_map/attention/pallas_call | solution.py:865
  383.5 14.2 convolution_convert_fusion.5.source
  397.7 41.5 %sum_attention.2 = f32[256,2048]{1,0:T(8,128)} custom-call(bf16[1024,2048]{1,0:T(8,128)(2,1)} %convolution_convert_fusion.5.source), custom_call_target="tpu_custom_call" | custom-call | tf_op jit(solution)/shard_map/sum_attention/pallas_call | solution.py:780
  443.9 71.1 %all-gather.7.cloned.1.call-done.cots = bf16[8192,2048]{1,0:T(8,128)(2,1)} async-done(((bf16[256,2048]{1,0:T(8,128)(2,1)}), bf16[8192,2048]{1,0:T(8,128)(2,1)}) %all-gather.7.cloned.1.call-update) | async-done | bytes 33554448 | tf_op jit(solution)/shard_map/all_gather | solution.py:1398
  515.0 368.1 %feed_forward.1 = (bf16[8192,2048]{1,0:T(8,128)(2,1)}, bf16[8192,2048]{1,0:T(8,128)(2,1)}, bf16[8192,2048]{1,0:T(8,128)(2,1)}, bf16[5120,2048]{1,0:T(8,128)(2,1)...) custom-call(bf16[256,2048]{1,0:T(8,128)(2,1)} %multiply_convert_fusio, ...), custom_call_target="tpu_custom_call" | custom-call | tf_op jit(solution)/shard_map/feed_forward/pallas_call | solution.py:1295
  885.2 155.7 %sum_rows.1 = f32[256,2048]{1,0:T(8,128)} custom-call(bf16[8192,2048]{1,0:T(8,128)(2,1)} %get-tuple-element.36.source), custom_call_target="tpu_custom_call" | custom-call | tf_op jit(solution)/shard_map/sum_rows/pallas_call | solution.py:780
  1050.5 38.7 %gather_cotangents.1 = bf16[1024,2048]{1,0:T(8,128)(2,1)} custom-call(bf16[256,2048]{1,0:T(8,128)(2,1)} %fusion.32.refs_0_), custom_call_target="tpu_custom_call" | custom-call | tf_op jit(solution)/shard_map/gather_cotangents/pallas_call | solution.py:592
  1089.2 13.9 convolution_convert_fusion.4.dmix
  1103.0 40.0 %attention_back.1 = (bf16[1024,3072]{1,0:T(8,128)(2,1)}, f32[1024,128]{1,0:T(8,128)}) custom-call(s32[1]{0:T(128)S(6)} %copy.112.prefix, bf16[1024,3072]{1,0:T(8,128)(2,1)} %convolution_convert_fusion.2.q.k.v, bf16[1024,3072]{1,0:T(8,128)(2,1)} %convolution_convert_fusion.2.q.k.v, bf16[1024,3072]{1,0:T(8,128)(2,1)} %convolution_convert_fusion.2.q.k.v, ...), custom_call_target="tpu_custom_call" | custom-call | tf_op jit(solution)/shard_map/attention_back/pallas_call | solution.py:960
  1143.0 19.5 %convolution_convert_fusion.3.source = bf16[1024,2048]{1,0:T(8,128)(2,1)} fusion(bf16[1024,3072]{1,0:T(8,128)(2,1)} %get-tuple-element.39, bf16[2048,3072]{1,0:T(8,128)(2,1)} %get-tuple-element.30), kind=kOutput, calls=%fused_computation.8 | convolution fusion | flops 12886999040 | bytes 23068672 | tf_op jit(solution)/shard_map/dot_general | solution.py:1476
  1162.6 29.4 %sum_attention.3 = f32[256,2048]{1,0:T(8,128)} custom-call(bf16[1024,2048]{1,0:T(8,128)(2,1)} %convolution_convert_fusion.3.source), custom_call_target="tpu_custom_call" | custom-call | tf_op jit(solution)/shard_map/sum_attention/pallas_call | solution.py:780
  1193.5 11.6 all-reduce.3
  1213.4 19.8 %convolution_convert_fusion.source = bf16[2048,3072]{1,0:T(8,128)(2,1)} fusion(bf16[1024,2048]{1,0:T(8,128)(2,1)} %get-tuple-element.29, bf16[1024,3072]{1,0:T(8,128)(2,1)} %get-tuple-element.39), kind=kOutput, calls=%fused_computation | convolution fusion | flops 12891193344 | bytes 23068672 | tf_op jit(solution)/shard_map/dot_general | solution.py:1477
  1233.1 146.3 %sum_input_weight.1 = f32[256,3072]{1,0:T(8,128)} custom-call(bf16[2048,3072]{1,0:T(8,128)(2,1)} %convolution_convert_fusion.source), custom_call_target="tpu_custom_call" | custom-call | tf_op jit(solution)/shard_map/sum_input_weight/pallas_call | solution.py:780
  1383.0 22.1 %fusion.2 = f32[1,704,2048]{2,1,0:T(8,128)} fusion(bf16[5120,2048]{1,0:T(8,128)(2,1)} %get-tuple-element.44, bf16[5120,768]{1,0:T(8,128)(2,1)} %get-tuple-element.43), kind=kOutput, calls=%fused_computation.11 | convolution fusion | flops 14763950080 | bytes 34603008 | tf_op jit(solution)/shard_map/dot_general | solution.py:1444
  1405.1 42.2 %fusion.38 = f32[1536,2048]{1,0:T(8,128)} fusion(bf16[5120,1536]{1,0:T(8,128)(2,1)} %get-tuple-element.41, bf16[5120,2048]{1,0:T(8,128)(2,1)} %get-tuple-element.42), kind=kOutput, calls=%fused_computation.93 | convolution fusion | flops 32212254720 | bytes 49283072 | tf_op jit(solution)/shard_map/dot_general | solution.py:1441
  1452.9 14.1 convolution_convert_fusion.1.source
  1467.0 179.0 %sum_output_weight.1 = f32[256,2048]{1,0:T(8,128)} custom-call(bf16[2048,2048]{1,0:T(8,128)(2,1)} %convolution_convert_fusion.1.source), custom_call_target="tpu_custom_call" | custom-call | tf_op jit(solution)/shard_map/sum_output_weight/pallas_call | solution.py:780
  1648.8 23.4 %collective-permute-start.1 = (bf16[256,2048]{1,0:T(8,128)(2,1)}, bf16[256,2048]{1,0:T(8,128)(2,1)}, u32[]{:S(2)}, u32[]{:S(2)}) collective-permute-start(bf16[256,2048]{1,0:T(8,128)(2,1)} %convert_element_type.146), channel_id=1, source_target_pairs={{0,0},{1,8},{2,16},{3,24},{4,4},{5,12},{6,20},{7,28},{8,1},{9,9},{... | collective-permute-start | bytes 3145736 | tf_op jit(solution)/shard_map/ppermute | solution.py:1511
  1691.4 24.1 %collective-permute-done.1 = bf16[256,2048]{1,0:T(8,128)(2,1)} collective-permute-done((bf16[256,2048]{1,0:T(8,128)(2,1)}, bf16[256,2048]{1,0:T(8,128)(2,1)}, u32[]{:S(2)}, u32[]{:S(2)}) %collective-permute-start.1) | collective-permute-done | bytes 1048608 | tf_op jit(solution)/shard_map/ppermute | solution.py:1511
  1738.1 63.3 %reduce-scatter.3.cloned.1.call-done = bf16[256,2048]{1,0:T(8,128)(2,1)} async-done(((bf16[8192,2048]{1,0:T(8,128)(2,1)}), bf16[256,2048]{1,0:T(8,128)(2,1)}) %reduce-scatter.3.cloned.1.call-update) | async-done | bytes 1048592 | tf_op jit(solution)/shard_map/reduce_scatter | solution.py:1455
  (161 shorter events, 131.6 us)
Async XLA Ops:
  7.2 376.3 %all-gather.5.cloned.1.call-start = ((), (), s32[]{:S(2)}) async-start(), calls=%async_computation.3 | async-start | bytes 9437184 | tf_op jit(solution)/shard_map/all_gather | solution.py:1385
  7.2 51.9 %collective-permute-start = (bf16[256,2048]{1,0:T(8,128)(2,1)}, bf16[256,2048]{1,0:T(8,128)(2,1)S(1)}, u32[]{:S(2)}, u32[]{:S(2)}) collective-permute-start(bf16[256,2048]{1,0:T(8,128)(2,1)} %bitcast.119), channel_id=1, source_target_pairs={{0,0},{1,8},{2,16},{3,24},{4,4},{5,12},{6,20},{7,28},{8,1},{9,9},{... | collective-permute-start | bytes 3145736 | tf_op jit(solution)/shard_map/ppermute | solution.py:1374
  63.1 16.1 all-to-all-start
  66.6 448.4 %all-gather.7.cloned.1.call-start = ((), (), s32[]{:S(2)}) async-start(), calls=%async_computation.4 | async-start | bytes 34603008 | tf_op jit(solution)/shard_map/all_gather | solution.py:1398
  69.9 10.8 copy-start.21
  79.3 235.1 %copy-start.26 = (s32[1,1024,2]{1,2,0:T(2,128)S(1)}, s32[1,1024,2]{1,2,0:T(2,128)}, u32[]{:S(2)}) copy-start(s32[1,1024,2]{1,2,0:T(2,128)} %param.16) | copy-start | bytes 24580
  80.6 234.3 %copy-start.28 = (u32[32]{0:T(128)S(1)}, u32[32]{0:T(128)}, u32[]{:S(2)}) copy-start(u32[32]{0:T(128)} %constant.69) | copy-start | bytes 388
  313.7 727.2 %all-reduce.9.cloned.1.call-start = ((), (), s32[]{:S(2)}) async-start(), calls=%async_computation.8 | async-start | bytes 262144
  331.8 18.6 %copy-start = (f32[1024,128]{1,0:T(8,128)}, f32[1024,128]{1,0:T(8,128)S(1)}, u32[]{:S(2)}) copy-start(f32[1024,128]{1,0:T(8,128)S(1)} %select_maximum_fusion.side) | copy-start | bytes 1572868
  350.4 31.0 %copy-start.5 = (s32[32,256,2]{2,1,0:T(8,128)S(1)}, s32[32,256,2]{2,1,0:T(8,128)}, u32[]{:S(2)}) copy-start(s32[32,256,2]{2,1,0:T(8,128)} %reshape.176) | copy-start | bytes 196612
  441.4 606.1 %copy-start.19 = (f32[256]{0:T(256)}, f32[256]{0:T(256)S(1)}, u32[]{:S(2)}) copy-start(f32[256]{0:T(256)S(1)} %add_rsqrt_fusion) | copy-start | bytes 3076
  515.0 369.8 %copy-start.8 = (bf16[256,2048]{1,0:T(8,128)(2,1)S(1)}, bf16[256,2048]{1,0:T(8,128)(2,1)}, u32[]{:S(2)}) copy-start(bf16[256,2048]{1,0:T(8,128)(2,1)} %multiply_convert_fusion.own_rows) | copy-start | bytes 3145732
  884.8 798.3 %all-reduce.7.cloned.1.call-start = ((), (), s32[]{:S(2)}) async-start(), calls=%async_computation.6 | async-start | bytes 262144 | tf_op jit(solution)/shard_map/psum | solution.py:1505
  1162.6 47.2 %copy-start.16 = (f32[2048]{0:T(1024)S(1)}, f32[2048]{0:T(1024)}, u32[]{:S(2)}) copy-start(f32[2048]{0:T(1024)} %param.19) | copy-start | bytes 24580
  1162.6 47.2 %copy-start.22 = (f32[256]{0:T(256)S(1)}, f32[256]{0:T(256)}, u32[]{:S(2)}) copy-start(f32[256]{0:T(256)} %copy-done.21) | copy-start | bytes 3076
  1191.9 17.8 copy-start.10
  1213.3 505.0 %all-gather.9.cloned.1.call-start = ((), (), s32[]{:S(2)}) async-start(), calls=%async_computation.7 | async-start | bytes 2621440 | tf_op jit(solution)/shard_map/all_gather | solution.py:1516
  1382.4 418.9 %reduce-scatter.3.cloned.1.call-start = ((), (), s32[]{:S(2)}) async-start(), calls=%async_computation.5 | async-start | bytes 34603008 | tf_op jit(solution)/shard_map/reduce_scatter | solution.py:1455
  1448.5 237.2 %all-to-all-start.1 = ((bf16[256,4,512]{2,0,1:T(8,128)(2,1)}), bf16[256,4,512]{2,0,1:T(8,128)(2,1)}, u32[]{:S(2)}, u32[]{:S(2)}) async-start(bf16[256,4,512]{2,0,1:T(8,128)(2,1)} %bitcast.95), calls=%async_computation.2 | async-start | bytes 2097152 | tf_op jit(solution)/shard_map/all_to_all | solution.py:1513
  1648.8 66.7 %collective-permute-start.1 = (bf16[256,2048]{1,0:T(8,128)(2,1)}, bf16[256,2048]{1,0:T(8,128)(2,1)}, u32[]{:S(2)}, u32[]{:S(2)}) collective-permute-start(bf16[256,2048]{1,0:T(8,128)(2,1)} %convert_element_type.146), channel_id=1, source_target_pairs={{0,0},{1,8},{2,16},{3,24},{4,4},{5,12},{6,20},{7,28},{8,1},{9,9},{... | collective-permute-start | bytes 3145736 | tf_op jit(solution)/shard_map/ppermute | solution.py:1511
  1731.9 69.5 %copy-start.4 = (f32[256,2048]{1,0:T(8,128)S(1)}, f32[256,2048]{1,0:T(8,128)}, u32[]{:S(2)}) copy-start(f32[256,2048]{1,0:T(8,128)} %copy-done.2) | copy-start | bytes 6291460
  1731.9 69.5 %copy-start.14 = (f32[2048]{0:T(1024)S(1)}, f32[2048]{0:T(1024)}, u32[]{:S(2)}) copy-start(f32[2048]{0:T(1024)} %param.20) | copy-start | bytes 24580
  1731.9 69.5 %copy-start.20 = (f32[256]{0:T(256)S(1)}, f32[256]{0:T(256)}, u32[]{:S(2)}) copy-start(f32[256]{0:T(256)} %copy-done.19) | copy-start | bytes 3076
  1731.9 69.5 %copy-start.25 = (f32[256]{0:T(256)S(1)}, f32[256]{0:T(256)}, u32[]{:S(2)}) copy-start(f32[256]{0:T(256)} %copy-done.24) | copy-start | bytes 3076
  (15 other events, 59.0 us)
Sparse Core Ops, SparseCore 0:
  60.3 201.2 all-gather.4
  313.8 201.1 all-gather.6
  884.9 124.3 all-reduce.8
  1213.4 125.8 all-reduce.6
  1382.5 21.5 all-gather.8
  1406.3 394.9 reduce-scatter.2

commit v3 on v2

--- a/solution.py
+++ b/solution.py
@@ -431,8 +431,15 @@
         return {"all": dp * 4 + expert, "dp": dp, "expert": expert}[whose]
 
 
-def enter(place, axes):
+def enter(place, axes, others=()):
     barrier, count = pltpu.get_barrier_semaphore(), 0
+    for device, condition in others:
+
+        def greet(device=device):
+            pl.semaphore_signal(barrier, inc=1, device_id=device, device_id_type=MESH)
+
+        on(condition, greet)
+        count = count + (1 if condition is None else condition.astype(jnp.int32))
     for axis in axes:
         if axis != "z":
             pl.semaphore_signal(
@@ -502,26 +509,19 @@
 FLIPS = {"x": 4, "y": 2, "c": 1}
 
 
-def gather_kernel(jobs, axes, *refs):
-    count = len(jobs)
-    sources, targets = refs[:count], refs[count : 2 * count]
-    send_sems, arrive_sems, own_sems = refs[2 * count :]
-    place = Place()
-    enter(place, axes)
-    post = Post(send_sems, place)
+def gather_plan(jobs, place, post, sources, targets, arrive_sems, own_sems):
     z_here = place.at["z"]
     line = 0
-    waves, owns = {}, []
+    waves, owns, starts = {}, [], []
     for j, (whose, rows, pieces) in enumerate(jobs):
         own = pltpu.make_async_copy(
             sources[j],
             targets[j].at[pl.ds(place.block(whose, z_here, {}) * rows, rows)],
             own_sems.at[j],
         )
-        own.start()
         owns.append(own)
+        begin = [own.start]
         for first, length, order in pieces:
-
             def part(z, flips, j=j, whose=whose, rows=rows, first=first, length=length):
                 at = place.block(whose, z, flips) * rows + first
                 return targets[j].at[pl.ds(at, length)]
@@ -551,9 +551,27 @@
                 waves.setdefault(wave, []).append(act)
                 spread(z, flips, depth, side, hops, wave, condition, order, come)
 
-            hand_on(sources[j].at[pl.ds(first, length)], z_here, {}, -1, 0, 0, None)
+            begin.append(
+                lambda hand_on=hand_on, j=j, first=first, length=length: hand_on(
+                    sources[j].at[pl.ds(first, length)], z_here, {}, -1, 0, 0, None
+                )
+            )
             spread(z_here, {}, -1, 0, 0, 0, None, order, come)
             line += 1
+        starts.append(begin)
+    return starts, waves, owns
+
+
+def gather_kernel(jobs, axes, *refs):
+    count = len(jobs)
+    sources, targets = refs[:count], refs[count : 2 * count]
+    send_sems, arrive_sems, own_sems = refs[2 * count :]
+    place = Place()
+    enter(place, axes)
+    post = Post(send_sems, place)
+    starts, waves, owns = gather_plan(jobs, place, post, sources, targets, arrive_sems, own_sems)
+    for act in sum(starts, []):
+        act()
     for wave in sorted(waves):
         for act in waves[wave]:
             act()
@@ -609,7 +627,7 @@
     )(*arrays)
 
 
-def scatter_kernel(whose, rows, pieces, source, result, acc, *refs):
+def scatter_kernel(whose, rows, pieces, source, _, result, acc, *refs):
     place = Place()
     orders = [order for _, _, order in pieces]
     flat = [order.replace("z", "") for order in orders]
@@ -759,7 +777,7 @@
     post.close()
 
 
-def scatter(array, whose, pieces, collective_id, name, dtype=jnp.float32):
+def scatter(array, whose, pieces, collective_id, name, after=None):
     size = {"all": 32, "dp": 8, "expert": 4}[whose]
     rows, width = array.shape[0] // size, array.shape[1]
     flat = pieces[0][2].replace("z", "")
@@ -779,15 +797,110 @@
     ]
     return pl.pallas_call(
         functools.partial(scatter_kernel, whose, rows, pieces),
-        out_shape=jax.ShapeDtypeStruct((rows, width), dtype),
-        in_specs=[pl.BlockSpec(memory_space=pltpu.HBM)],
+        out_shape=jax.ShapeDtypeStruct((rows, width), jnp.float32),
+        in_specs=[pl.BlockSpec(memory_space=pltpu.HBM), pl.BlockSpec(memory_space=pl.ANY)],
         out_specs=pl.BlockSpec(memory_space=pltpu.VMEM),
         scratch_shapes=scratch,
         compiler_params=pltpu.CompilerParams(
             collective_id=collective_id, has_side_effects=True, vmem_limit_bytes=62 * 2**20
         ),
         name=name,
-    )(array)
+    )(array, array if after is None else after)
+
+
+def weights_kernel(jobs, *refs):
+    ready = len(jobs) - 2
+    sources, (query, keyvalue, output) = refs[:ready], refs[ready : ready + 3]
+    in_shard, out_shard = refs[ready + 3 : ready + 5]
+    targets = refs[ready + 5 : 2 * ready + 7]
+    send_sems, arrive_sems, own_sems, deal_sems = refs[2 * ready + 7 :]
+    place = Place()
+    z, y, e = place.at["z"], place.at["y"], place.expert
+    span = (in_shard.shape[1] - query.shape[1]) // 2
+    wide = query.shape[1]
+    partner, moves = (e * 2 + y, z), z != e
+    peers = []
+    for flip_x, flip_c in ((1, 1), (1, 0), (0, 1)):
+        x = place.at["x"] + flip_x * (1 - 2 * place.at["x"])
+        core = place.at["c"] + flip_c * (1 - 2 * place.at["c"])
+        peers.append((x * 2 + core, flip_x * 2 + flip_c))
+    enter(place, "cxyz", [((place.dp, peers[0][0]), None), (partner, moves)])
+    post = Post(send_sems, place)
+    starts, waves, owns = gather_plan(
+        jobs, place, post, list(sources) + [in_shard, out_shard], targets, arrive_sems, own_sems
+    )
+    cols = lambda block: pl.ds(pl.multiple_of(block * span, span), span)
+    for peer, flips in peers:
+        post.send(
+            query.at[:, cols(peer)], in_shard.at[:, cols(e)], deal_sems.at[flips], (place.dp, peer)
+        )
+    post.send(output, out_shard, deal_sems.at[4], partner, moves)
+    local = [
+        pltpu.make_async_copy(query.at[:, cols(e)], in_shard.at[:, cols(e)], deal_sems.at[0]),
+        pltpu.make_async_copy(
+            keyvalue.at[:, cols(e)], in_shard.at[:, pl.ds(wide, span)], deal_sems.at[5]
+        ),
+        pltpu.make_async_copy(
+            keyvalue.at[:, cols(wide // span + e)],
+            in_shard.at[:, pl.ds(wide + span, span)],
+            deal_sems.at[6],
+        ),
+    ]
+    for copy in local:
+        copy.start()
+    stay = pltpu.make_async_copy(output, out_shard, deal_sems.at[7])
+    pl.when(~moves)(stay.start)
+    for act in sum(starts[:ready], []):
+        act()
+    for copy in local:
+        copy.wait()
+    for peer, flips in peers:
+        post.arrived(in_shard.at[:, cols(peer)], deal_sems.at[flips])
+    for act in starts[ready]:
+        act()
+    pl.when(~moves)(stay.wait)
+    pl.when(moves)(lambda: post.arrived(out_shard, deal_sems.at[4]))
+    for act in starts[ready + 1]:
+        act()
+    for wave in sorted(waves):
+        for act in waves[wave]:
+            act()
+    for own in owns:
+        own.wait()
+    post.close()
+
+
+def gather_weights(jobs, query, keyvalue, output, pieces, collective_id):
+    rows, wide = query.shape
+    span = wide // lax.axis_size("expert")
+    shards = [
+        jax.ShapeDtypeStruct((rows, wide + 2 * span), query.dtype),
+        jax.ShapeDtypeStruct(output.shape, output.dtype),
+    ]
+    sizes = {"all": 32, "dp": 8, "expert": 4}
+    plan = tuple((whose, r.shape[0], ps) for r, whose, ps in jobs)
+    plan += tuple(("dp", s.shape[0], pieces) for s in shards)
+    lines = sum(len(ps) for _, _, ps in plan)
+    hbm = pl.BlockSpec(memory_space=pltpu.HBM)
+    gathered = [
+        jax.ShapeDtypeStruct((sizes[whose] * r.shape[0], r.shape[1]), r.dtype)
+        for r, (whose, _, _) in zip([r for r, _, _ in jobs] + shards, plan)
+    ]
+    out = pl.pallas_call(
+        functools.partial(weights_kernel, plan),
+        out_shape=shards + gathered,
+        in_specs=[hbm] * (len(jobs) + 3),
+        out_specs=[hbm] * (2 + len(gathered)),
+        scratch_shapes=[
+            pltpu.SemaphoreType.DMA((110 * lines,)),
+            pltpu.SemaphoreType.DMA((lines, 32)),
+            pltpu.SemaphoreType.DMA((len(plan),)),
+            pltpu.SemaphoreType.DMA((8,)),
+        ],
+        compiler_params=pltpu.CompilerParams(collective_id=collective_id, has_side_effects=True),
+        name="gather_weights",
+    )(*[r for r, _, _ in jobs], query, keyvalue, output)
+    return out[2:]
 
 
 def attention_bias(bias, block, rows, width, prefix):
@@ -985,9 +1098,6 @@
         compiler_params=pltpu.CompilerParams(vmem_limit_bytes=56 * 2**20),
         name="attention_back",
     )(prefix, projected, projected, projected, side, log_total, dmix)
-
-
-NEAREST = ((0, 1, 2, 3), (1, 2, 0, 3), (2, 1, 3, 0), (3, 2, 1, 0))
 
 
 def expert_slots(ids, my_index, tok_rows):
@@ -1064,13 +1174,16 @@
     enter(place, "cxyz")
 
     def chip(u):
-        k, xr, yr = u // 4, u % 2, (u // 2) % 2
-        z = sum(
-            ((z_here == at) & (k == i)).astype(jnp.int32) * seq[i]
-            for at, seq in enumerate(NEAREST)
-            for i in range(CHIPS_Z)
-        )
-        return z, xr, yr
+        u = jnp.asarray(u, jnp.int32)
+        turn, q = u // 4, u % 4
+        flip = lambda *at: ((q == at[0]) | (q == at[1])).astype(jnp.int32)
+        k, xr, yr = turn + (q == 3) - (q == 0), flip(0, 1), flip(0, 2)
+        k = jnp.where(u == 0, 0, jnp.minimum(k, CHIPS_Z - 1))
+        xr = jnp.where(u == 0, 0, jnp.where(u == chips - 1, 1, xr))
+        yr = jnp.where(u == 0, 0, jnp.where(u == chips - 1, 1, yr))
+        inner = (z_here == 1) | (z_here == 2)
+        near = jnp.where(inner, jnp.where(k == 3, 3, jnp.where(k == 2, 0, k + 1)), k)
+        return jnp.where(z_here < 2, near, CHIPS_Z - 1 - near), xr, yr
 
     def first_block(u):
         z, xr, yr = chip(u)
@@ -1110,8 +1223,8 @@
             (None, base + 4, mark + here + 1, place.across("c")),
         ]
 
-    def hand_on(u, sources):
-        for p in range(2):
+    def hand_on(u, sources, pieces=(0, 1)):
+        for p in pieces:
             for condition, number, mark, device in routes(u, p):
                 target = part(p, u, place.at["c"])
                 source = target if sources is None else sources[p]
@@ -1129,14 +1242,12 @@
             mark = (p * CHIPS_Z + z) * 8 + xr * 4 + yr * 2 + 1
             remote(ref, ref, 0, mark, place.across("c")).wait_recv()
 
-    def take_in(u):
+    def take_in(u, p):
         z, xr, yr = chip(u)
-        for p in range(2):
-            ref = part(p, u, place.at["c"])
-            mark = (p * CHIPS_Z + z) * 8 + xr * 4 + yr * 2
-            remote(ref, ref, 0, mark, place.across("c")).wait_recv()
-        hand_on(u, None)
-        sibling_came(u)
+        ref = part(p, u, place.at["c"])
+        mark = (p * CHIPS_Z + z) * 8 + xr * 4 + yr * 2
+        remote(ref, ref, 0, mark, place.across("c")).wait_recv()
+        hand_on(u, None, (p,))
 
     def fetch(u):
         at = pl.ds(first_block(u) * tok, 2 * tok)
@@ -1163,7 +1274,8 @@
     sibling_came(0)
     for copy in fetch(0):
         copy.start()
-    take_in(1)
+    for p in range(2):
+        take_in(1, p)
     for load in loads[:4]:
         load.wait()
 
@@ -1189,6 +1301,10 @@
         def _(n):
             at = pl.ds(pl.multiple_of(n * 256, 256), 256)
             pre[:, at] = lax.dot_general(xs[s], w_in[at, :], ACROSS, preferred_element_type=f32)
+
+        @pl.when(u + 2 < chips)
+        def _():
+            take_in(u + 2, 1)
 
         @pl.loop(0, padded // 256)
         def _(n):
@@ -1242,14 +1358,15 @@
 
     @pl.loop(0, chips)
     def _(u):
+        @pl.when(u + 1 < chips)
+        def _():
+            sibling_came(u + 1)
+            for copy in fetch(u + 1):
+                copy.start()
+
         @pl.when(u + 2 < chips)
         def _():
-            take_in(u + 2)
-
-        @pl.when(u + 1 < chips)
-        def _():
-            for copy in fetch(u + 1):
-                copy.start()
+            take_in(u + 2, 0)
 
         for copy in fetch(u):
             copy.wait()
@@ -1367,35 +1484,30 @@
         for y in range(half)
         for e in range(group_size)
     ]
-    query_cols = lax.all_to_all(query_weight[0], "expert", split_axis=1, concat_axis=1, tiled=True)
-    key_cols = lax.dynamic_slice_in_dim(keyvalue_weight, my_index * span, span, 1)
-    value_cols = lax.dynamic_slice_in_dim(keyvalue_weight, query_width + my_index * span, span, 1)
-    in_shard = jnp.concatenate([query_cols, key_cols, value_cols], axis=1)
-    out_shard = lax.ppermute(output_weight[0], ("dp", "expert"), swap)
+    cot_everyone = lax.all_gather(cotangent[0], ("dp", "expert"), axis=0, tiled=True)
 
     normed_attention, unit_attention, factor_attention = norm_parts(inputs, gain_attention)
     attention_in = normed_attention.astype(low)
     quarters = lambda order: tuple(
         (i * tok_rows // 4, tok_rows // 4, order) for i in range(4)
     )
-    rows_in = in_shard.shape[0]
+    rows_in = keyvalue_weight.shape[0]
     route_shard = feedforward_routes[0].astype(low).reshape(-1, 128)
     router_shard = router_weight.T.reshape(-1, 128)
     whole = lambda a: ((0, a.shape[0], "zy"),)
-    out_weight = lax.all_gather(out_shard, "dp", axis=0, tiled=True)
     cut = rows_in * 13 // 16
-    sequence_in, in_weight, every_route, router_full = gather(
+    sequence_in, every_route, router_full, in_weight, out_weight = gather_weights(
         [
             (attention_in, "expert", quarters("xc")),
-            (in_shard, "dp", ((0, cut, "zy"), (cut, rows_in - cut, "yz"))),
             (route_shard, "dp", whole(route_shard)),
             (router_shard, "dp", whole(router_shard)),
         ],
+        query_weight[0],
+        keyvalue_weight,
+        output_weight[0],
+        ((0, cut, "zy"), (cut, rows_in - cut, "yz")),
         1,
-        "gather_weights",
-    )
-    cot_late, sequence_in = lax.optimization_barrier((cotangent[0], sequence_in))
-    cot_everyone = lax.all_gather(cot_late, ("dp", "expert"), axis=0, tiled=True)
+    )
     every_route = every_route.reshape(-1, 2).astype(jnp.int32)
     router_full = (
         router_full.reshape(dp_size, 2 * group_size, rows_in)
@@ -1452,13 +1564,14 @@
         tiled=True,
     ).T
     feed_home = scatter(dx_part, "all", everywhere("cxyz", "cyxz"), 4, "sum_rows")
+    out_part, feed_home = lax.optimization_barrier((out_part, feed_home))
     feed_sum = lax.psum_scatter(
         out_part,
         ("dp", "expert"),
         scatter_dimension=0,
         tiled=True,
-    ).astype(f32)
-    layer_output = hidden + feed_sum
+    )
+    layer_output = hidden + feed_sum.astype(f32)
     gradient = cotangent[0].astype(f32)
     feed_dlogits = gates_back(feed_dgate, feed_weights, feed_matches)
     feed_dnorm = feed_home + jnp.dot(feed_dlogits, feedforward_cols.astype(f32).T, precision=HIGH)
@@ -1507,7 +1620,9 @@
 
     down_dp = ((0, rows_in, "yz"),)
     out_rows = scatter(grad_out.astype(low), "dp", down_dp, 6, "sum_output_weight")
-    in_rows = scatter(grad_in.astype(low), "dp", down_dp, 7, "sum_input_weight").astype(low)
+    in_rows = scatter(
+        grad_in.astype(low), "dp", down_dp, 7, "sum_input_weight", feed_sum
+    ).astype(low)
     grad_projection = lax.ppermute(out_rows.astype(low), ("dp", "expert"), swap).astype(f32)
     wide = group_size * span
     grad_query = lax.all_to_all(

time: 1830 us -> 1690 us (0.923)
  waiting for transfers between devices: 215 us -> 11.9 us
  Pallas kernels: 1260 us -> 1350 us
  starting transfers between devices: 36.1 us -> 11.1 us
    pallas_call x0 -> x1, Pallas kernels: none -> 389 us  [gather_weights(): pl.pallas_call(functools.partial(weights_kernel, plan), out_shape=shards...]
    pallas_call x2 -> x1, Pallas kernels: 272 us -> 58.5 us  [gather(): pl.pallas_call(functools.partial(gather_kernel, plan, axes), out_shape=[j...]
    all_gather x2 -> x1, waiting for transfers between devices: 71.1 us -> 0.01 us  [per_device_torus(): lax.all_gather(cotangent[0], ('dp', 'expert'), axis=0, tiled=True)]
    pallas_call x1, Pallas kernels: 368 us -> 298 us  [feed(): pl.pallas_call(functools.partial(feed_kernel, tok, slot_count), in_specs=...]
    reduce_scatter x1, waiting for transfers between devices: 63.3 us -> 0.02 us  [per_device_torus(): lax.psum_scatter(out_part, ('dp', 'expert'), scatter_dimension=0, tiled=T...]
    ppermute x1 -> x0, waiting for transfers between devices: 47.5 us -> none  [per_device_torus(): out_shard = lax.ppermute(output_weight[0], ('dp', 'expert'), swap)]
    ppermute x1, waiting for transfers between devices: 24.1 us -> 0.01 us  [per_device_torus(): lax.ppermute(out_rows.astype(low), ('dp', 'expert'), swap).astype(f32)]
    ppermute x1, starting transfers between devices: 23.4 us -> 4.53 us  [per_device_torus(): lax.ppermute(out_rows.astype(low), ('dp', 'expert'), swap).astype(f32)]
  transfers between devices with their start and end apart: 10 -> 7, of which waited for: 5 -> 1; matrix products, arithmetic and copies ran while one was open for 12% -> 14% of each run, Pallas kernels for 43% -> 63%
where the time goes in v3:
time: 1690 us; the launch traced here: 1680 us
  Pallas kernels  1350 us (80%)
  matrix products  176 us (10%)
  local copies, waits for them, and re-layouts  60.9 us (4%)
  other arithmetic  29.9 us (2%)
    pallas_call x5, Pallas kernels, scatter(): pl.pallas_call(functools.partial(scatter_kernel, whose, rows, pieces), ou...  538 us
    pallas_call x1, Pallas kernels, gather_weights(): pl.pallas_call(functools.partial(weights_kernel, plan), out_shape=shards...  389 us
    pallas_call x1, Pallas kernels, feed(): pl.pallas_call(functools.partial(feed_kernel, tok, slot_count), in_specs=...  298 us
    pallas_call x1, Pallas kernels, gather(): pl.pallas_call(functools.partial(gather_kernel, plan, axes), out_shape=[j...  58.5 us
    dot_general x1, matrix products, per_device_torus(): lax.dot_general(kept_back, kept_rows, DOWNWARD, preferred_element_type=f32)  42.8 us
    pallas_call x1, Pallas kernels, attention_back(): pl.pallas_call(functools.partial(attention_back_kernel, experts), grid=(l...  40.3 us
  transfers between devices with their start and end apart: 7, of which 1 were waited for; matrix products, arithmetic and copies ran while one was open for 14% of the time, Pallas kernels for 63%

profile of v3, /device:TPU:2, one launch (start us, length us, event | category | flops | bytes accessed | tf_op | source)
XLA Modules:
  0.0 1675.6 jit_solution(2220923583458989614)
XLA Ops:
  16.3 389.2 %gather_weights.1 = (bf16[256,3072]{1,0:T(8,128)(2,1)}, bf16[256,2048]{1,0:T(8,128)(2,1)}, bf16[1024,2048]{1,0:T(8,128)(2,1)}, bf16[128,128]{1,0:T(8,128)(2,1)},...) custom-call(bf16[256,2048]{1,0:T(8,128)(2,1)} %fusion.9.refs_0_, ...), custom_call_target="tpu_custom_call" | custom-call | tf_op jit(solution)/shard_map/gather_weights/pallas_call | solution.py:889
  411.8 19.4 %convolution_convert_fusion.2.q.k.v = bf16[1024,3072]{1,0:T(8,128)(2,1)} fusion(bf16[1024,2048]{1,0:T(8,128)(2,1)} %get-tuple-element.29, bf16[2048,3072]{1,0:T(8,128)(2,1)} %get-tuple-element.30), kind=kOutput, calls=%fused_computation.6 | convolution fusion | flops 12888047616 | bytes 23068672 | tf_op jit(solution)/shard_map/dot_general | solution.py:1519
  431.2 28.9 %attention.1 = (bf16[1024,2048]{1,0:T(8,128)(2,1)S(1)}, f32[1024,1024]{1,0:T(8,128)}) custom-call(s32[1]{0:T(128)S(6)} %copy.101.prefix, bf16[1024,3072]{1,0:T(8,128)(2,1)} %convolution_convert_fusion.2.q.k.v, bf16[1024,3072]{1,0:T(8,128)(2,1)} %convolution_convert_fusion.2.q.k.v, bf16[1024,3072]{1,0:T(8,128)(2,1)} %convolution_convert_fusion.2.q.k.v, ...), custom_call_target="tpu_custom_call" | custom-call | tf_op jit(solution)/shard_map/attention/pallas_call | solution.py:978
  462.1 10.3 convolution_convert_fusion.5.source._
  472.4 48.6 %sum_attention.2 = f32[256,2048]{1,0:T(8,128)} custom-call(bf16[1024,2048]{1,0:T(8,128)(2,1)} %convolution_convert_fusion.5.source._, bf16[1024,2048]{1,0:T(8,128)(2,1)} %convolution_convert_fusion.5.source._), custom_call_target="tpu_custom_call" | custom-call | tf_op jit(solution)/shard_map/sum_attention/pallas_call | solution.py:798
  537.2 298.3 %feed_forward.1 = (bf16[8192,2048]{1,0:T(8,128)(2,1)}, bf16[8192,2048]{1,0:T(8,128)(2,1)}, bf16[8192,2048]{1,0:T(8,128)(2,1)}, bf16[5120,2048]{1,0:T(8,128)(2,1)...) custom-call(bf16[256,2048]{1,0:T(8,128)(2,1)} %multiply_convert_fusio, ...), custom_call_target="tpu_custom_call" | custom-call | tf_op jit(solution)/shard_map/feed_forward/pallas_call | solution.py:1412
  837.2 156.8 %sum_rows.1 = f32[256,2048]{1,0:T(8,128)} custom-call(bf16[8192,2048]{1,0:T(8,128)(2,1)} %get-tuple-element.36.source._, bf16[8192,2048]{1,0:T(8,128)(2,1)} %get-tuple-element.36.source._), custom_call_target="tpu_custom_call" | custom-call | tf_op jit(solution)/shard_map/sum_rows/pallas_call | solution.py:798
  997.0 21.9 %fusion.2 = f32[1,704,2048]{2,1,0:T(8,128)} fusion(bf16[5120,2048]{1,0:T(8,128)(2,1)} %get-tuple-element.46, bf16[5120,768]{1,0:T(8,128)(2,1)} %get-tuple-element.45), kind=kOutput, calls=%fused_computation.11 | convolution fusion | flops 14763950080 | bytes 34603008 | tf_op jit(solution)/shard_map/dot_general | solution.py:1556
  1018.9 42.8 %fusion.38 = f32[1536,2048]{1,0:T(8,128)} fusion(bf16[5120,1536]{1,0:T(8,128)(2,1)} %get-tuple-element.43, bf16[5120,2048]{1,0:T(8,128)(2,1)} %get-tuple-element.44), kind=kOutput, calls=%fused_computation.90 | convolution fusion | flops 32212254720 | bytes 49283072 | tf_op jit(solution)/shard_map/dot_general | solution.py:1553
  1068.8 58.5 %gather_cotangents.1 = bf16[1024,2048]{1,0:T(8,128)(2,1)} custom-call(bf16[256,2048]{1,0:T(8,128)(2,1)} %fusion.32.refs_0_), custom_call_target="tpu_custom_call" | custom-call | tf_op jit(solution)/shard_map/gather_cotangents/pallas_call | solution.py:610
  1127.3 13.9 convolution_convert_fusion.4.dmix
  1141.3 40.3 %attention_back.1 = (bf16[1024,3072]{1,0:T(8,128)(2,1)}, f32[1024,128]{1,0:T(8,128)}) custom-call(s32[1]{0:T(128)S(6)} %copy.101.prefix, bf16[1024,3072]{1,0:T(8,128)(2,1)} %convolution_convert_fusion.2.q.k.v, bf16[1024,3072]{1,0:T(8,128)(2,1)} %convolution_convert_fusion.2.q.k.v, bf16[1024,3072]{1,0:T(8,128)(2,1)} %convolution_convert_fusion.2.q.k.v, ...), custom_call_target="tpu_custom_call" | custom-call | tf_op jit(solution)/shard_map/attention_back/pallas_call | solution.py:1073
  1181.6 19.6 %convolution_convert_fusion.3.source._ = bf16[1024,2048]{1,0:T(8,128)(2,1)} fusion(bf16[1024,3072]{1,0:T(8,128)(2,1)} %get-tuple-element.41, bf16[2048,3072]{1,0:T(8,128)(2,1)} %get-tuple-element.30), kind=kOutput, calls=%fused_computation.8 | convolution fusion | flops 12886999040 | bytes 23068672 | tf_op jit(solution)/shard_map/dot_general | solution.py:1589
  1201.2 54.9 %sum_attention.3 = f32[256,2048]{1,0:T(8,128)} custom-call(bf16[1024,2048]{1,0:T(8,128)(2,1)} %convolution_convert_fusion.3.source._, bf16[1024,2048]{1,0:T(8,128)(2,1)} %convolution_convert_fusion.3.source._), custom_call_target="tpu_custom_call" | custom-call | tf_op jit(solution)/shard_map/sum_attention/pallas_call | solution.py:798
  1257.7 16.2 all-reduce.3
  1283.2 19.6 %convolution_convert_fusion.source = bf16[2048,3072]{1,0:T(8,128)(2,1)} fusion(bf16[1024,2048]{1,0:T(8,128)(2,1)} %get-tuple-element.29, bf16[1024,3072]{1,0:T(8,128)(2,1)} %get-tuple-element.41), kind=kOutput, calls=%fused_computation | convolution fusion | flops 12891193344 | bytes 23068672 | tf_op jit(solution)/shard_map/dot_general | solution.py:1590
  1302.8 14.3 convolution_convert_fusion.1.source._
  1317.2 133.9 %sum_output_weight.1 = f32[256,2048]{1,0:T(8,128)} custom-call(bf16[2048,2048]{1,0:T(8,128)(2,1)} %convolution_convert_fusion.1.source._, bf16[2048,2048]{1,0:T(8,128)(2,1)} %convolution_convert_fusion.1.source._), custom_call_target="tpu_custom_call" | custom-call | tf_op jit(solution)/shard_map/sum_output_weight/pallas_call | solution.py:798
  1458.4 144.2 %sum_input_weight.1 = f32[256,3072]{1,0:T(8,128)} custom-call(bf16[2048,3072]{1,0:T(8,128)(2,1)} %convolution_convert_fusion.source, bf16[256,2048]{1,0:T(8,128)(2,1)} %reduce-scatter.3.cloned.1.call-done._), custom_call_target="tpu_custom_call" | custom-call | tf_op jit(solution)/shard_map/sum_input_weight/pallas_call | solution.py:798
  1605.6 10.7 slice_bitcast_fusion
  1620.1 6.4 all-to-all-start
  1634.6 11.1 all-to-all-done
  1649.2 6.6 reshape.177
  1655.7 6.8 copy.89
  (140 shorter events, 86.4 us)
Async XLA Ops:
  7.2 530.1 %all-gather.5.cloned.1.call-start = ((), (), s32[]{:S(2)}) async-start(), calls=%async_computation.4 | async-start | bytes 34603008 | tf_op jit(solution)/shard_map/all_gather | solution.py:1487
  7.9 1053.7 %all-reduce.9.cloned.1.call-start = ((), (), s32[]{:S(2)}) async-start(), calls=%async_computation.6 | async-start | bytes 262144
  11.7 394.6 %copy-start.20 = (s32[1,1024,2]{1,2,0:T(2,128)S(1)}, s32[1,1024,2]{1,2,0:T(2,128)}, u32[]{:S(2)}) copy-start(s32[1,1024,2]{1,2,0:T(2,128)} %param.16) | copy-start | bytes 24580
  411.6 50.6 %slice-start = ((s8[8388608]{0:T(1024)(128)(4,1)}), s8[4194304]{0:T(1024)(128)(4,1)S(1)}, s32[]{:S(2)}) async-start(s8[8388608]{0:T(1024)(128)(4,1)} %bitcast.119), calls=%async_computation.7 | async-start | bytes 8388608
  411.8 19.4 %copy-start = (f32[1024,128]{1,0:T(8,128)}, f32[1024,128]{1,0:T(8,128)S(1)}, u32[]{:S(2)}) copy-start(f32[1024,128]{1,0:T(8,128)S(1)} %select_maximum_fusion.side) | copy-start | bytes 1572868
  411.8 50.3 %slice-start.1 = ((s8[8388608]{0:T(1024)(128)(4,1)}), s8[4194304]{0:T(1024)(128)(4,1)S(1)}, s32[]{:S(2)}) async-start(s8[8388608]{0:T(1024)(128)(4,1)} %bitcast.119), calls=%async_computation.8 | async-start | bytes 8388608
  472.4 48.6 %copy-start.17 = (bf16[128,128]{1,0:T(8,128)(2,1)S(1)}, bf16[128,128]{1,0:T(8,128)(2,1)}, u32[]{:S(2)}) copy-start(bf16[128,128]{1,0:T(8,128)(2,1)} %get-tuple-element.34) | copy-start | bytes 98308
  521.0 9.9 copy-start.6
  521.0 9.9 copy-start.13
  531.0 5.0 copy-start.15
  531.4 4.7 copy-start.2
  837.1 621.2 %reduce-scatter.3.cloned.1.call-start = ((), (), s32[]{:S(2)}) async-start(), calls=%async_computation.2 | async-start | bytes 34603008 | tf_op jit(solution)/shard_map/reduce_scatter | solution.py:1568
  994.1 622.2 %all-reduce.7.cloned.1.call-start = ((), (), s32[]{:S(2)}) async-start(), calls=%async_computation.3 | async-start | bytes 262144 | tf_op jit(solution)/shard_map/psum | solution.py:1618
  1018.8 43.7 %copy-start.3 = (f32[256,2048]{1,0:T(8,128)S(1)}, f32[256,2048]{1,0:T(8,128)}, u32[]{:S(2)}) copy-start(f32[256,2048]{1,0:T(8,128)} %copy-done.2) | copy-start | bytes 6291460
  1061.6 5.6 copy-start.11
  1201.2 78.4 %copy-start.16 = (f32[2048]{0:T(1024)S(1)}, f32[2048]{0:T(1024)}, u32[]{:S(2)}) copy-start(f32[2048]{0:T(1024)} %param.19) | copy-start | bytes 24580
  1201.2 78.4 %copy-start.19 = (f32[256]{0:T(256)S(1)}, f32[256]{0:T(256)}, u32[]{:S(2)}) copy-start(f32[256]{0:T(256)} %copy-done.18) | copy-start | bytes 3076
  1256.1 23.5 %copy-start.7 = (bf16[1,256,2048]{2,1,0:T(8,128)(2,1)S(1)}, bf16[1,256,2048]{2,1,0:T(8,128)(2,1)}, u32[]{:S(2)}) copy-start(bf16[1,256,2048]{2,1,0:T(8,128)(2,1)} %param.14) | copy-start | bytes 3145732
  1256.1 23.5 %copy-start.12 = (f32[256,2048]{1,0:T(8,128)S(1)}, f32[256,2048]{1,0:T(8,128)}, u32[]{:S(2)}) copy-start(f32[256,2048]{1,0:T(8,128)} %sum_attention.3) | copy-start | bytes 6291460
  1302.8 346.4 %all-gather.7.cloned.1.call-start = ((), (), s32[]{:S(2)}) async-start(), calls=%async_computation.5 | async-start | bytes 2621440 | tf_op jit(solution)/shard_map/all_gather | solution.py:1631
  1453.8 172.8 %collective-permute-start = (bf16[256,2048]{1,0:T(8,128)(2,1)}, bf16[256,2048]{1,0:T(8,128)(2,1)}, u32[]{:S(2)}, u32[]{:S(2)}) collective-permute-start(bf16[256,2048]{1,0:T(8,128)(2,1)} %convert_element_type.146), channel_id=1, source_target_pairs={{0,0},{1,8},{2,16},{3,24},{4,4},{5,12},{6,20},{7,28},{8,1},{9,9},{... | collective-permute-start | bytes 3145736 | tf_op jit(solution)/shard_map/ppermute | solution.py:1626
  1619.1 10.5 copy-start.4
  1620.1 25.5 %all-to-all-start = ((bf16[256,4,512]{2,0,1:T(8,128)(2,1)}), bf16[256,4,512]{2,0,1:T(8,128)(2,1)}, u32[]{:S(2)}, u32[]{:S(2)}) async-start(bf16[256,4,512]{2,0,1:T(8,128)(2,1)} %bitcast.100), calls=%async_computation.1 | async-start | bytes 2097152 | tf_op jit(solution)/shard_map/all_to_all | solution.py:1628
  1626.6 3.0 copy-start.9
  (7 other events, 11.0 us)
Sparse Core Ops, SparseCore 0:
  10.9 343.1 all-gather.4
  837.3 123.7 all-reduce.8
  994.2 406.4 reduce-scatter.2
  1406.6 147.0 all-reduce.6
  1605.7 36.3 all-gather.6

commit v4 on v3

--- a/solution.py
+++ b/solution.py
@@ -627,16 +627,41 @@
     )(*arrays)
 
 
-def scatter_kernel(whose, rows, pieces, source, _, result, acc, *refs):
-    place = Place()
-    orders = [order for _, _, order in pieces]
-    flat = [order.replace("z", "") for order in orders]
+def add_into(target, terms, length):
+    @pl.loop(0, length // 16)
+    def _(r):
+        at = pl.ds(pl.multiple_of(r * 16, 16), 16)
+        total = target[at, :].astype(jnp.float32)
+        for term in terms:
+            total = total + term[at, :].astype(jnp.float32)
+        target[at, :] = total.astype(jnp.bfloat16)
+
+
+def scatter_rooms(rows, width, order):
+    steps, turns = len(order.replace("z", "")), CHIPS_Z if "z" in order else 1
+    blocks = [turns * 2 ** (steps - 1)]
+    blocks += [turns * 2 ** (steps - 1 - stage) for stage in range(steps)]
+    if "z" in order:
+        blocks.append(CHIPS_Z + 1)
+    return [pltpu.VMEM((n, rows, width), jnp.bfloat16) for n in blocks]
+
+
+def scatter_sems(order, pieces):
+    steps, turns = len(order.replace("z", "")), CHIPS_Z if "z" in order else 1
+    return [
+        pltpu.SemaphoreType.DMA((turns * 2 ** (steps - 1),)),
+        pltpu.SemaphoreType.DMA((pieces, steps, turns * 2 ** (steps - 1))),
+        pltpu.SemaphoreType.DMA((pieces, CHIPS_Z + 1)),
+    ]
+
+
+def scatter_plan(whose, rows, pieces, place, post, source, rooms, sems):
+    flat = [order.replace("z", "") for _, _, order in pieces]
     steps = len(flat[0])
-    lined = "z" in orders[0]
+    lined = "z" in pieces[0][2]
     turns = CHIPS_Z if lined else 1
-    bins = refs[:steps]
-    line = refs[steps] if lined else None
-    send_sems, load_sems, bin_sems, line_sems = refs[-4:]
+    acc, bins, line = rooms[0], rooms[1 : 1 + steps], rooms[-1]
+    load_sems, bin_sems, line_sems = sems
     z_here = place.at["z"]
     if lined:
         turn = [
@@ -646,22 +671,6 @@
     else:
         turn = [z_here]
     slot_z = lambda k: turn[k] if lined else 0
-    post = Post(send_sems, place)
-
-    def flips_of(p, stage, code):
-        later = flat[p][stage + 1 :]
-        flips = {a: (code >> i) & 1 for i, a in enumerate(later)}
-        if stage < steps:
-            flips[flat[p][stage]] = 1
-        return flips
-
-    def kept(p, flips):
-        names = sorted(flat[p][1:])
-        return sum(flips.get(a, 0) << i for i, a in enumerate(names))
-
-    def code_after(p, stage, flips):
-        return sum(flips.get(a, 0) << i for i, a in enumerate(flat[p][stage + 1 :]))
-
     keep = 2 ** (steps - 1)
     names = sorted(flat[0][1:])
     loads = {}
@@ -674,58 +683,49 @@
                 acc.at[at],
                 load_sems.at[at],
             )
-            loads[k, n].start()
-    enter(place, "".join(flat[0]) + ("z" if lined else ""))
     loaded = set()
-
-    def add(target, terms, length):
-        @pl.loop(0, length // 16)
-        def _(r):
-            at = pl.ds(pl.multiple_of(r * 16, 16), 16)
-            total = target[at, :].astype(jnp.float32)
-            for term in terms:
-                total = total + term[at, :].astype(jnp.float32)
-            target[at, :] = total.astype(jnp.bfloat16)
 
     def mine(p, ref):
         first, length, _ = pieces[p]
         return ref.at[pl.ds(first, length)]
 
+    def code_after(p, stage, flips):
+        return sum(flips.get(a, 0) << i for i, a in enumerate(flat[p][stage + 1 :]))
+
     def gathered(p, k, stage, flips):
-        n = kept(p, flips)
-        at = slot_z(k) * keep + n
+        n = sum(flips.get(a, 0) << i for i, a in enumerate(names))
         if (k, n) not in loaded:
             loads[k, n].wait()
             loaded.add((k, n))
         terms = []
         for before in range(stage):
-            code = code_after(p, before, flips)
-            width = 2 ** (steps - 1 - before)
-            ref = mine(p, bins[before].at[slot_z(k) * width + code])
-            post.arrived(ref, bin_sems.at[p, before, slot_z(k) * width + code])
+            at = slot_z(k) * 2 ** (steps - 1 - before) + code_after(p, before, flips)
+            ref = mine(p, bins[before].at[at])
+            post.arrived(ref, bin_sems.at[p, before, at])
             terms.append(ref)
-        block = mine(p, acc.at[at])
-        add(block, terms, pieces[p][1])
+        block = mine(p, acc.at[slot_z(k) * keep + n])
+        add_into(block, terms, pieces[p][1])
         return block
 
-    def leave(p, k, stage, code, block, flips):
-        axis = flat[p][stage]
-        width = 2 ** (steps - 1 - stage)
-        at = slot_z(k) * width + code
-        post.send(block, mine(p, bins[stage].at[at]), bin_sems.at[p, stage, at], place.across(axis))
-
-    def work(k, stage):
-        if stage < steps:
-            for code in reversed(range(2 ** (steps - 1 - stage))):
-                for p in range(len(pieces)):
-                    flips = flips_of(p, stage, code)
-                    if stage == 0:
-                        first, length, _ = pieces[p]
-                        at = place.block(whose, turn[k], flips) * rows + first
-                        leave(p, k, stage, code, source.at[pl.ds(at, length)], flips)
-                    else:
-                        leave(p, k, stage, code, gathered(p, k, stage, flips), flips)
-            return
+    def leave(k, stage):
+        for code in reversed(range(2 ** (steps - 1 - stage))):
+            for p in range(len(pieces)):
+                flips = {a: (code >> i) & 1 for i, a in enumerate(flat[p][stage + 1 :])}
+                flips[flat[p][stage]] = 1
+                if stage == 0:
+                    at = place.block(whose, turn[k], flips) * rows + pieces[p][0]
+                    block = source.at[pl.ds(at, pieces[p][1])]
+                else:
+                    block = gathered(p, k, stage, flips)
+                at = slot_z(k) * 2 ** (steps - 1 - stage) + code
+                post.send(
+                    block,
+                    mine(p, bins[stage].at[at]),
+                    bin_sems.at[p, stage, at],
+                    place.across(flat[p][stage]),
+                )
+
+    def settle(k):
         for p in range(len(pieces)):
             block = gathered(p, k, steps, {})
             if not lined or k == turns - 1:
@@ -736,7 +736,7 @@
             def pass_on(p=p, t=t, block=block):
                 ref = mine(p, line.at[t])
                 post.arrived(ref, line_sems.at[p, t])
-                add(block, [ref], pieces[p][1])
+                add_into(block, [ref], pieces[p][1])
 
             pl.when((right & (z_here > 0)) | (~right & (z_here < CHIPS_Z - 1)))(pass_on)
             slot = jnp.where(t == z_here - 1, CHIPS_Z, t)
@@ -747,65 +747,325 @@
                 place.along(jnp.where(right, 1, -1)),
             )
 
-    for k in range(turns):
-        work(k, 0)
+    def finish(p):
+        block = mine(p, acc.at[z_here * keep if lined else 0])
+        if lined:
+            for slot, there in ((z_here, z_here > 0), (CHIPS_Z, z_here < CHIPS_Z - 1)):
+
+                def last(slot=slot):
+                    ref = mine(p, line.at[slot])
+                    post.arrived(ref, line_sems.at[p, slot])
+                    add_into(block, [ref], pieces[p][1])
+
+                pl.when(there)(last)
+        return block
+
+    works = [(-1, lambda k=k: leave(k, 0)) for k in range(turns)]
     for time in range(turns + steps):
         for stage in range(1, steps + 1):
             k = time - stage + 1
             if 0 <= k < turns:
-                work(k, stage)
+                act = settle if stage == steps else lambda k, stage=stage: leave(k, stage)
+                works.append((time, lambda k=k, act=act: act(k)))
+    return list(loads.values()), works, finish
+
+
+def sends_of(order, pieces):
+    steps, turns = len(order.replace("z", "")), CHIPS_Z if "z" in order else 1
+    return pieces * (turns * 2**steps + 4)
+
+
+def widen(target, block, length):
+    @pl.loop(0, length // 16)
+    def _(r):
+        at = pl.ds(pl.multiple_of(r * 16, 16), 16)
+        target[at, :] = block[at, :].astype(jnp.float32)
+
+
+def scatter_kernel(whose, rows, pieces, filler, source, *refs):
+    given, refs = refs[: filler.operands], refs[filler.operands :]
+    result, made, refs = refs[0], refs[1 : 1 + filler.results], refs[1 + filler.results :]
+    rooms, refs = refs[: len(refs) - 4 - filler.rooms], refs[len(refs) - 4 - filler.rooms :]
+    send_sems, sems, own = refs[0], refs[1:4], refs[4:]
+    place = Place()
+    post = Post(send_sems, place)
+    loads, works, finish = scatter_plan(whose, rows, pieces, place, post, source, rooms, sems)
+    for load in loads:
+        load.start()
+    enter(place, "".join(a for a in "cxyz" if a in pieces[0][2]))
+    steps = filler.start(given, made, own)
+    slots = sum(1 for time, _ in works if time >= 0)
+    done = 0
+    for number, (time, act) in enumerate(works):
+        act()
+        if time >= 0:
+            share = steps * (number + 1 - (len(works) - slots)) // slots
+            filler.run(given, made, own, done, share)
+            done = share
     for p in range(len(pieces)):
         first, length, _ = pieces[p]
-        block = mine(p, acc.at[z_here * keep if lined else 0])
-        if lined:
-            for slot, there in ((z_here, z_here > 0), (CHIPS_Z, z_here < CHIPS_Z - 1)):
-
-                def last(p=p, slot=slot, block=block):
-                    ref = mine(p, line.at[slot])
-                    post.arrived(ref, line_sems.at[p, slot])
-                    add(block, [ref], pieces[p][1])
-
-                pl.when(there)(last)
-
-        @pl.loop(0, length // 16)
-        def _(r, first=first, block=block):
-            at = pl.ds(pl.multiple_of(r * 16, 16), 16)
-            result[pl.ds(pl.multiple_of(first + r * 16, 16), 16), :] = block[at, :].astype(
-                result.dtype
+        widen(result.at[pl.ds(first, length)], finish(p), length)
+    filler.end(given, made, own)
+    post.close()
+
+
+class Nothing:
+    operands = results = rooms = 0
+    shapes, scratch = [], []
+
+    def start(self, given, made, own):
+        return 0
+
+    def run(self, given, made, own, first, last):
+        pass
+
+    def end(self, given, made, own):
+        pass
+
+
+class After(Nothing):
+    operands = 1
+
+
+class WeightGrads:
+    operands, results, rooms = 4, 2, 6
+    TILE, CHUNK = 256, 512
+
+    def __init__(self, rows, wide, narrow, width):
+        self.chunks = rows // self.CHUNK
+        self.tiles = (wide // self.TILE, narrow // self.TILE)
+        self.shapes = [
+            jax.ShapeDtypeStruct((wide, width), jnp.float32),
+            jax.ShapeDtypeStruct((narrow, width), jnp.float32),
+        ]
+        self.scratch = [
+            pltpu.VMEM((2, self.CHUNK, self.TILE), jnp.bfloat16),
+            pltpu.VMEM((2, self.CHUNK, width), jnp.bfloat16),
+            pltpu.VMEM((self.TILE, width), jnp.float32),
+            pltpu.VMEM((self.TILE, width), jnp.float32),
+            pltpu.SemaphoreType.DMA((2, 2)),
+            pltpu.SemaphoreType.DMA((2,)),
+        ]
+
+    def copies(self, given, own, step, second):
+        tile, chunk = step // self.chunks - (self.tiles[0] if second else 0), step % self.chunks
+        slot = step % 2
+        rows = pl.ds(pl.multiple_of(chunk * self.CHUNK, self.CHUNK), self.CHUNK)
+        cols = pl.ds(pl.multiple_of(tile * self.TILE, self.TILE), self.TILE)
+        left, right = given[2 * second], given[2 * second + 1]
+        return [
+            pltpu.make_async_copy(left.at[rows, cols], own[0].at[slot], own[4].at[slot, 0]),
+            pltpu.make_async_copy(right.at[rows], own[1].at[slot], own[4].at[slot, 1]),
+        ]
+
+    def fetch(self, given, own, step, start):
+        edge = self.tiles[0] * self.chunks
+        for second in (0, 1):
+
+            @pl.when((step >= edge) if second else (step < edge))
+            def _(second=second):
+                for copy in self.copies(given, own, step, second):
+                    copy.start() if start else copy.wait()
+
+    def put(self, made, own, tile, parity, start):
+        for second in (0, 1):
+
+            @pl.when((tile >= self.tiles[0]) if second else (tile < self.tiles[0]))
+            def _(second=second):
+                at = tile - (self.tiles[0] if second else 0)
+                rows = pl.ds(pl.multiple_of(at * self.TILE, self.TILE), self.TILE)
+                copy = pltpu.make_async_copy(
+                    own[2 + parity], made[second].at[rows], own[5].at[parity]
+                )
+                copy.start() if start else copy.wait()
+
+    def start(self, given, made, own):
+        self.fetch(given, own, jnp.int32(0), True)
+        return sum(self.tiles) * self.chunks
+
+    def run(self, given, made, own, first, last):
+        total = sum(self.tiles) * self.chunks
+
+        @pl.loop(first, last)
+        def _(step):
+            tile, chunk = step // self.chunks, step % self.chunks
+
+            @pl.when(step + 1 < total)
+            def _():
+                self.fetch(given, own, step + 1, True)
+
+            self.fetch(given, own, step, False)
+            part = lax.dot_general(
+                own[0][step % 2], own[1][step % 2], DOWNWARD, preferred_element_type=jnp.float32
             )
-
-    post.close()
-
-
-def scatter(array, whose, pieces, collective_id, name, after=None):
+            for parity in (0, 1):
+
+                @pl.when(tile % 2 == parity)
+                def _(parity=parity):
+                    acc = own[2 + parity]
+
+                    @pl.when(chunk == 0)
+                    def _():
+                        @pl.when(tile >= 2)
+                        def _():
+                            self.put(made, own, tile - 2, parity, False)
+
+                        acc[...] = part
+
+                    @pl.when(chunk > 0)
+                    def _():
+                        acc[...] += part
+
+                    @pl.when(chunk == self.chunks - 1)
+                    def _():
+                        self.put(made, own, tile, parity, True)
+
+    def end(self, given, made, own):
+        tiles = sum(self.tiles)
+        for tile in (tiles - 2, tiles - 1):
+            self.put(made, own, jnp.int32(tile), tile % 2, False)
+
+
+def scatter(array, whose, pieces, collective_id, name, filler=Nothing(), operands=()):
     size = {"all": 32, "dp": 8, "expert": 4}[whose]
     rows, width = array.shape[0] // size, array.shape[1]
-    flat = pieces[0][2].replace("z", "")
-    steps, lined = len(flat), "z" in pieces[0][2]
-    turns = CHIPS_Z if lined else 1
-    room = lambda blocks: pltpu.VMEM((blocks, rows, width), jnp.bfloat16)
-    scratch = [room(turns * 2 ** (steps - 1))]
-    scratch += [room(turns * 2 ** (steps - 1 - stage)) for stage in range(steps)]
-    if lined:
-        scratch.append(room(CHIPS_Z + 1))
-    count = len(pieces)
-    scratch += [
-        pltpu.SemaphoreType.DMA((count * (turns * 2**steps + 4),)),
-        pltpu.SemaphoreType.DMA((turns * 2 ** (steps - 1),)),
-        pltpu.SemaphoreType.DMA((count, steps, turns * 2 ** (steps - 1))),
-        pltpu.SemaphoreType.DMA((count, CHIPS_Z + 1)),
-    ]
-    return pl.pallas_call(
-        functools.partial(scatter_kernel, whose, rows, pieces),
-        out_shape=jax.ShapeDtypeStruct((rows, width), jnp.float32),
-        in_specs=[pl.BlockSpec(memory_space=pltpu.HBM), pl.BlockSpec(memory_space=pl.ANY)],
-        out_specs=pl.BlockSpec(memory_space=pltpu.VMEM),
-        scratch_shapes=scratch,
+    order, count = pieces[0][2], len(pieces)
+    hbm = pl.BlockSpec(memory_space=pltpu.HBM)
+    out = pl.pallas_call(
+        functools.partial(scatter_kernel, whose, rows, pieces, filler),
+        out_shape=[jax.ShapeDtypeStruct((rows, width), jnp.float32)] + filler.shapes,
+        in_specs=[hbm] * (1 + len(operands)),
+        out_specs=[pl.BlockSpec(memory_space=pltpu.VMEM)] + [hbm] * filler.results,
+        scratch_shapes=scatter_rooms(rows, width, order)
+        + [pltpu.SemaphoreType.DMA((sends_of(order, count),))]
+        + scatter_sems(order, count)
+        + filler.scratch,
         compiler_params=pltpu.CompilerParams(
-            collective_id=collective_id, has_side_effects=True, vmem_limit_bytes=62 * 2**20
+            collective_id=collective_id, has_side_effects=True, vmem_limit_bytes=63 * 2**20
         ),
         name=name,
-    )(array, array if after is None else after)
+    )(array, *operands)
+    return out if filler.results else out[0]
+
+
+def sum_weights_kernel(rows, pieces, in_grad, out_grad, after, query, keyvalue, output, *refs):
+    count = len(scatter_rooms(rows, 128, pieces[0][2]))
+    in_rooms, out_rooms = refs[:count], refs[count : 2 * count]
+    dealt, shared, out_dealt = refs[2 * count : 2 * count + 3]
+    send_sems, deal_sems = refs[2 * count + 3 : 2 * count + 5]
+    in_sems, out_sems = refs[2 * count + 5 : 2 * count + 8], refs[2 * count + 8 :]
+    place = Place()
+    post = Post(send_sems, place)
+    z, y, e = place.at["z"], place.at["y"], place.expert
+    wide = query.shape[1]
+    span = (in_grad.shape[1] - wide) // 2
+    partner, moves = (e * 2 + y, z), z != e
+    peers = []
+    for flip_x, flip_c in ((1, 1), (1, 0), (0, 1)):
+        x = place.at["x"] + flip_x * (1 - 2 * place.at["x"])
+        core = place.at["c"] + flip_c * (1 - 2 * place.at["c"])
+        peers.append((x * 2 + core, flip_x * 2 + flip_c))
+    in_loads, in_works, in_finish = scatter_plan(
+        "dp", rows, pieces, place, post, in_grad, in_rooms, in_sems
+    )
+    out_loads, out_works, out_finish = scatter_plan(
+        "dp", rows, pieces, place, post, out_grad, out_rooms, out_sems
+    )
+    for load in in_loads + out_loads:
+        load.start()
+    enter(place, "cxyz", [((place.dp, peers[0][0]), None), (partner, moves)])
+    for (_, one), (_, other) in zip(in_works, out_works):
+        one()
+        other()
+    cols = lambda block: pl.ds(pl.multiple_of(block * span, span), span)
+    keep = slice(wide, wide + 2 * span)
+    for p in range(len(pieces)):
+        first, length, _ = pieces[p]
+        at = pl.ds(first, length)
+        block = in_finish(p)
+        for n, (peer, flips) in enumerate(peers):
+            post.send(
+                block.at[:, cols(peer)],
+                dealt.at[at, cols(e)],
+                deal_sems.at[p, flips],
+                (place.dp, peer),
+            )
+        post.send(block.at[:, keep], shared.at[2, at], deal_sems.at[p, 4], place.across("x"))
+        post.send(block.at[:, keep], shared.at[1, at], deal_sems.at[p, 5], place.across("c"))
+        done = out_finish(p)
+        post.send(done, out_dealt.at[at], deal_sems.at[p, 6], partner, moves)
+
+    def place_keys(p, flips, block):
+        first, length, _ = pieces[p]
+        rows_at = pl.ds(first, length)
+        x = place.at["x"] + (flips // 2) * (1 - 2 * place.at["x"])
+        core = place.at["c"] + (flips % 2) * (1 - 2 * place.at["c"])
+        owner = x * 2 + core
+        widen(keyvalue.at[rows_at, cols(owner)], block.at[:, pl.ds(0, span)], length)
+        widen(
+            keyvalue.at[rows_at, cols(wide // span + owner)], block.at[:, pl.ds(span, span)], length
+        )
+
+    for p in range(len(pieces)):
+        first, length, _ = pieces[p]
+        at = pl.ds(first, length)
+        post.arrived(shared.at[2, at], deal_sems.at[p, 4])
+        post.send(shared.at[2, at], shared.at[3, at], deal_sems.at[p, 7], place.across("c"))
+        block = in_rooms[0].at[z, at]
+        widen(query.at[at, cols(e)], block.at[:, cols(e)], length)
+        place_keys(p, 0, block.at[:, keep])
+        place_keys(p, 2, shared.at[2, at])
+        post.arrived(shared.at[1, at], deal_sems.at[p, 5])
+        place_keys(p, 1, shared.at[1, at])
+        for peer, flips in peers:
+            post.arrived(dealt.at[at, cols(peer)], deal_sems.at[p, flips])
+            widen(query.at[at, cols(peer)], dealt.at[at, cols(peer)], length)
+
+        def came(p=p, at=at, length=length):
+            post.arrived(out_dealt.at[at], deal_sems.at[p, 6])
+            widen(output.at[at], out_dealt.at[at], length)
+
+        pl.when(moves)(came)
+        pl.when(~moves)(
+            lambda at=at, length=length: widen(output.at[at], out_rooms[0].at[z, at], length)
+        )
+        post.arrived(shared.at[3, at], deal_sems.at[p, 7])
+        place_keys(p, 3, shared.at[3, at])
+    post.close()
+
+
+def sum_weights(in_grad, out_grad, after, pieces, collective_id):
+    rows, wide = out_grad.shape[0] // 8, out_grad.shape[1]
+    order, count = pieces[0][2], len(pieces)
+    total = in_grad.shape[1]
+    hbm = pl.BlockSpec(memory_space=pltpu.HBM)
+    vmem = pl.BlockSpec(memory_space=pltpu.VMEM)
+    shape = jax.ShapeDtypeStruct
+    return pl.pallas_call(
+        functools.partial(sum_weights_kernel, rows, pieces),
+        out_shape=[
+            shape((rows, wide), jnp.float32),
+            shape((rows, 2 * wide), jnp.float32),
+            shape((rows, wide), jnp.float32),
+        ],
+        in_specs=[hbm] * 3,
+        out_specs=[vmem] * 3,
+        scratch_shapes=scatter_rooms(rows, total, order)
+        + scatter_rooms(rows, wide, order)
+        + [
+            pltpu.VMEM((rows, wide), jnp.bfloat16),
+            pltpu.VMEM((4, rows, total - wide), jnp.bfloat16),
+            pltpu.VMEM((rows, wide), jnp.bfloat16),
+            pltpu.SemaphoreType.DMA((2 * sends_of(order, count) + 8 * count,)),
+            pltpu.SemaphoreType.DMA((count, 8)),
+        ]
+        + scatter_sems(order, count)
+        + scatter_sems(order, count),
+        compiler_params=pltpu.CompilerParams(
+            collective_id=collective_id, has_side_effects=True, vmem_limit_bytes=63 * 2**20
+        ),
+        name="sum_weights",
+    )(in_grad, out_grad, after)
 
 
 def weights_kernel(jobs, *refs):
@@ -1139,6 +1399,8 @@
     acts,
     dx_buf,
     out_buf,
+    dxs,
+    outs,
     send_sems,
     arrive_sems,
     own_sem,
@@ -1343,18 +1605,21 @@
         @pl.loop(0, width // 256)
         def _(n):
             cols = pl.ds(pl.multiple_of(n * 256, 256), 256)
-            dx = jnp.dot(ds[s], w_in[:, cols], preferred_element_type=f32).astype(low)
-            out = jnp.dot(acts[s], w_down[:, cols], preferred_element_type=f32).astype(low)
-            for b in range(2):
-                at = slice(b * slot_count, (b + 1) * slot_count)
-                table = spread[b].astype(low)
-                to = pl.ds(b * tok, tok)
-                dx_buf[s, to, cols] = lax.dot_general(
-                    table, dx[at], DOWNWARD, preferred_element_type=f32
-                ).astype(low)
-                out_buf[s, to, cols] = lax.dot_general(
-                    table, out[at], DOWNWARD, preferred_element_type=f32
-                ).astype(low)
+            dxs[:, cols] = jnp.dot(ds[s], w_in[:, cols], preferred_element_type=f32).astype(low)
+            outs[:, cols] = jnp.dot(acts[s], w_down[:, cols], preferred_element_type=f32).astype(
+                low
+            )
+
+        for b in range(2):
+            at = pl.ds(b * slot_count, slot_count)
+            back_table = spread[b].T.astype(low)
+            to = pl.ds(b * tok, tok)
+            dx_buf[s, to, :] = jnp.dot(
+                back_table, dxs[at, :], preferred_element_type=f32
+            ).astype(low)
+            out_buf[s, to, :] = jnp.dot(
+                back_table, outs[at, :], preferred_element_type=f32
+            ).astype(low)
 
     @pl.loop(0, chips)
     def _(u):
@@ -1436,6 +1701,8 @@
             pltpu.VMEM((2, pair, padded), low),
             pltpu.VMEM((2, 2 * tok, width), low),
             pltpu.VMEM((2, 2 * tok, width), low),
+            pltpu.VMEM((pair, width), low),
+            pltpu.VMEM((pair, width), low),
             pltpu.SemaphoreType.DMA((10 * chips,)),
             pltpu.SemaphoreType.DMA((16 * CHIPS_Z,)),
             pltpu.SemaphoreType.DMA,
@@ -1477,15 +1744,6 @@
     low = jnp.bfloat16
     f32 = jnp.float32
 
-    half = dp_size // group_size
-    swap = [
-        ((z * half + y) * group_size + e, (e * half + y) * group_size + z)
-        for z in range(group_size)
-        for y in range(half)
-        for e in range(group_size)
-    ]
-    cot_everyone = lax.all_gather(cotangent[0], ("dp", "expert"), axis=0, tiled=True)
-
     normed_attention, unit_attention, factor_attention = norm_parts(inputs, gain_attention)
     attention_in = normed_attention.astype(low)
     quarters = lambda order: tuple(
@@ -1495,10 +1753,11 @@
     route_shard = feedforward_routes[0].astype(low).reshape(-1, 128)
     router_shard = router_weight.T.reshape(-1, 128)
     whole = lambda a: ((0, a.shape[0], "zy"),)
-    cut = rows_in * 13 // 16
-    sequence_in, every_route, router_full, in_weight, out_weight = gather_weights(
+    cut = rows_in * 12 // 16
+    sequence_in, cot_everyone, every_route, router_full, in_weight, out_weight = gather_weights(
         [
             (attention_in, "expert", quarters("xc")),
+            (cotangent[0], "all", quarters("zyxc")),
             (route_shard, "dp", whole(route_shard)),
             (router_shard, "dp", whole(router_shard)),
         ],
@@ -1550,12 +1809,6 @@
         others,
         slot_count,
     )
-    grad_in_feed = lax.dot_general(kept_back, kept_rows, DOWNWARD, preferred_element_type=f32)
-    grad_gate = grad_in_feed[:hidden_rows]
-    grad_up = grad_in_feed[padded : padded + hidden_rows]
-    grad_down = lax.dot_general(
-        kept_act[:, :hidden_rows], kept_cots, DOWNWARD, preferred_element_type=f32
-    )
     own_row = (jnp.arange(group_size) == my_index).astype(f32)[None, :, None]
     feed_dgate = lax.psum_scatter(
         (token_dgate[:, None, :] * own_row).reshape(-1, tok_rows),
@@ -1563,7 +1816,18 @@
         scatter_dimension=0,
         tiled=True,
     ).T
-    feed_home = scatter(dx_part, "all", everywhere("cxyz", "cyxz"), 4, "sum_rows")
+    feed_home, grad_in_feed, grad_down = scatter(
+        dx_part,
+        "all",
+        everywhere("cxyz", "cyxz"),
+        4,
+        "sum_rows",
+        WeightGrads(kept_rows.shape[0], 2 * padded, padded, model_width),
+        (kept_back, kept_rows, kept_act, kept_cots),
+    )
+    grad_gate = grad_in_feed[:hidden_rows]
+    grad_up = grad_in_feed[padded : padded + hidden_rows]
+    grad_down = grad_down[:hidden_rows]
     out_part, feed_home = lax.optimization_barrier((out_part, feed_home))
     feed_sum = lax.psum_scatter(
         out_part,
@@ -1618,22 +1882,8 @@
     small = lax.psum(small.astype(f32), ("dp", "expert"))
     small = lax.dynamic_slice_in_dim(small, lax.axis_index("dp") * rows_in, rows_in, 1)
 
-    down_dp = ((0, rows_in, "yz"),)
-    out_rows = scatter(grad_out.astype(low), "dp", down_dp, 6, "sum_output_weight")
-    in_rows = scatter(
-        grad_in.astype(low), "dp", down_dp, 7, "sum_input_weight", feed_sum
-    ).astype(low)
-    grad_projection = lax.ppermute(out_rows.astype(low), ("dp", "expert"), swap).astype(f32)
-    wide = group_size * span
-    grad_query = lax.all_to_all(
-        in_rows[:, :wide], "expert", split_axis=1, concat_axis=1, tiled=True
-    ).astype(f32)
-    grad_keyvalue = lax.all_gather(in_rows[:, wide:], "expert", axis=0, tiled=False)
-    grad_keyvalue = (
-        grad_keyvalue.reshape(group_size, rows_in, 2, span)
-        .transpose(1, 2, 0, 3)
-        .reshape(rows_in, 2 * query_width)
-        .astype(f32)
+    grad_query, grad_keyvalue, grad_projection = sum_weights(
+        grad_in.astype(low), grad_out.astype(low), feed_sum, ((0, rows_in, "yz"),), 6
     )
     return (
         layer_output.astype(low)[None],

time: 1690 us -> 1870 us (1.11)
  waiting for transfers between devices: 11.9 us -> 445 us
  Pallas kernels: 1350 us -> 1210 us
  matrix products: 176 us -> 108 us
    reduce_scatter x1, waiting for transfers between devices: 0.02 us -> 357 us  [per_device_torus(): lax.psum_scatter(out_part, ('dp', 'expert'), scatter_dimension=0, tiled=T...]
    psum x1, waiting for transfers between devices: 0.01 us -> 87.7 us  [per_device_torus(): small = lax.psum(small.astype(f32), ('dp', 'expert'))]
    dot_general x2 -> x0, matrix products: 64.6 us -> none  [the longest x1 42.8 us: per_device_torus(): lax.dot_general(kept_back, kept_rows, DOWNWARD, preferred_element_type=f32)]
    pallas_call x1, Pallas kernels: 389 us -> 343 us  [gather_weights(): pl.pallas_call(functools.partial(weights_kernel, plan), out_shape=shards...]
    pallas_call x1, Pallas kernels: 298 us -> 253 us  [feed(): pl.pallas_call(functools.partial(feed_kernel, tok, slot_count), in_specs=...]
    pallas_call x5 -> x4, Pallas kernels: 538 us -> 505 us  [the longest x1 286 us: sum_weights(): pl.pallas_call(functools.partial(sum_weights_kernel, rows, pieces), out_s...]
    pallas_call x1, Pallas kernels: 58.5 us -> 38.5 us  [gather(): pl.pallas_call(functools.partial(gather_kernel, plan, axes), out_shape=[j...]
    convert_element_type x3 -> x0, local copies, waits for them, and re-layouts: 19.4 us -> none  [per_device_torus(): grad_keyvalue = grad_keyvalue.reshape(group_size, rows_in, 2, span).trans...]
  transfers between devices with their start and end apart: 7 -> 3, of which waited for: 1 -> 2; matrix products, arithmetic and copies ran while one was open for 14% -> 3% of each run, Pallas kernels for 63% -> 9%
where the time goes in v4:
time: 1870 us; the launch traced here: 1860 us
  Pallas kernels  1210 us (65%)
  waiting for transfers between devices  445 us (24%)
  matrix products  108 us (6%)
  local copies, waits for them, and re-layouts  44.1 us (2%)
  other arithmetic  25.8 us (1%)
    reduce_scatter x1, waiting for transfers between devices, per_device_torus(): lax.psum_scatter(out_part, ('dp', 'expert'), scatter_dimension=0, tiled=T...  357 us
    pallas_call x1, Pallas kernels, gather_weights(): pl.pallas_call(functools.partial(weights_kernel, plan), out_shape=shards...  343 us
    pallas_call x1, Pallas kernels, sum_weights(): pl.pallas_call(functools.partial(sum_weights_kernel, rows, pieces), out_s...  286 us
    pallas_call x1, Pallas kernels, feed(): pl.pallas_call(functools.partial(feed_kernel, tok, slot_count), in_specs=...  253 us
    pallas_call x3, Pallas kernels, scatter(): pl.pallas_call(functools.partial(scatter_kernel, whose, rows, pieces, fil...  219 us
    psum x1, waiting for transfers between devices, per_device_torus(): small = lax.psum(small.astype(f32), ('dp', 'expert'))  87.7 us
    pallas_call x1, Pallas kernels, attention_back(): pl.pallas_call(functools.partial(attention_back_kernel, experts), grid=(l...  40 us
    pallas_call x1, Pallas kernels, gather(): pl.pallas_call(functools.partial(gather_kernel, plan, axes), out_shape=[j...  38.5 us
  transfers between devices with their start and end apart: 3, of which 2 were waited for; matrix products, arithmetic and copies ran while one was open for 3% of the time, Pallas kernels for 9%

profile of v4, /device:TPU:2, one launch (start us, length us, event | category | flops | bytes accessed | tf_op | source)
XLA Modules:
  0.0 1859.0 jit_solution(8874202773273568742)
XLA Ops:
  15.0 342.7 %gather_weights.1 = (bf16[256,3072]{1,0:T(8,128)(2,1)}, bf16[256,2048]{1,0:T(8,128)(2,1)}, bf16[1024,2048]{1,0:T(8,128)(2,1)}, bf16[8192,2048]{1,0:T(8,128)(2,1)...) custom-call(bf16[256,2048]{1,0:T(8,128)(2,1)} %fusion.4.refs_0_, ...), custom_call_target="tpu_custom_call" | custom-call | tf_op jit(solution)/shard_map/gather_weights/pallas_call | solution.py:1149
  362.1 17.6 convolution_convert_fusion.2.q.k.v
  380.9 29.2 %attention.1 = (bf16[1024,2048]{1,0:T(8,128)(2,1)S(1)}, f32[1024,1024]{1,0:T(8,128)}) custom-call(s32[1]{0:T(128)S(6)} %copy.75.prefix, bf16[1024,3072]{1,0:T(8,128)(2,1)} %convolution_convert_fusion.2.q.k.v, bf16[1024,3072]{1,0:T(8,128)(2,1)} %convolution_convert_fusion.2.q.k.v, bf16[1024,3072]{1,0:T(8,128)(2,1)} %convolution_convert_fusion.2.q.k.v, ...), custom_call_target="tpu_custom_call" | custom-call | tf_op jit(solution)/shard_map/attention/pallas_call | solution.py:1238
  412.1 10.3 convolution_convert_fusion.5.source
  422.4 29.8 %sum_attention.2 = f32[256,2048]{1,0:T(8,128)} custom-call(bf16[1024,2048]{1,0:T(8,128)(2,1)} %convolution_convert_fusion.5.source), custom_call_target="tpu_custom_call" | custom-call | tf_op jit(solution)/shard_map/sum_attention/pallas_call | solution.py:934
  454.5 5.5 reshape.153
  469.7 253.1 %feed_forward.1 = (bf16[8192,2048]{1,0:T(8,128)(2,1)}, bf16[8192,2048]{1,0:T(8,128)(2,1)}, bf16[8192,2048]{1,0:T(8,128)(2,1)}, bf16[5120,2048]{1,0:T(8,128)(2,1)...) custom-call(bf16[256,2048]{1,0:T(8,128)(2,1)} %multiply_convert_fusio, ...), custom_call_target="tpu_custom_call" | custom-call | tf_op jit(solution)/shard_map/feed_forward/pallas_call | solution.py:1677
  725.0 159.6 %sum_rows.1 = (f32[256,2048]{1,0:T(8,128)}, f32[1536,2048]{1,0:T(8,128)}, f32[768,2048]{1,0:T(8,128)}) custom-call(bf16[8192,2048]{1,0:T(8,128)(2,1)} %get-tuple-element.44.source, bf16[5120,1536]{1,0:T(8,128)(2,1)} %get-tuple-element.45.refs_0_, bf16[5120,2048]{1,0:T(8,128)(2,1)} %get-tuple-element.46.refs_1_, bf16[5120,768]{1,0:T(8,128)(2,1)} %get-tuple-element.47.refs_2_, ...), custom_call_target="tpu_custom_call" | custom-call | tf_op jit(solution)/shard_map/sum_rows/pallas_call | solution.py:934
  889.1 4.0 multiply_reduce_fusion
  896.1 38.5 %gather_cotangents.1 = bf16[1024,2048]{1,0:T(8,128)(2,1)} custom-call(bf16[256,2048]{1,0:T(8,128)(2,1)} %fusion.27.refs_0_), custom_call_target="tpu_custom_call" | custom-call | tf_op jit(solution)/shard_map/gather_cotangents/pallas_call | solution.py:610
  934.6 13.9 convolution_convert_fusion.4.dmix
  948.5 40.0 %attention_back.1 = (bf16[1024,3072]{1,0:T(8,128)(2,1)}, f32[1024,128]{1,0:T(8,128)}) custom-call(s32[1]{0:T(128)S(6)} %copy.75.prefix, bf16[1024,3072]{1,0:T(8,128)(2,1)} %convolution_convert_fusion.2.q.k.v, bf16[1024,3072]{1,0:T(8,128)(2,1)} %convolution_convert_fusion.2.q.k.v, bf16[1024,3072]{1,0:T(8,128)(2,1)} %convolution_convert_fusion.2.q.k.v, ...), custom_call_target="tpu_custom_call" | custom-call | tf_op jit(solution)/shard_map/attention_back/pallas_call | solution.py:1333
  988.5 19.5 %convolution_convert_fusion.3.source = bf16[1024,2048]{1,0:T(8,128)(2,1)} fusion(bf16[1024,3072]{1,0:T(8,128)(2,1)} %get-tuple-element.54, bf16[2048,3072]{1,0:T(8,128)(2,1)} %get-tuple-element.37), kind=kOutput, calls=%fused_computation.7 | convolution fusion | flops 12886999040 | bytes 23068672 | tf_op jit(solution)/shard_map/dot_general | solution.py:1853
  1008.0 29.4 %sum_attention.3 = f32[256,2048]{1,0:T(8,128)} custom-call(bf16[1024,2048]{1,0:T(8,128)(2,1)} %convolution_convert_fusion.3.source), custom_call_target="tpu_custom_call" | custom-call | tf_op jit(solution)/shard_map/sum_attention/pallas_call | solution.py:934
  1038.9 12.1 all-reduce.3
  1053.3 4.4 fusion.10
  1059.2 5.9 slice_bitcast_fusion
  1065.1 10.8 slice_bitcast_fusion.1
  1075.9 11.7 convolution_convert_fusion.1.out_grad
  1087.6 18.4 convolution_convert_fusion.in_grad
  1106.0 87.7 %all-reduce.7.cloned.1.call-done = f32[10,2048]{1,0:T(8,128)} async-done(((f32[10,2048]{1,0:T(8,128)}), f32[10,2048]{1,0:T(8,128)}) %all-reduce.7.cloned.1.call-update) | async-done | bytes 81936 | tf_op jit(solution)/shard_map/psum | solution.py:1882
  1196.4 356.6 %reduce-scatter.3.cloned.1.call-done.after = bf16[256,2048]{1,0:T(8,128)(2,1)} async-done(((bf16[8192,2048]{1,0:T(8,128)(2,1)}), bf16[256,2048]{1,0:T(8,128)(2,1)}) %reduce-scatter.3.cloned.1.call-update) | async-done | bytes 1048592 | tf_op jit(solution)/shard_map/reduce_scatter | solution.py:1832
  1553.0 285.8 %sum_weights.1 = (f32[256,2048]{1,0:T(8,128)}, f32[256,4096]{1,0:T(8,128)}, f32[256,2048]{1,0:T(8,128)}) custom-call(bf16[2048,3072]{1,0:T(8,128)(2,1)} %convolution_convert_fusion.in_grad, bf16[2048,2048]{1,0:T(8,128)(2,1)} %convolution_convert_fusion.1.out_grad, bf16[256,2048]{1,0:T(8,128)(2,1)} %reduce-scatter.3.cloned.1.call-done.after), custom_call_target="tpu_custom_call" | custom-call | tf_op jit(solution)/shard_map/sum_weights/pallas_call | solution.py:1044
  1838.8 6.6 fusion.9
  (119 shorter events, 50.0 us)
Async XLA Ops:
  7.2 879.4 %all-reduce.9.cloned.1.call-start = ((), (), s32[]{:S(2)}) async-start(), calls=%async_computation.3 | async-start | bytes 262144
  8.7 349.0 %copy-start.18 = (f32[256]{0:T(256)}, f32[256]{0:T(256)S(1)}, u32[]{:S(2)}) copy-start(f32[256]{0:T(256)S(1)} %add_rsqrt_fusion.1) | copy-start | bytes 3076
  358.5 3.6 copy-start.9
  362.1 17.6 copy-start.20
  380.7 31.4 %slice-start = ((s8[8388608]{0:T(1024)(128)(4,1)}), s8[4194304]{0:T(1024)(128)(4,1)S(1)}, s32[]{:S(2)}) async-start(s8[8388608]{0:T(1024)(128)(4,1)} %bitcast.104), calls=%async_computation.4 | async-start | bytes 8388608
  380.9 29.2 %copy-start = (f32[1024,128]{1,0:T(8,128)}, f32[1024,128]{1,0:T(8,128)S(1)}, u32[]{:S(2)}) copy-start(f32[1024,128]{1,0:T(8,128)S(1)} %select_maximum_fusion.side) | copy-start | bytes 1572868
  380.9 31.2 %slice-start.1 = ((s8[8388608]{0:T(1024)(128)(4,1)}), s8[4194304]{0:T(1024)(128)(4,1)S(1)}, s32[]{:S(2)}) async-start(s8[8388608]{0:T(1024)(128)(4,1)} %bitcast.104), calls=%async_computation.5 | async-start | bytes 8388608
  454.5 14.0 copy-start.3
  463.0 5.5 copy-start.15
  469.7 254.9 %copy-start.7 = (bf16[256,2048]{1,0:T(8,128)(2,1)S(1)}, bf16[256,2048]{1,0:T(8,128)(2,1)}, u32[]{:S(2)}) copy-start(bf16[256,2048]{1,0:T(8,128)(2,1)} %multiply_convert_fusion.own_rows) | copy-start | bytes 3145732
  724.5 469.2 %all-reduce.7.cloned.1.call-start = ((), (), s32[]{:S(2)}) async-start(), calls=%async_computation.2 | async-start | bytes 262144 | tf_op jit(solution)/shard_map/psum | solution.py:1882
  725.0 159.7 %copy-start.21 = (u32[32]{0:T(128)S(1)}, u32[32]{0:T(128)}, u32[]{:S(2)}) copy-start(u32[32]{0:T(128)} %constant.63) | copy-start | bytes 388
  889.1 5.3 copy-start.4
  889.1 5.3 copy-start.8
  1008.0 45.2 %copy-start.16 = (f32[2048]{0:T(1024)S(1)}, f32[2048]{0:T(1024)}, u32[]{:S(2)}) copy-start(f32[2048]{0:T(1024)} %param.19) | copy-start | bytes 24580
  1008.0 45.2 %copy-start.19 = (f32[256]{0:T(256)S(1)}, f32[256]{0:T(256)}, u32[]{:S(2)}) copy-start(f32[256]{0:T(256)} %copy-done.18) | copy-start | bytes 3076
  1037.4 15.8 copy-start.5
  1058.4 494.6 %reduce-scatter.3.cloned.1.call-start = ((), (), s32[]{:S(2)}) async-start(), calls=%async_computation.1 | async-start | bytes 34603008 | tf_op jit(solution)/shard_map/reduce_scatter | solution.py:1832
  1065.0 10.8 copy-start.2
  1065.1 10.8 copy-start.11
  1075.9 11.7 copy-start.10
  1838.8 6.7 copy-start.12
  1845.5 3.1 copy-start.14
  1848.6 2.3 copy-start.13
  (3 other events, 5.6 us)
Sparse Core Ops, SparseCore 0:
  724.6 124.6 all-reduce.8
  1058.5 135.0 all-reduce.6
  1196.0 356.9 reduce-scatter.2

commit v5 on v4

--- a/solution.py
+++ b/solution.py
@@ -782,7 +782,8 @@
         target[at, :] = block[at, :].astype(jnp.float32)
 
 
-def scatter_kernel(whose, rows, pieces, filler, source, *refs):
+def scatter_kernel(whose, rows, pieces, columns, filler, source, *refs):
+    source = source.at[:, pl.ds(*columns)]
     given, refs = refs[: filler.operands], refs[filler.operands :]
     result, made, refs = refs[0], refs[1 : 1 + filler.results], refs[1 + filler.results :]
     rooms, refs = refs[: len(refs) - 4 - filler.rooms], refs[len(refs) - 4 - filler.rooms :]
@@ -794,12 +795,13 @@
         load.start()
     enter(place, "".join(a for a in "cxyz" if a in pieces[0][2]))
     steps = filler.start(given, made, own)
-    slots = sum(1 for time, _ in works if time >= 0)
+    slots = [number for number, (time, _) in enumerate(works) if time >= 0]
+    slots = slots[:: -(-len(slots) // filler.turns)]
     done = 0
-    for number, (time, act) in enumerate(works):
+    for number, (_, act) in enumerate(works):
         act()
-        if time >= 0:
-            share = steps * (number + 1 - (len(works) - slots)) // slots
+        if number in slots:
+            share = steps * (slots.index(number) + 1) // len(slots)
             filler.run(given, made, own, done, share)
             done = share
     for p in range(len(pieces)):
@@ -811,6 +813,7 @@
 
 class Nothing:
     operands = results = rooms = 0
+    turns = 12
     shapes, scratch = [], []
 
     def start(self, given, made, own):
@@ -823,11 +826,7 @@
         pass
 
 
-class After(Nothing):
-    operands = 1
-
-
-class WeightGrads:
+class WeightGrads(Nothing):
     operands, results, rooms = 4, 2, 6
     TILE, CHUNK = 256, 512
 
@@ -926,13 +925,97 @@
             self.put(made, own, jnp.int32(tile), tile % 2, False)
 
 
-def scatter(array, whose, pieces, collective_id, name, filler=Nothing(), operands=()):
+class LowGrads(Nothing):
+    operands, results, rooms = 4, 2, 6
+    TILE, turns = 256, 6
+
+    def __init__(self, rows, left, widths):
+        self.rows, self.widths = rows, widths
+        self.tiles = [n // self.TILE for n in left]
+        low = jnp.bfloat16
+        self.shapes = [jax.ShapeDtypeStruct((n, w), low) for n, w in zip(left, widths)]
+        self.scratch = [
+            pltpu.VMEM((2, rows, self.TILE), low),
+            pltpu.VMEM((rows, widths[0]), low),
+            pltpu.VMEM((rows, widths[1]), low),
+            pltpu.VMEM((2, self.TILE, max(widths)), low),
+            pltpu.SemaphoreType.DMA((4,)),
+            pltpu.SemaphoreType.DMA((2,)),
+        ]
+
+    def left(self, given, own, tile, second):
+        at = pl.ds(pl.multiple_of(tile * self.TILE, self.TILE), self.TILE)
+        slot = tile % 2
+        return pltpu.make_async_copy(
+            given[2 * second].at[:, at], own[0].at[slot], own[4].at[slot]
+        )
+
+    def put(self, made, own, tile, second):
+        rows = pl.ds(pl.multiple_of(tile * self.TILE, self.TILE), self.TILE)
+        slot = tile % 2
+        return pltpu.make_async_copy(
+            own[3].at[slot, :, pl.ds(0, self.widths[second])],
+            made[second].at[rows],
+            own[5].at[slot],
+        )
+
+    def start(self, given, made, own):
+        for second in (0, 1):
+            pltpu.make_async_copy(given[2 * second + 1], own[1 + second], own[4].at[2 + second]).start()
+        self.left(given, own, jnp.int32(0), 0).start()
+        return sum(self.tiles)
+
+    def run(self, given, made, own, first, last):
+        for second in (0, 1):
+            base = self.tiles[0] if second else 0
+            begin, end = max(first, base), min(last, base + self.tiles[second])
+            if begin >= end:
+                continue
+            if begin == base:
+                pltpu.make_async_copy(
+                    given[2 * second + 1], own[1 + second], own[4].at[2 + second]
+                ).wait()
+                if second:
+                    self.left(given, own, jnp.int32(0), second).start()
+
+            @pl.loop(begin - base, end - base)
+            def _(tile, second=second):
+                slot = tile % 2
+
+                @pl.when(tile + 1 < self.tiles[second])
+                def _():
+                    self.left(given, own, tile + 1, second).start()
+
+                self.left(given, own, tile, second).wait()
+
+                @pl.when(tile >= 2)
+                def _():
+                    self.put(made, own, tile - 2, second).wait()
+
+                half = self.widths[second] // 2
+                for part in (0, 1):
+                    cols = slice(part * half, (part + 1) * half)
+                    own[3][slot, :, cols] = lax.dot_general(
+                        own[0][slot],
+                        own[1 + second][:, cols],
+                        DOWNWARD,
+                        preferred_element_type=jnp.float32,
+                    ).astype(jnp.bfloat16)
+                self.put(made, own, tile, second).start()
+
+            if end == base + self.tiles[second]:
+                for tile in (self.tiles[second] - 2, self.tiles[second] - 1):
+                    self.put(made, own, jnp.int32(tile), second).wait()
+
+
+def scatter(array, whose, pieces, collective_id, name, filler=Nothing(), operands=(), columns=None):
     size = {"all": 32, "dp": 8, "expert": 4}[whose]
-    rows, width = array.shape[0] // size, array.shape[1]
+    columns = columns or (0, array.shape[1])
+    rows, width = array.shape[0] // size, columns[1]
     order, count = pieces[0][2], len(pieces)
     hbm = pl.BlockSpec(memory_space=pltpu.HBM)
     out = pl.pallas_call(
-        functools.partial(scatter_kernel, whose, rows, pieces, filler),
+        functools.partial(scatter_kernel, whose, rows, pieces, columns, filler),
         out_shape=[jax.ShapeDtypeStruct((rows, width), jnp.float32)] + filler.shapes,
         in_specs=[hbm] * (1 + len(operands)),
         out_specs=[pl.BlockSpec(memory_space=pltpu.VMEM)] + [hbm] * filler.results,
@@ -948,7 +1031,7 @@
     return out if filler.results else out[0]
 
 
-def sum_weights_kernel(rows, pieces, in_grad, out_grad, after, query, keyvalue, output, *refs):
+def sum_weights_kernel(rows, pieces, in_grad, out_grad, query, keyvalue, output, *refs):
     count = len(scatter_rooms(rows, 128, pieces[0][2]))
     in_rooms, out_rooms = refs[:count], refs[count : 2 * count]
     dealt, shared, out_dealt = refs[2 * count : 2 * count + 3]
@@ -1034,7 +1117,7 @@
     post.close()
 
 
-def sum_weights(in_grad, out_grad, after, pieces, collective_id):
+def sum_weights(in_grad, out_grad, pieces, collective_id):
     rows, wide = out_grad.shape[0] // 8, out_grad.shape[1]
     order, count = pieces[0][2], len(pieces)
     total = in_grad.shape[1]
@@ -1048,7 +1131,7 @@
             shape((rows, 2 * wide), jnp.float32),
             shape((rows, wide), jnp.float32),
         ],
-        in_specs=[hbm] * 3,
+        in_specs=[hbm] * 2,
         out_specs=[vmem] * 3,
         scratch_shapes=scatter_rooms(rows, total, order)
         + scatter_rooms(rows, wide, order)
@@ -1065,7 +1148,7 @@
             collective_id=collective_id, has_side_effects=True, vmem_limit_bytes=63 * 2**20
         ),
         name="sum_weights",
-    )(in_grad, out_grad, after)
+    )(in_grad, out_grad)
 
 
 def weights_kernel(jobs, *refs):
@@ -1259,105 +1342,117 @@
     )(prefix, projected, projected, projected, side)
 
 
-def attention_back_kernel(
-    experts, prefix, q, k, v, side, log_total, dmix, dprojected, dgate, bias, dk, dv
-):
-    rows, span = q.shape[0], k.shape[1]
-    length = k.shape[0]
-    heads = span // HEAD_DIM
-    block = pl.program_id(0)
-    scaling = HEAD_DIM**-0.5
-    chosen = [side[:, 0:1], side[:, 1:2]]
-    gates = [side[:, 2:3], side[:, 3:4]]
-    row_at = pl.ds(pl.multiple_of(block * rows, rows), rows)
-    column = lax.broadcasted_iota(jnp.int32, (rows, 128), 1)
-
-    @pl.when(block == 0)
-    def _():
-        dk[...] = jnp.zeros_like(dk)
-        dv[...] = jnp.zeros_like(dv)
-
-    dgate[...] = jnp.zeros_like(dgate)
-
-    def body(width):
-        attention_bias(bias, block, rows, width, prefix[0])
-
-        @pl.loop(0, heads)
-        def _(head):
-            lane = head * HEAD_DIM
-            lanes = pl.ds(pl.multiple_of(lane, HEAD_DIM), HEAD_DIM)
-            keys, values = k[:width, lanes], v[:width, lanes]
-            dqueries = []
-            for j in range(2):
-                query = pick_expert(q, lane, experts, span, chosen[j])
-                dm = pick_expert(dmix, lane, experts, span, chosen[j])
-                at = pl.ds(pl.multiple_of((2 * head + j) * HEAD_DIM, HEAD_DIM), HEAD_DIM)
-                logs = jnp.tile(log_total[:, at], (1, width // HEAD_DIM))
-                scores = lax.dot_general(query, keys, ACROSS, preferred_element_type=jnp.float32)
-                probs = jnp.exp(scores * scaling + bias[:, :width] - logs)
-                dprobs = lax.dot_general(dm, values, ACROSS, preferred_element_type=jnp.float32)
-                inner = jnp.sum(probs * dprobs, axis=1, keepdims=True)
-                dgate[...] += jnp.where(column == j, inner, 0.0)
-                probs = probs * gates[j]
-                dscores = (probs * (dprobs - inner)).astype(jnp.bfloat16)
-                low = probs.astype(jnp.bfloat16)
-                dquery = jnp.dot(dscores, keys, preferred_element_type=jnp.float32) * scaling
-                dqueries.append(dquery)
-                dk[:width, lanes] += lax.dot_general(
-                    dscores, query, DOWNWARD, preferred_element_type=jnp.float32
-                )
-                dv[:width, lanes] += lax.dot_general(
-                    low, dm, DOWNWARD, preferred_element_type=jnp.float32
-                )
-            for e in range(experts):
-                cols = jnp.where(chosen[0] == e, dqueries[0], 0.0) + jnp.where(
-                    chosen[1] == e, dqueries[1], 0.0
-                )
-                at = pl.ds(pl.multiple_of(e * span + lane, HEAD_DIM), HEAD_DIM)
-                dprojected[row_at, at] = cols.astype(jnp.bfloat16)
-
-    for_each_limit(length // rows, rows, body)
-
-    @pl.when(block == pl.num_programs(0) - 1)
-    def _():
-        dprojected[:, experts * span : (experts + 1) * span] = (dk[...] * scaling).astype(
-            jnp.bfloat16
-        )
-        dprojected[:, (experts + 1) * span :] = dv[...].astype(jnp.bfloat16)
-
-
-def attention_back(projected, side, prefix, log_total, dmix, experts, rows):
-    length, total = projected.shape
-    span = total // (experts + 2)
-    wide = experts * span
-    return pl.pallas_call(
-        functools.partial(attention_back_kernel, experts),
-        grid=(length // rows,),
-        in_specs=[
-            pl.BlockSpec(memory_space=pltpu.SMEM),
-            pl.BlockSpec((rows, wide), lambda i: (i, 0)),
-            pl.BlockSpec((length, span), lambda i: (0, experts)),
-            pl.BlockSpec((length, span), lambda i: (0, experts + 1)),
-            pl.BlockSpec((rows, 128), lambda i: (i, 0)),
-            pl.BlockSpec((rows, 2 * span), lambda i: (i, 0)),
-            pl.BlockSpec((rows, wide), lambda i: (i, 0)),
-        ],
-        out_specs=[
-            pl.BlockSpec((length, total), lambda i: (0, 0)),
-            pl.BlockSpec((rows, 128), lambda i: (i, 0)),
-        ],
-        out_shape=[
-            jax.ShapeDtypeStruct((length, total), jnp.bfloat16),
-            jax.ShapeDtypeStruct((length, 128), jnp.float32),
-        ],
-        scratch_shapes=[
-            pltpu.VMEM((rows, length), jnp.float32),
-            pltpu.VMEM((length, span), jnp.float32),
-            pltpu.VMEM((length, span), jnp.float32),
-        ],
-        compiler_params=pltpu.CompilerParams(vmem_limit_bytes=56 * 2**20),
-        name="attention_back",
-    )(prefix, projected, projected, projected, side, log_total, dmix)
+class AttentionBack(Nothing):
+    operands, results, rooms = 4, 2, 11
+    turns = 4
+
+    def __init__(self, length, total, experts, rows):
+        self.length, self.experts, self.rows = length, experts, rows
+        self.span = total // (experts + 2)
+        low, f32 = jnp.bfloat16, jnp.float32
+        self.heads = self.span // HEAD_DIM
+        self.blocks = length // rows
+        self.shapes = [
+            jax.ShapeDtypeStruct((length, total), low),
+            jax.ShapeDtypeStruct((length, 128), f32),
+        ]
+        self.scratch = [
+            pltpu.VMEM((length, total), low),
+            pltpu.VMEM((length, 128), f32),
+            pltpu.VMEM((length, 2 * self.span), f32),
+            pltpu.VMEM((length, experts * self.span), low),
+            pltpu.VMEM((length, total), low),
+            pltpu.VMEM((length, 128), f32),
+            pltpu.VMEM((rows, length), f32),
+            pltpu.VMEM((length, self.span), f32),
+            pltpu.VMEM((length, self.span), f32),
+            pltpu.SemaphoreType.DMA((4,)),
+            pltpu.SemaphoreType.DMA((2,)),
+        ]
+
+    def loads(self, given, own):
+        return [pltpu.make_async_copy(given[i], own[i], own[9].at[i]) for i in range(4)]
+
+    def start(self, given, made, own):
+        for load in self.loads(given, own):
+            load.start()
+        for ref in (own[5], own[7], own[8]):
+            ref[...] = jnp.zeros_like(ref)
+        return self.blocks * self.heads
+
+    def run(self, given, made, own, first, last):
+        if first == 0:
+            for load in self.loads(given, own):
+                load.wait()
+
+        @pl.loop(first, last)
+        def _(step):
+            block = step // self.heads
+            limits = key_limits(self.blocks, self.rows)
+            for width in sorted(set(limits)):
+                members = [i for i, limit in enumerate(limits) if limit == width]
+
+                @pl.when((block >= members[0]) & (block <= members[-1]))
+                def _(width=width):
+                    self.step(own, block, step % self.heads, width)
+
+    def step(self, own, block, head, width):
+        qkv, side_ref, log_total, dmix, dprojected, dgate, bias, dk, dv = own[:9]
+        experts, span, rows = self.experts, self.span, self.rows
+        scaling = HEAD_DIM**-0.5
+        row_at = pl.ds(pl.multiple_of(block * rows, rows), rows)
+        side = side_ref[row_at, :]
+        chosen = [side[:, 0:1], side[:, 1:2]]
+        gates = [side[:, 2:3], side[:, 3:4]]
+        column = lax.broadcasted_iota(jnp.int32, (rows, 128), 1)
+        query_at = block * rows + lax.broadcasted_iota(jnp.int32, (rows, width), 0)
+        key_at = lax.broadcasted_iota(jnp.int32, (rows, width), 1)
+        reach = key_at.astype(jnp.float32) < side[:, 4:5]
+        bias[:, :width] = jnp.where((key_at <= query_at) | reach, 0.0, NEG)
+        lane = head * HEAD_DIM
+        lanes = lambda base: pl.ds(pl.multiple_of(base + lane, HEAD_DIM), HEAD_DIM)
+        keys = qkv[:width, lanes(experts * span)]
+        values = qkv[:width, lanes((experts + 1) * span)]
+        dqueries = []
+        for j in range(2):
+            query = pick_expert(qkv.at[row_at], lane, experts, span, chosen[j])
+            dm = pick_expert(dmix.at[row_at], lane, experts, span, chosen[j])
+            at = pl.ds(pl.multiple_of((2 * head + j) * HEAD_DIM, HEAD_DIM), HEAD_DIM)
+            logs = jnp.tile(log_total[row_at, at], (1, width // HEAD_DIM))
+            scores = lax.dot_general(query, keys, ACROSS, preferred_element_type=jnp.float32)
+            probs = jnp.exp(scores * scaling + bias[:, :width] - logs)
+            dprobs = lax.dot_general(dm, values, ACROSS, preferred_element_type=jnp.float32)
+            inner = jnp.sum(probs * dprobs, axis=1, keepdims=True)
+            dgate[row_at, :] += jnp.where(column == j, inner, 0.0)
+            probs = probs * gates[j]
+            dscores = (probs * (dprobs - inner)).astype(jnp.bfloat16)
+            low = probs.astype(jnp.bfloat16)
+            dqueries.append(jnp.dot(dscores, keys, preferred_element_type=jnp.float32) * scaling)
+            dk[:width, lanes(0)] += lax.dot_general(
+                dscores, query, DOWNWARD, preferred_element_type=jnp.float32
+            )
+            dv[:width, lanes(0)] += lax.dot_general(
+                low, dm, DOWNWARD, preferred_element_type=jnp.float32
+            )
+        for e in range(experts):
+            cols = jnp.where(chosen[0] == e, dqueries[0], 0.0) + jnp.where(
+                chosen[1] == e, dqueries[1], 0.0
+            )
+            dprojected[row_at, lanes(e * span)] = cols.astype(jnp.bfloat16)
+
+    def end(self, given, made, own):
+        dprojected, dgate, dk, dv = own[4], own[5], own[7], own[8]
+        wide = self.experts * self.span
+        dprojected[:, wide : wide + self.span] = (dk[...] * HEAD_DIM**-0.5).astype(jnp.bfloat16)
+        dprojected[:, wide + self.span :] = dv[...].astype(jnp.bfloat16)
+        copies = [
+            pltpu.make_async_copy(dprojected, made[0], own[10].at[0]),
+            pltpu.make_async_copy(dgate, made[1], own[10].at[1]),
+        ]
+        for copy in copies:
+            copy.start()
+        for copy in copies:
+            copy.wait()
 
 
 def expert_slots(ids, my_index, tok_rows):
@@ -1779,7 +1874,8 @@
     attend_matches_all = expert_matches(attention_routes[0], group_size)
     attend_logits = jnp.dot(sequence_in, attention_cols, preferred_element_type=f32)
     attend_weights_all, _ = pair_gates(attend_logits, attend_matches_all)
-    side = jnp.concatenate([attention_routes[0].astype(f32), attend_weights_all], axis=1)
+    reach = jnp.broadcast_to(prefix_length.astype(f32)[None], (attend_logits.shape[0], 1))
+    side = jnp.concatenate([attention_routes[0].astype(f32), attend_weights_all, reach], axis=1)
     side = jnp.pad(side, ((0, 0), (0, 128 - side.shape[1])))
     mixed, log_total = attention(projected, side, prefix_length, group_size, tok_rows)
     attend_part = jnp.dot(mixed, out_weight, preferred_element_type=f32).astype(low)
@@ -1828,14 +1924,6 @@
     grad_gate = grad_in_feed[:hidden_rows]
     grad_up = grad_in_feed[padded : padded + hidden_rows]
     grad_down = grad_down[:hidden_rows]
-    out_part, feed_home = lax.optimization_barrier((out_part, feed_home))
-    feed_sum = lax.psum_scatter(
-        out_part,
-        ("dp", "expert"),
-        scatter_dimension=0,
-        tiled=True,
-    )
-    layer_output = hidden + feed_sum.astype(f32)
     gradient = cotangent[0].astype(f32)
     feed_dlogits = gates_back(feed_dgate, feed_weights, feed_matches)
     feed_dnorm = feed_home + jnp.dot(feed_dlogits, feedforward_cols.astype(f32).T, precision=HIGH)
@@ -1846,13 +1934,31 @@
         [(hidden_grad.astype(low), "expert", quarters("xc"))], 5, "gather_cotangents"
     )
     dmix = lax.dot_general(sequence_grad, out_weight, ACROSS, preferred_element_type=f32).astype(low)
-    grad_out = lax.dot_general(mixed, sequence_grad, DOWNWARD, preferred_element_type=f32)
-    dprojected, gate_parts = attention_back(
-        projected, side, prefix_length, log_total, dmix, group_size, tok_rows
+    length, total = projected.shape
+    columns = model_width // 2
+    first_sum, dprojected, gate_parts = scatter(
+        out_part,
+        "all",
+        everywhere("cxyz", "cyxz"),
+        7,
+        "sum_output_left",
+        AttentionBack(length, total, group_size, tok_rows),
+        (projected, side, log_total, dmix),
+        (0, columns),
     )
     attend_dx = lax.dot_general(dprojected, in_weight, ACROSS, preferred_element_type=f32)
-    grad_in = lax.dot_general(sequence_in, dprojected, DOWNWARD, preferred_element_type=f32)
     attend_home = scatter(attend_dx.astype(low), "expert", quarters("cx"), 2, "sum_attention")
+    second_sum, grad_in, grad_out = scatter(
+        out_part,
+        "all",
+        everywhere("cxyz", "cyxz"),
+        8,
+        "sum_output_right",
+        LowGrads(length, (model_width, query_width), (total, model_width)),
+        (sequence_in, dprojected, mixed, sequence_grad),
+        (columns, model_width - columns),
+    )
+    layer_output = hidden + jnp.concatenate([first_sum, second_sum], axis=1)
     pair_dgate = lax.psum_scatter(
         gate_parts[:, :2].reshape(group_size, tok_rows, 2).transpose(0, 2, 1).reshape(-1, tok_rows),
         "expert",
@@ -1883,7 +1989,7 @@
     small = lax.dynamic_slice_in_dim(small, lax.axis_index("dp") * rows_in, rows_in, 1)
 
     grad_query, grad_keyvalue, grad_projection = sum_weights(
-        grad_in.astype(low), grad_out.astype(low), feed_sum, ((0, rows_in, "yz"),), 6
+        grad_in, grad_out, ((0, rows_in, "yz"),), 6
     )
     return (
         layer_output.astype(low)[None],

time: 1870 us -> 1530 us (0.82)
  waiting for transfers between devices: 445 us -> 0.06 us
  Pallas kernels: 1210 us -> 1350 us
  matrix products: 108 us -> 77.3 us
    reduce_scatter x1 -> x0, waiting for transfers between devices: 357 us -> none  [per_device_torus(): lax.psum_scatter(out_part, ('dp', 'expert'), scatter_dimension=0, tiled=T...]
    pallas_call x4 -> x5, Pallas kernels: 259 us -> 398 us  [scatter(): pl.pallas_call(functools.partial(scatter_kernel, whose, rows, pieces, col...]
    psum x1, waiting for transfers between devices: 87.7 us -> 0.02 us  [per_device_torus(): small = lax.psum(small.astype(f32), ('dp', 'expert'))]
    dot_general x2 -> x0, matrix products: 30.1 us -> none  [the longest x1 18.4 us: per_device_torus(): lax.dot_general(sequence_in, dprojected, DOWNWARD, preferred_element_type...]
  transfers between devices with their start and end apart: 3 -> 2, of which waited for: 2 -> 0; matrix products, arithmetic and copies ran while one was open for 3% -> 1% of each run, Pallas kernels for 9% -> 29%
where the time goes in v5:
time: 1530 us; the launch traced here: 1520 us
  Pallas kernels  1350 us (88%)
  matrix products  77.3 us (5%)
  local copies, waits for them, and re-layouts  43.2 us (3%)
  other arithmetic  23.5 us (2%)
  between operations  16.1 us (1%)
    pallas_call x5, Pallas kernels, scatter(): pl.pallas_call(functools.partial(scatter_kernel, whose, rows, pieces, col...  398 us
    pallas_call x1, Pallas kernels, gather_weights(): pl.pallas_call(functools.partial(weights_kernel, plan), out_shape=shards...  343 us
    pallas_call x1, Pallas kernels, sum_weights(): pl.pallas_call(functools.partial(sum_weights_kernel, rows, pieces), out_s...  286 us
    pallas_call x1, Pallas kernels, feed(): pl.pallas_call(functools.partial(feed_kernel, tok, slot_count), in_specs=...  253 us
    pallas_call x1, Pallas kernels, gather(): pl.pallas_call(functools.partial(gather_kernel, plan, axes), out_shape=[j...  38.5 us
  transfers between devices with their start and end apart: 2, of which 0 were waited for; matrix products, arithmetic and copies ran while one was open for 1% of the time, Pallas kernels for 29%

profile of v5, /device:TPU:2, one launch (start us, length us, event | category | flops | bytes accessed | tf_op | source)
XLA Modules:
  0.0 1521.7 jit_solution(9820455685501430166)
XLA Ops:
  13.9 342.7 %gather_weights.1 = (bf16[256,3072]{1,0:T(8,128)(2,1)}, bf16[256,2048]{1,0:T(8,128)(2,1)}, bf16[1024,2048]{1,0:T(8,128)(2,1)}, bf16[8192,2048]{1,0:T(8,128)(2,1)...) custom-call(bf16[256,2048]{1,0:T(8,128)(2,1)} %fusion.4.refs_0_, ...), custom_call_target="tpu_custom_call" | custom-call | tf_op jit(solution)/shard_map/gather_weights/pallas_call | solution.py:1232
  357.5 3.4 fusion.19
  362.4 18.6 %convolution_convert_fusion.q.k.v.refs_0_ = bf16[1024,3072]{1,0:T(8,128)(2,1)} fusion(bf16[1024,2048]{1,0:T(8,128)(2,1)} %get-tuple-element.38.refs_0_, bf16[2048,3072]{1,0:T(8,128)(2,1)} %get-tuple-element.39), kind=kOutput, calls=%fused_computation.3 | convolution fusion | flops 12888047616 | bytes 23068672 | tf_op jit(solution)/shard_map/dot_general | solution.py:1873
  382.1 29.7 %attention.1 = (bf16[1024,2048]{1,0:T(8,128)(2,1)S(1)}, f32[1024,1024]{1,0:T(8,128)}) custom-call(s32[1]{0:T(128)S(6)} %copy.75.prefix, bf16[1024,3072]{1,0:T(8,128)(2,1)} %convolution_convert_fusion.q.k.v.refs_0_, bf16[1024,3072]{1,0:T(8,128)(2,1)} %convolution_convert_fusion.q.k.v.refs_0_, bf16[1024,3072]{1,0:T(8,128)(2,1)} %convolution_convert_fusion.q.k.v.refs_0_, ...), custom_call_target="tpu_custom_call" | custom-call | tf_op jit(solution)/shard_map/attention/pallas_call | solution.py:1321
  413.8 10.3 convolution_convert_fusion.3.source
  424.1 29.6 %sum_attention.2 = f32[256,2048]{1,0:T(8,128)} custom-call(bf16[1024,2048]{1,0:T(8,128)(2,1)} %convolution_convert_fusion.3.source), custom_call_target="tpu_custom_call" | custom-call | tf_op jit(solution)/shard_map/sum_attention/pallas_call | solution.py:1017
  456.0 6.1 reshape.156
  465.0 3.3 reduce_sum.158
  471.7 253.1 %feed_forward.1 = (bf16[8192,2048]{1,0:T(8,128)(2,1)}, bf16[8192,2048]{1,0:T(8,128)(2,1)}, bf16[8192,2048]{1,0:T(8,128)(2,1)}, bf16[5120,2048]{1,0:T(8,128)(2,1)...) custom-call(bf16[256,2048]{1,0:T(8,128)(2,1)} %multiply_convert_fusio, ...), custom_call_target="tpu_custom_call" | custom-call | tf_op jit(solution)/shard_map/feed_forward/pallas_call | solution.py:1772
  727.6 159.5 %sum_rows.1 = (f32[256,2048]{1,0:T(8,128)}, f32[1536,2048]{1,0:T(8,128)}, f32[768,2048]{1,0:T(8,128)}) custom-call(bf16[8192,2048]{1,0:T(8,128)(2,1)} %get-tuple-element.47.source, bf16[5120,1536]{1,0:T(8,128)(2,1)} %get-tuple-element.48.refs_0_, bf16[5120,2048]{1,0:T(8,128)(2,1)} %get-tuple-element.49.refs_1_, bf16[5120,768]{1,0:T(8,128)(2,1)} %get-tuple-element.50.refs_2_, ...), custom_call_target="tpu_custom_call" | custom-call | tf_op jit(solution)/shard_map/sum_rows/pallas_call | solution.py:1017
  887.2 10.8 slice_bitcast_fusion.1
  898.0 3.2 slice_bitcast_fusion
  903.9 3.3 multiply_reduce_fusion
  910.2 38.5 %gather_cotangents.1.refs_3_ = bf16[1024,2048]{1,0:T(8,128)(2,1)} custom-call(bf16[256,2048]{1,0:T(8,128)(2,1)} %fusion.28.refs_0_), custom_call_target="tpu_custom_call" | custom-call | tf_op jit(solution)/shard_map/gather_cotangents/pallas_call | solution.py:610
  948.7 14.0 convolution_convert_fusion.2.refs_3_
  962.7 95.2 %sum_output_left.1 = (f32[256,1024]{1,0:T(8,128)}, bf16[1024,3072]{1,0:T(8,128)(2,1)}, f32[1024,128]{1,0:T(8,128)}) custom-call(bf16[8192,2048]{1,0:T(8,128)(2,1)} %get-tuple-element.45.source, bf16[1024,3072]{1,0:T(8,128)(2,1)} %convolution_convert_fusion.q.k.v.refs_0_, f32[1024,128]{1,0:T(8,128)} %copy-done, f32[1024,1024]{1,0:T(8,128)} %get-tuple-element.46.refs_2_, ...), custom_call_target="tpu_custom_call" | custom-call | tf_op jit(solution)/shard_map/sum_output_left/pallas_call | solution.py:1017
  1057.9 84.6 %sum_output_right.1 = (f32[256,1024]{1,0:T(8,128)}, bf16[2048,3072]{1,0:T(8,128)(2,1)}, bf16[2048,2048]{1,0:T(8,128)(2,1)}) custom-call(bf16[8192,2048]{1,0:T(8,128)(2,1)} %get-tuple-element.45.source, bf16[1024,2048]{1,0:T(8,128)(2,1)} %get-tuple-element.38.refs_0_, bf16[1024,3072]{1,0:T(8,128)(2,1)} %get-tuple-element.55.refs_1_, ...), custom_call_target="tpu_custom_call" | custom-call | tf_op jit(solution)/shard_map/sum_output_right/pallas_call | solution.py:1017
  1142.5 19.4 %convolution_convert_fusion.1.source = bf16[1024,2048]{1,0:T(8,128)(2,1)} fusion(bf16[1024,3072]{1,0:T(8,128)(2,1)} %get-tuple-element.55.refs_1_, bf16[2048,3072]{1,0:T(8,128)(2,1)} %get-tuple-element.39), kind=kOutput, calls=%fused_computation.5 | convolution fusion | flops 12886999040 | bytes 23068672 | tf_op jit(solution)/shard_map/dot_general | solution.py:1949
  1162.3 13.3 all-reduce.3
  1176.0 29.5 %sum_attention.3 = f32[256,2048]{1,0:T(8,128)} custom-call(bf16[1024,2048]{1,0:T(8,128)(2,1)} %convolution_convert_fusion.1.source), custom_call_target="tpu_custom_call" | custom-call | tf_op jit(solution)/shard_map/sum_attention/pallas_call | solution.py:1017
  1207.3 4.9 fusion.10
  1212.9 4.8 fusion.9
  1217.7 285.8 %sum_weights.1 = (f32[256,2048]{1,0:T(8,128)}, f32[256,4096]{1,0:T(8,128)}, f32[256,2048]{1,0:T(8,128)}) custom-call(bf16[2048,3072]{1,0:T(8,128)(2,1)} %get-tuple-element.58.in_grad, bf16[2048,2048]{1,0:T(8,128)(2,1)} %get-tuple-element.59.out_grad), custom_call_target="tpu_custom_call" | custom-call | tf_op jit(solution)/shard_map/sum_weights/pallas_call | solution.py:1127
  1506.2 4.8 copy.76
  (121 shorter events, 37.2 us)
Async XLA Ops:
  7.2 4.8 copy-start.5
  7.2 895.4 %all-reduce.9.cloned.1.call-start = ((), (), s32[]{:S(2)}) async-start(), calls=%async_computation.1 | async-start | bytes 262144
  8.8 347.8 %copy-start.20 = (f32[256]{0:T(256)}, f32[256]{0:T(256)S(1)}, u32[]{:S(2)}) copy-start(f32[256]{0:T(256)S(1)} %add_rsqrt_fusion.1) | copy-start | bytes 3076
  357.5 3.4 copy-start.22
  381.2 32.5 %slice-start = ((s8[8388608]{0:T(1024)(128)(4,1)}), s8[4194304]{0:T(1024)(128)(4,1)S(1)}, s32[]{:S(2)}) async-start(s8[8388608]{0:T(1024)(128)(4,1)} %bitcast.101), calls=%async_computation.2 | async-start | bytes 8388608
  382.1 29.7 %copy-start = (f32[1024,128]{1,0:T(8,128)}, f32[1024,128]{1,0:T(8,128)S(1)}, u32[]{:S(2)}) copy-start(f32[1024,128]{1,0:T(8,128)S(1)} %pad.8.side.refs_1_) | copy-start | bytes 1572868
  382.1 31.7 %slice-start.1 = ((s8[8388608]{0:T(1024)(128)(4,1)}), s8[4194304]{0:T(1024)(128)(4,1)S(1)}, s32[]{:S(2)}) async-start(s8[8388608]{0:T(1024)(128)(4,1)} %bitcast.101), calls=%async_computation.3 | async-start | bytes 8388608
  456.0 14.5 copy-start.2
  465.0 5.5 copy-start.17
  471.7 254.9 %copy-start.8 = (bf16[256,2048]{1,0:T(8,128)(2,1)S(1)}, bf16[256,2048]{1,0:T(8,128)(2,1)}, u32[]{:S(2)}) copy-start(bf16[256,2048]{1,0:T(8,128)(2,1)} %multiply_convert_fusion.own_rows) | copy-start | bytes 3145732
  471.7 255.3 %copy-start.23 = (u32[32]{0:T(128)S(1)}, u32[32]{0:T(128)}, u32[]{:S(2)}) copy-start(u32[32]{0:T(128)} %constant.63) | copy-start | bytes 388
  726.5 777.0 %all-reduce.7.cloned.1.call-start = ((), (), s32[]{:S(2)}) async-start(), calls=%async_computation | async-start | bytes 262144 | tf_op jit(solution)/shard_map/psum | solution.py:1988
  887.1 10.8 copy-start.11
  898.0 5.4 copy-start.9
  898.0 5.9 copy-start.3
  903.9 4.6 copy-start.10
  1142.5 19.4 %copy-start.16 = (f32[1024,128]{1,0:T(8,128)S(1)}, f32[1024,128]{1,0:T(8,128)}, u32[]{:S(2)}) copy-start(f32[1024,128]{1,0:T(8,128)} %get-tuple-element.57) | copy-start | bytes 1572868
  1142.5 33.0 %copy-start.13 = (f32[1024,2]{1,0:T(8,128)S(1)}, f32[1024,2]{1,0:T(8,128)}, u32[]{:S(2)}) copy-start(f32[1024,2]{1,0:T(8,128)} %copy-done.12) | copy-start | bytes 24580
  1176.0 31.3 %copy-start.18 = (f32[2048]{0:T(1024)S(1)}, f32[2048]{0:T(1024)}, u32[]{:S(2)}) copy-start(f32[2048]{0:T(1024)} %param.19) | copy-start | bytes 24580
  1176.0 31.3 %copy-start.21 = (f32[256]{0:T(256)S(1)}, f32[256]{0:T(256)}, u32[]{:S(2)}) copy-start(f32[256]{0:T(256)} %copy-done.20) | copy-start | bytes 3076
  1207.2 5.7 copy-start.4
  1207.2 5.7 copy-start.6
  1506.2 4.8 copy-start.15
  1511.0 2.3 copy-start.14
  (4 other events, 6.4 us)
Sparse Core Ops, SparseCore 0:
  726.6 124.5 all-reduce.8
  1213.0 126.2 all-reduce.6

commit v6 on v5

--- a/solution.py
+++ b/solution.py
@@ -827,16 +827,15 @@
 
 
 class WeightGrads(Nothing):
-    operands, results, rooms = 4, 2, 6
+    operands, results, rooms = 4, 3, 6
     TILE, CHUNK = 256, 512
 
-    def __init__(self, rows, wide, narrow, width):
+    def __init__(self, rows, padded, hidden, width):
         self.chunks = rows // self.CHUNK
-        self.tiles = (wide // self.TILE, narrow // self.TILE)
-        self.shapes = [
-            jax.ShapeDtypeStruct((wide, width), jnp.float32),
-            jax.ShapeDtypeStruct((narrow, width), jnp.float32),
-        ]
+        self.each = padded // self.TILE
+        self.short = hidden - (self.each - 1) * self.TILE
+        self.tiles = (2 * self.each, self.each)
+        self.shapes = [jax.ShapeDtypeStruct((hidden, width), jnp.float32)] * 3
         self.scratch = [
             pltpu.VMEM((2, self.CHUNK, self.TILE), jnp.bfloat16),
             pltpu.VMEM((2, self.CHUNK, width), jnp.bfloat16),
@@ -867,16 +866,20 @@
                     copy.start() if start else copy.wait()
 
     def put(self, made, own, tile, parity, start):
-        for second in (0, 1):
-
-            @pl.when((tile >= self.tiles[0]) if second else (tile < self.tiles[0]))
-            def _(second=second):
-                at = tile - (self.tiles[0] if second else 0)
-                rows = pl.ds(pl.multiple_of(at * self.TILE, self.TILE), self.TILE)
-                copy = pltpu.make_async_copy(
-                    own[2 + parity], made[second].at[rows], own[5].at[parity]
-                )
-                copy.start() if start else copy.wait()
+        row = (tile % self.each) * self.TILE
+        for result in range(3):
+            for last in (0, 1):
+                length = self.short if last else self.TILE
+                at_end = (tile % self.each) == self.each - 1
+
+                @pl.when((tile // self.each == result) & (at_end if last else ~at_end))
+                def _(result=result, length=length):
+                    copy = pltpu.make_async_copy(
+                        own[2 + parity].at[pl.ds(0, length)],
+                        made[result].at[pl.ds(pl.multiple_of(row, self.TILE), length)],
+                        own[5].at[parity],
+                    )
+                    copy.start() if start else copy.wait()
 
     def start(self, given, made, own):
         self.fetch(given, own, jnp.int32(0), True)
@@ -925,87 +928,103 @@
             self.put(made, own, jnp.int32(tile), tile % 2, False)
 
 
-class LowGrads(Nothing):
-    operands, results, rooms = 4, 2, 6
-    TILE, turns = 256, 6
-
-    def __init__(self, rows, left, widths):
-        self.rows, self.widths = rows, widths
-        self.tiles = [n // self.TILE for n in left]
+class LowGrad(Nothing):
+    operands, results, rooms = 2, 1, 5
+    TILE, turns = 256, 4
+
+    def __init__(self, rows, left, width):
+        self.tiles, self.width = left // self.TILE, width
         low = jnp.bfloat16
-        self.shapes = [jax.ShapeDtypeStruct((n, w), low) for n, w in zip(left, widths)]
+        self.shapes = [jax.ShapeDtypeStruct((left, width), low)]
         self.scratch = [
             pltpu.VMEM((2, rows, self.TILE), low),
-            pltpu.VMEM((rows, widths[0]), low),
-            pltpu.VMEM((rows, widths[1]), low),
-            pltpu.VMEM((2, self.TILE, max(widths)), low),
-            pltpu.SemaphoreType.DMA((4,)),
+            pltpu.VMEM((rows, width), low),
+            pltpu.VMEM((2, self.TILE, width), low),
+            pltpu.SemaphoreType.DMA((3,)),
             pltpu.SemaphoreType.DMA((2,)),
         ]
 
-    def left(self, given, own, tile, second):
+    def left(self, given, own, tile):
         at = pl.ds(pl.multiple_of(tile * self.TILE, self.TILE), self.TILE)
-        slot = tile % 2
-        return pltpu.make_async_copy(
-            given[2 * second].at[:, at], own[0].at[slot], own[4].at[slot]
+        return pltpu.make_async_copy(given[0].at[:, at], own[0].at[tile % 2], own[3].at[tile % 2])
+
+    def right(self, given, own):
+        return pltpu.make_async_copy(given[1], own[1], own[3].at[2])
+
+    def put(self, made, own, tile):
+        rows = pl.ds(pl.multiple_of(tile * self.TILE, self.TILE), self.TILE)
+        return pltpu.make_async_copy(own[2].at[tile % 2], made[0].at[rows], own[4].at[tile % 2])
+
+    def start(self, given, made, own):
+        self.right(given, own).start()
+        self.left(given, own, jnp.int32(0)).start()
+        return self.tiles
+
+    def run(self, given, made, own, first, last):
+        if first == last:
+            return
+        if first == 0:
+            self.right(given, own).wait()
+
+        @pl.loop(first, last)
+        def _(tile):
+            slot = tile % 2
+
+            @pl.when(tile + 1 < self.tiles)
+            def _():
+                self.left(given, own, tile + 1).start()
+
+            self.left(given, own, tile).wait()
+
+            @pl.when(tile >= 2)
+            def _():
+                self.put(made, own, tile - 2).wait()
+
+            half = self.width // 2
+            for part in (0, 1):
+                cols = slice(part * half, (part + 1) * half)
+                own[2][slot, :, cols] = lax.dot_general(
+                    own[0][slot], own[1][:, cols], DOWNWARD, preferred_element_type=jnp.float32
+                ).astype(jnp.bfloat16)
+            self.put(made, own, tile).start()
+
+    def end(self, given, made, own):
+        for tile in (self.tiles - 2, self.tiles - 1):
+            self.put(made, own, jnp.int32(tile)).wait()
+
+
+class InTurn(Nothing):
+    def __init__(self, one, other):
+        self.parts = (one, other)
+        self.operands = one.operands + other.operands
+        self.results = one.results + other.results
+        self.rooms = one.rooms + other.rooms
+        self.turns = one.turns + other.turns
+        self.shapes, self.scratch = one.shapes + other.shapes, one.scratch + other.scratch
+
+    def split(self, given, made, own):
+        one = self.parts[0]
+        return (
+            (given[: one.operands], made[: one.results], own[: one.rooms]),
+            (given[one.operands :], made[one.results :], own[one.rooms :]),
         )
 
-    def put(self, made, own, tile, second):
-        rows = pl.ds(pl.multiple_of(tile * self.TILE, self.TILE), self.TILE)
-        slot = tile % 2
-        return pltpu.make_async_copy(
-            own[3].at[slot, :, pl.ds(0, self.widths[second])],
-            made[second].at[rows],
-            own[5].at[slot],
-        )
-
-    def start(self, given, made, own):
-        for second in (0, 1):
-            pltpu.make_async_copy(given[2 * second + 1], own[1 + second], own[4].at[2 + second]).start()
-        self.left(given, own, jnp.int32(0), 0).start()
-        return sum(self.tiles)
+    def start(self, *refs):
+        self.steps = [part.start(*own) for part, own in zip(self.parts, self.split(*refs))]
+        return self.parts[0].turns + self.parts[1].turns
 
     def run(self, given, made, own, first, last):
-        for second in (0, 1):
-            base = self.tiles[0] if second else 0
-            begin, end = max(first, base), min(last, base + self.tiles[second])
-            if begin >= end:
-                continue
-            if begin == base:
-                pltpu.make_async_copy(
-                    given[2 * second + 1], own[1 + second], own[4].at[2 + second]
-                ).wait()
-                if second:
-                    self.left(given, own, jnp.int32(0), second).start()
-
-            @pl.loop(begin - base, end - base)
-            def _(tile, second=second):
-                slot = tile % 2
-
-                @pl.when(tile + 1 < self.tiles[second])
-                def _():
-                    self.left(given, own, tile + 1, second).start()
-
-                self.left(given, own, tile, second).wait()
-
-                @pl.when(tile >= 2)
-                def _():
-                    self.put(made, own, tile - 2, second).wait()
-
-                half = self.widths[second] // 2
-                for part in (0, 1):
-                    cols = slice(part * half, (part + 1) * half)
-                    own[3][slot, :, cols] = lax.dot_general(
-                        own[0][slot],
-                        own[1 + second][:, cols],
-                        DOWNWARD,
-                        preferred_element_type=jnp.float32,
-                    ).astype(jnp.bfloat16)
-                self.put(made, own, tile, second).start()
-
-            if end == base + self.tiles[second]:
-                for tile in (self.tiles[second] - 2, self.tiles[second] - 1):
-                    self.put(made, own, jnp.int32(tile), second).wait()
+        edge = self.parts[0].turns
+        for n, (part, refs) in enumerate(zip(self.parts, self.split(given, made, own))):
+            low, high = (0, edge) if n == 0 else (edge, edge + part.turns)
+            begin, end = max(first, low) - low, min(last, high) - low
+            if begin < end:
+                steps = self.steps[n]
+                part.run(*refs, steps * begin // part.turns, steps * end // part.turns)
+
+    def end(self, *refs):
+        for part, own in zip(self.parts, self.split(*refs)):
+            part.end(*own)
 
 
 def scatter(array, whose, pieces, collective_id, name, filler=Nothing(), operands=(), columns=None):
@@ -1031,52 +1050,139 @@
     return out if filler.results else out[0]
 
 
-def sum_weights_kernel(rows, pieces, in_grad, out_grad, query, keyvalue, output, *refs):
+def sum_right_kernel(rows, pieces, columns, out_rows, out_pieces, filler, source, out_grad, *refs):
+    source = source.at[:, pl.ds(*columns)]
+    given, refs = refs[: filler.operands], refs[filler.operands :]
+    result, output, refs = refs[0], refs[1], refs[2:]
+    made, refs = refs[: filler.results], refs[filler.results :]
     count = len(scatter_rooms(rows, 128, pieces[0][2]))
-    in_rooms, out_rooms = refs[:count], refs[count : 2 * count]
-    dealt, shared, out_dealt = refs[2 * count : 2 * count + 3]
-    send_sems, deal_sems = refs[2 * count + 3 : 2 * count + 5]
-    in_sems, out_sems = refs[2 * count + 5 : 2 * count + 8], refs[2 * count + 8 :]
+    rooms, refs = refs[:count], refs[count:]
+    count = len(scatter_rooms(rows, 128, out_pieces[0][2]))
+    out_rooms, refs = refs[:count], refs[count:]
+    dealt, send_sems, deal_sems = refs[:3]
+    sems, out_sems, own = refs[3:6], refs[6:9], refs[9:]
     place = Place()
     post = Post(send_sems, place)
-    z, y, e = place.at["z"], place.at["y"], place.expert
+    z, e = place.at["z"], place.expert
+    partner, moves = (e * 2 + place.at["y"], z), z != e
+    loads, works, finish = scatter_plan(
+        "all", rows, pieces, place, post, source, rooms, sems
+    )
+    out_loads, out_works, out_finish = scatter_plan(
+        "dp", out_rows, out_pieces, place, post, out_grad, out_rooms, out_sems
+    )
+    for load in loads + out_loads:
+        load.start()
+    enter(place, "cxyz", [(partner, moves)])
+    steps = filler.start(given, made, own)
+    times = sorted({time for time, _ in works + out_works})
+    turns = [time for time in times if time >= 0]
+    done = 0
+    for time in times:
+        for plan in (out_works, works):
+            for at, act in plan:
+                if at == time:
+                    act()
+        if time >= 0:
+            share = steps * (turns.index(time) + 1) // len(turns)
+            filler.run(given, made, own, done, share)
+            done = share
+    for p in range(len(out_pieces)):
+        first, length, _ = out_pieces[p]
+        at = pl.ds(first, length)
+        post.send(out_finish(p), dealt.at[at], deal_sems.at[p], partner, moves)
+    for p in range(len(pieces)):
+        first, length, _ = pieces[p]
+        widen(result.at[pl.ds(first, length)], finish(p), length)
+    filler.end(given, made, own)
+    for p in range(len(out_pieces)):
+        first, length, _ = out_pieces[p]
+        at = pl.ds(first, length)
+
+        def came(p=p, at=at, length=length):
+            post.arrived(dealt.at[at], deal_sems.at[p])
+            widen(output.at[at], dealt.at[at], length)
+
+        pl.when(moves)(came)
+        pl.when(~moves)(
+            lambda at=at, length=length: widen(output.at[at], out_rooms[0].at[z, at], length)
+        )
+    post.close()
+
+
+def sum_right(array, columns, pieces, out_grad, out_pieces, collective_id, filler, operands):
+    rows, width = array.shape[0] // 32, columns[1]
+    out_rows, out_width = out_grad.shape[0] // 8, out_grad.shape[1]
+    order, out_order = pieces[0][2], out_pieces[0][2]
+    hbm = pl.BlockSpec(memory_space=pltpu.HBM)
+    vmem = pl.BlockSpec(memory_space=pltpu.VMEM)
+    shape = jax.ShapeDtypeStruct
+    sends = sends_of(order, len(pieces)) + sends_of(out_order, len(out_pieces)) + len(out_pieces)
+    return pl.pallas_call(
+        functools.partial(
+            sum_right_kernel, rows, pieces, columns, out_rows, out_pieces, filler
+        ),
+        out_shape=[
+            shape((rows, width), jnp.float32),
+            shape((out_rows, out_width), jnp.float32),
+        ]
+        + filler.shapes,
+        in_specs=[hbm] * (2 + len(operands)),
+        out_specs=[vmem] * 2 + [hbm] * filler.results,
+        scratch_shapes=scatter_rooms(rows, width, order)
+        + scatter_rooms(out_rows, out_width, out_order)
+        + [
+            pltpu.VMEM((out_rows, out_width), jnp.bfloat16),
+            pltpu.SemaphoreType.DMA((sends,)),
+            pltpu.SemaphoreType.DMA((len(out_pieces),)),
+        ]
+        + scatter_sems(order, len(pieces))
+        + scatter_sems(out_order, len(out_pieces))
+        + filler.scratch,
+        compiler_params=pltpu.CompilerParams(
+            collective_id=collective_id, has_side_effects=True, vmem_limit_bytes=63 * 2**20
+        ),
+        name="sum_output_right",
+    )(array, out_grad, *operands)
+
+
+def sum_weights_kernel(rows, pieces, in_grad, query, keyvalue, *refs):
+    count = len(scatter_rooms(rows, 128, pieces[0][2]))
+    rooms = refs[:count]
+    dealt, shared, send_sems, deal_sems = refs[count : count + 4]
+    place = Place()
+    post = Post(send_sems, place)
+    z, e = place.at["z"], place.expert
     wide = query.shape[1]
     span = (in_grad.shape[1] - wide) // 2
-    partner, moves = (e * 2 + y, z), z != e
     peers = []
     for flip_x, flip_c in ((1, 1), (1, 0), (0, 1)):
         x = place.at["x"] + flip_x * (1 - 2 * place.at["x"])
         core = place.at["c"] + flip_c * (1 - 2 * place.at["c"])
         peers.append((x * 2 + core, flip_x * 2 + flip_c))
-    in_loads, in_works, in_finish = scatter_plan(
-        "dp", rows, pieces, place, post, in_grad, in_rooms, in_sems
-    )
-    out_loads, out_works, out_finish = scatter_plan(
-        "dp", rows, pieces, place, post, out_grad, out_rooms, out_sems
-    )
-    for load in in_loads + out_loads:
+    loads, works, finish = scatter_plan(
+        "dp", rows, pieces, place, post, in_grad, rooms, refs[count + 4 :]
+    )
+    for load in loads:
         load.start()
-    enter(place, "cxyz", [((place.dp, peers[0][0]), None), (partner, moves)])
-    for (_, one), (_, other) in zip(in_works, out_works):
-        one()
-        other()
+    enter(place, "cxyz", [((place.dp, peers[0][0]), None)])
+    for _, act in works:
+        act()
     cols = lambda block: pl.ds(pl.multiple_of(block * span, span), span)
     keep = slice(wide, wide + 2 * span)
     for p in range(len(pieces)):
         first, length, _ = pieces[p]
         at = pl.ds(first, length)
-        block = in_finish(p)
-        for n, (peer, flips) in enumerate(peers):
+        block = finish(p)
+        post.send(block.at[:, keep], shared.at[2, at], deal_sems.at[p, 4], place.across("x"))
+        for peer, flips in peers:
             post.send(
                 block.at[:, cols(peer)],
                 dealt.at[at, cols(e)],
                 deal_sems.at[p, flips],
                 (place.dp, peer),
             )
-        post.send(block.at[:, keep], shared.at[2, at], deal_sems.at[p, 4], place.across("x"))
         post.send(block.at[:, keep], shared.at[1, at], deal_sems.at[p, 5], place.across("c"))
-        done = out_finish(p)
-        post.send(done, out_dealt.at[at], deal_sems.at[p, 6], partner, moves)
 
     def place_keys(p, flips, block):
         first, length, _ = pieces[p]
@@ -1092,36 +1198,25 @@
     for p in range(len(pieces)):
         first, length, _ = pieces[p]
         at = pl.ds(first, length)
-        post.arrived(shared.at[2, at], deal_sems.at[p, 4])
-        post.send(shared.at[2, at], shared.at[3, at], deal_sems.at[p, 7], place.across("c"))
-        block = in_rooms[0].at[z, at]
+        block = rooms[0].at[z, at]
         widen(query.at[at, cols(e)], block.at[:, cols(e)], length)
         place_keys(p, 0, block.at[:, keep])
-        place_keys(p, 2, shared.at[2, at])
         post.arrived(shared.at[1, at], deal_sems.at[p, 5])
         place_keys(p, 1, shared.at[1, at])
-        for peer, flips in peers:
+        post.arrived(shared.at[2, at], deal_sems.at[p, 4])
+        post.send(shared.at[2, at], shared.at[3, at], deal_sems.at[p, 6], place.across("c"))
+        place_keys(p, 2, shared.at[2, at])
+        for peer, flips in reversed(peers):
             post.arrived(dealt.at[at, cols(peer)], deal_sems.at[p, flips])
             widen(query.at[at, cols(peer)], dealt.at[at, cols(peer)], length)
-
-        def came(p=p, at=at, length=length):
-            post.arrived(out_dealt.at[at], deal_sems.at[p, 6])
-            widen(output.at[at], out_dealt.at[at], length)
-
-        pl.when(moves)(came)
-        pl.when(~moves)(
-            lambda at=at, length=length: widen(output.at[at], out_rooms[0].at[z, at], length)
-        )
-        post.arrived(shared.at[3, at], deal_sems.at[p, 7])
+        post.arrived(shared.at[3, at], deal_sems.at[p, 6])
         place_keys(p, 3, shared.at[3, at])
     post.close()
 
 
-def sum_weights(in_grad, out_grad, pieces, collective_id):
-    rows, wide = out_grad.shape[0] // 8, out_grad.shape[1]
+def sum_weights(in_grad, wide, pieces, collective_id):
+    rows, total = in_grad.shape[0] // 8, in_grad.shape[1]
     order, count = pieces[0][2], len(pieces)
-    total = in_grad.shape[1]
-    hbm = pl.BlockSpec(memory_space=pltpu.HBM)
     vmem = pl.BlockSpec(memory_space=pltpu.VMEM)
     shape = jax.ShapeDtypeStruct
     return pl.pallas_call(
@@ -1129,26 +1224,22 @@
         out_shape=[
             shape((rows, wide), jnp.float32),
             shape((rows, 2 * wide), jnp.float32),
-            shape((rows, wide), jnp.float32),
         ],
-        in_specs=[hbm] * 2,
-        out_specs=[vmem] * 3,
+        in_specs=[pl.BlockSpec(memory_space=pltpu.HBM)],
+        out_specs=[vmem] * 2,
         scratch_shapes=scatter_rooms(rows, total, order)
-        + scatter_rooms(rows, wide, order)
         + [
             pltpu.VMEM((rows, wide), jnp.bfloat16),
             pltpu.VMEM((4, rows, total - wide), jnp.bfloat16),
-            pltpu.VMEM((rows, wide), jnp.bfloat16),
-            pltpu.SemaphoreType.DMA((2 * sends_of(order, count) + 8 * count,)),
-            pltpu.SemaphoreType.DMA((count, 8)),
+            pltpu.SemaphoreType.DMA((sends_of(order, count) + 7 * count,)),
+            pltpu.SemaphoreType.DMA((count, 7)),
         ]
-        + scatter_sems(order, count)
         + scatter_sems(order, count),
         compiler_params=pltpu.CompilerParams(
             collective_id=collective_id, has_side_effects=True, vmem_limit_bytes=63 * 2**20
         ),
         name="sum_weights",
-    )(in_grad, out_grad)
+    )(in_grad)
 
 
 def weights_kernel(jobs, *refs):
@@ -1455,19 +1546,20 @@
             copy.wait()
 
 
-def expert_slots(ids, my_index, tok_rows):
-    blocks = ids.reshape(-1, tok_rows, 2)
-    chosen = jnp.sum((blocks == my_index).astype(jnp.float32), axis=2)
+def expert_slots(first, second, my_index):
+    tok_rows = first.shape[1]
+    chosen = ((first == my_index) | (second == my_index)).astype(jnp.float32)
     before = jnp.triu(jnp.ones((tok_rows, tok_rows), jnp.float32), 1)
     slots = jnp.where(chosen > 0, jnp.dot(chosen, before), -1.0).astype(jnp.int32)
-    return slots, jnp.sum(blocks, axis=2) - my_index
+    return slots, first + second - my_index
 
 
 def feed_kernel(
     tok,
     slot_count,
     own_rows,
-    cots,
+    cots_left,
+    cots_right,
     gate_weight,
     up_weight,
     down_weight,
@@ -1610,7 +1702,14 @@
         at = pl.ds(first_block(u) * tok, 2 * tok)
         return [
             pltpu.make_async_copy(everyone.at[at], rows_buf.at[u % 2], load_sems.at[u % 2, 0]),
-            pltpu.make_async_copy(cots.at[at], cots_buf.at[u % 2], load_sems.at[u % 2, 1]),
+            pltpu.make_async_copy(
+                cots_left.at[at], cots_buf.at[u % 2, :, pl.ds(0, width // 2)], load_sems.at[u % 2, 1]
+            ),
+            pltpu.make_async_copy(
+                cots_right.at[at],
+                cots_buf.at[u % 2, :, pl.ds(width // 2, width // 2)],
+                load_sems.at[u % 2, 2],
+            ),
         ]
 
     def keep(u):
@@ -1757,11 +1856,22 @@
                 )
 
 
-def feed(own_rows, cots, gate_weight, up_weight, down_weight, router_rows, slots, others, slot_count):
+def feed(
+    own_rows,
+    cots_left,
+    cots_right,
+    gate_weight,
+    up_weight,
+    down_weight,
+    router_rows,
+    slots,
+    others,
+    slot_count,
+):
     tok, width = own_rows.shape
     hidden = gate_weight.shape[0]
     padded = hidden + router_rows.shape[0]
-    total = cots.shape[0]
+    total = cots_left.shape[0]
     kept = total // tok * slot_count
     low = jnp.bfloat16
     hbm = pl.BlockSpec(memory_space=pltpu.HBM)
@@ -1771,7 +1881,7 @@
     chips = 4 * CHIPS_Z
     return pl.pallas_call(
         functools.partial(feed_kernel, tok, slot_count),
-        in_specs=[hbm] * 6 + [vmem] * 2,
+        in_specs=[hbm] * 7 + [vmem] * 2,
         out_specs=[hbm] * 7 + [vmem],
         out_shape=[
             shape((total, width), low),
@@ -1802,14 +1912,24 @@
             pltpu.SemaphoreType.DMA((16 * CHIPS_Z,)),
             pltpu.SemaphoreType.DMA,
             pltpu.SemaphoreType.DMA((4,)),
-            pltpu.SemaphoreType.DMA((2, 2)),
+            pltpu.SemaphoreType.DMA((2, 3)),
             pltpu.SemaphoreType.DMA((2, 6)),
         ],
         compiler_params=pltpu.CompilerParams(
             collective_id=3, has_side_effects=True, vmem_limit_bytes=60 * 2**20
         ),
         name="feed_forward",
-    )(own_rows, cots, gate_weight, up_weight, down_weight, router_rows, slots, others)
+    )(
+        own_rows,
+        cots_left,
+        cots_right,
+        gate_weight,
+        up_weight,
+        down_weight,
+        router_rows,
+        slots,
+        others,
+    )
 
 
 def per_device_torus(
@@ -1845,14 +1965,15 @@
         (i * tok_rows // 4, tok_rows // 4, order) for i in range(4)
     )
     rows_in = keyvalue_weight.shape[0]
-    route_shard = feedforward_routes[0].astype(low).reshape(-1, 128)
+    route_shard = feedforward_routes[0].T.astype(low).reshape(-1, 128)
+    half_model = model_width // 2
     router_shard = router_weight.T.reshape(-1, 128)
     whole = lambda a: ((0, a.shape[0], "zy"),)
-    cut = rows_in * 12 // 16
-    sequence_in, cot_everyone, every_route, router_full, in_weight, out_weight = gather_weights(
+    cut = rows_in * 13 // 16
+    sequence_in, cots_left, every_route, router_full, in_weight, out_weight = gather_weights(
         [
             (attention_in, "expert", quarters("xc")),
-            (cotangent[0], "all", quarters("zyxc")),
+            (cotangent[0, :, :half_model], "all", quarters("zyxc")),
             (route_shard, "dp", whole(route_shard)),
             (router_shard, "dp", whole(router_shard)),
         ],
@@ -1862,7 +1983,9 @@
         ((0, cut, "zy"), (cut, rows_in - cut, "yz")),
         1,
     )
-    every_route = every_route.reshape(-1, 2).astype(jnp.int32)
+    cots_late, sequence_in = lax.optimization_barrier((cotangent[0, :, half_model:], sequence_in))
+    cots_right = lax.all_gather(cots_late, ("dp", "expert"), axis=0, tiled=True)
+    every_route = every_route.reshape(dp_size, 2, group_size, tok_rows).astype(jnp.int32)
     router_full = (
         router_full.reshape(dp_size, 2 * group_size, rows_in)
         .transpose(0, 2, 1)
@@ -1888,7 +2011,9 @@
     feed_matches = expert_matches(mine(feedforward_routes[0]), group_size)
     feed_logits = jnp.dot(feed_in, feedforward_cols, preferred_element_type=f32)
     feed_weights, _ = pair_gates(feed_logits, feed_matches)
-    slots, others = expert_slots(every_route, my_index, tok_rows)
+    slots, others = expert_slots(
+        every_route[:, 0].reshape(-1, tok_rows), every_route[:, 1].reshape(-1, tok_rows), my_index
+    )
     hidden_rows = gate_weight.shape[1]
     padded = -(-hidden_rows // 256) * 256
     router_rows = jnp.pad(
@@ -1896,7 +2021,8 @@
     )
     _, dx_part, out_part, kept_rows, kept_cots, kept_back, kept_act, token_dgate = feed(
         feed_in,
-        cot_everyone,
+        cots_left,
+        cots_right,
         gate_weight[0],
         up_weight[0],
         down_weight[0],
@@ -1912,18 +2038,15 @@
         scatter_dimension=0,
         tiled=True,
     ).T
-    feed_home, grad_in_feed, grad_down = scatter(
+    feed_home, grad_gate, grad_up, grad_down = scatter(
         dx_part,
         "all",
         everywhere("cxyz", "cyxz"),
         4,
         "sum_rows",
-        WeightGrads(kept_rows.shape[0], 2 * padded, padded, model_width),
+        WeightGrads(kept_rows.shape[0], padded, hidden_rows, model_width),
         (kept_back, kept_rows, kept_act, kept_cots),
     )
-    grad_gate = grad_in_feed[:hidden_rows]
-    grad_up = grad_in_feed[padded : padded + hidden_rows]
-    grad_down = grad_down[:hidden_rows]
     gradient = cotangent[0].astype(f32)
     feed_dlogits = gates_back(feed_dgate, feed_weights, feed_matches)
     feed_dnorm = feed_home + jnp.dot(feed_dlogits, feedforward_cols.astype(f32).T, precision=HIGH)
@@ -1936,35 +2059,35 @@
     dmix = lax.dot_general(sequence_grad, out_weight, ACROSS, preferred_element_type=f32).astype(low)
     length, total = projected.shape
     columns = model_width // 2
-    first_sum, dprojected, gate_parts = scatter(
+    first_sum, dprojected, gate_parts, grad_out = scatter(
         out_part,
         "all",
         everywhere("cxyz", "cyxz"),
         7,
         "sum_output_left",
-        AttentionBack(length, total, group_size, tok_rows),
-        (projected, side, log_total, dmix),
+        InTurn(
+            AttentionBack(length, total, group_size, tok_rows),
+            LowGrad(length, query_width, model_width),
+        ),
+        (projected, side, log_total, dmix, mixed, sequence_grad),
         (0, columns),
     )
     attend_dx = lax.dot_general(dprojected, in_weight, ACROSS, preferred_element_type=f32)
-    attend_home = scatter(attend_dx.astype(low), "expert", quarters("cx"), 2, "sum_attention")
-    second_sum, grad_in, grad_out = scatter(
+    attend_dx = jnp.concatenate([attend_dx.astype(low), gate_parts.astype(low)], axis=1)
+    attend_home = scatter(attend_dx, "expert", quarters("cx"), 9, "sum_attention_back")
+    pair_dgate = attend_home[:, model_width : model_width + 2]
+    attend_home = attend_home[:, :model_width]
+    second_sum, grad_projection, grad_in = sum_right(
         out_part,
-        "all",
-        everywhere("cxyz", "cyxz"),
+        (columns, model_width - columns),
+        everywhere("cxyz", "cxyz"),
+        grad_out,
+        ((0, rows_in, "yz"),),
         8,
-        "sum_output_right",
-        LowGrads(length, (model_width, query_width), (total, model_width)),
-        (sequence_in, dprojected, mixed, sequence_grad),
-        (columns, model_width - columns),
+        LowGrad(length, model_width, total),
+        (sequence_in, dprojected),
     )
     layer_output = hidden + jnp.concatenate([first_sum, second_sum], axis=1)
-    pair_dgate = lax.psum_scatter(
-        gate_parts[:, :2].reshape(group_size, tok_rows, 2).transpose(0, 2, 1).reshape(-1, tok_rows),
-        "expert",
-        scatter_dimension=0,
-        tiled=True,
-    ).T
     matches = mine(attend_matches_all)
     weights = mine(attend_weights_all)
     dselected = weights * (pair_dgate - jnp.sum(weights * pair_dgate, axis=1, keepdims=True))
@@ -1988,9 +2111,7 @@
     small = lax.psum(small.astype(f32), ("dp", "expert"))
     small = lax.dynamic_slice_in_dim(small, lax.axis_index("dp") * rows_in, rows_in, 1)
 
-    grad_query, grad_keyvalue, grad_projection = sum_weights(
-        grad_in, grad_out, ((0, rows_in, "yz"),), 6
-    )
+    grad_query, grad_keyvalue = sum_weights(grad_in, query_width, ((0, rows_in, "yz"),), 6)
     return (
         layer_output.astype(low)[None],
         grad_tokens[None],

time: 1530 us -> 1500 us (0.980)
  Pallas kernels: 1350 us -> 1330 us
    pallas_call x0 -> x1, Pallas kernels: none -> 205 us  [sum_right(): pl.pallas_call(functools.partial(sum_right_kernel, rows, pieces, columns,...]
    pallas_call x1, Pallas kernels: 286 us -> 167 us  [sum_weights(): pl.pallas_call(functools.partial(sum_weights_kernel, rows, pieces), out_s...]
    pallas_call x5 -> x4, Pallas kernels: 398 us -> 334 us  [scatter(): pl.pallas_call(functools.partial(scatter_kernel, whose, rows, pieces, col...]
    pallas_call x1, Pallas kernels: 343 us -> 294 us  [gather_weights(): pl.pallas_call(functools.partial(weights_kernel, plan), out_shape=shards...]
  transfers between devices with their start and end apart: 2 -> 3, of which waited for: 0 -> 1; matrix products, arithmetic and copies ran while one was open for 1% -> 3% of each run, Pallas kernels for 29% -> 27%
where the time goes in v6:
time: 1500 us; the launch traced here: 1490 us
  Pallas kernels  1330 us (89%)
  matrix products  75.5 us (5%)
  local copies, waits for them, and re-layouts  36.9 us (2%)
  other arithmetic  19.6 us (1%)
  between operations  15.4 us (1%)
    pallas_call x4, Pallas kernels, scatter(): pl.pallas_call(functools.partial(scatter_kernel, whose, rows, pieces, col...  334 us
    pallas_call x1, Pallas kernels, gather_weights(): pl.pallas_call(functools.partial(weights_kernel, plan), out_shape=shards...  294 us
    pallas_call x1, Pallas kernels, feed(): pl.pallas_call(functools.partial(feed_kernel, tok, slot_count), in_specs=...  263 us
    pallas_call x1, Pallas kernels, sum_right(): pl.pallas_call(functools.partial(sum_right_kernel, rows, pieces, columns,...  205 us
    pallas_call x1, Pallas kernels, sum_weights(): pl.pallas_call(functools.partial(sum_weights_kernel, rows, pieces), out_s...  167 us
    pallas_call x1, Pallas kernels, gather(): pl.pallas_call(functools.partial(gather_kernel, plan, axes), out_shape=[j...  38 us
  transfers between devices with their start and end apart: 3, of which 1 were waited for; matrix products, arithmetic and copies ran while one was open for 3% of the time, Pallas kernels for 27%

profile of v6, /device:TPU:2, one launch (start us, length us, event | category | flops | bytes accessed | tf_op | source)
XLA Modules:
  0.0 1490.3 jit_solution(5247737618220406663)
XLA Ops:
  13.6 294.4 %gather_weights.1 = (bf16[256,3072]{1,0:T(8,128)(2,1)}, bf16[256,2048]{1,0:T(8,128)(2,1)}, bf16[1024,2048]{1,0:T(8,128)(2,1)}, bf16[8192,1024]{1,0:T(8,128)(2,1)...) custom-call(bf16[256,2048]{1,0:T(8,128)(2,1)} %fusion.4.refs_0_, ...), custom_call_target="tpu_custom_call" | custom-call | tf_op jit(solution)/shard_map/gather_weights/pallas_call | solution.py:1323
  309.4 3.4 fusion.19
  316.5 18.0 %convolution_convert_fusion.q.k.v.refs_0_ = bf16[1024,3072]{1,0:T(8,128)(2,1)} fusion(bf16[1024,2048]{1,0:T(8,128)(2,1)S(1)} %copy-done.5, bf16[2048,3072]{1,0:T(8,128)(2,1)} %get-tuple-element.43), kind=kOutput, calls=%fused_computation | convolution fusion | flops 12888047616 | bytes 23068672 | tf_op jit(solution)/shard_map/dot_general | solution.py:1996
  334.5 28.9 %attention.1 = (bf16[1024,2048]{1,0:T(8,128)(2,1)S(1)}, f32[1024,1024]{1,0:T(8,128)}) custom-call(s32[1]{0:T(128)S(6)} %copy.75.prefix, bf16[1024,3072]{1,0:T(8,128)(2,1)} %convolution_convert_fusion.q.k.v.refs_0_, bf16[1024,3072]{1,0:T(8,128)(2,1)} %convolution_convert_fusion.q.k.v.refs_0_, bf16[1024,3072]{1,0:T(8,128)(2,1)} %convolution_convert_fusion.q.k.v.refs_0_, ...), custom_call_target="tpu_custom_call" | custom-call | tf_op jit(solution)/shard_map/attention/pallas_call | solution.py:1412
  365.4 10.3 convolution_convert_fusion.3.source
  375.7 49.6 %sum_attention.1 = f32[256,2048]{1,0:T(8,128)} custom-call(bf16[1024,2048]{1,0:T(8,128)(2,1)} %convolution_convert_fusion.3.source), custom_call_target="tpu_custom_call" | custom-call | tf_op jit(solution)/shard_map/sum_attention/pallas_call | solution.py:1036
  431.9 11.3 all-gather.2.cloned.1.call-done.cots_right
  443.2 263.4 %feed_forward.1 = (bf16[8192,2048]{1,0:T(8,128)(2,1)}, bf16[8192,2048]{1,0:T(8,128)(2,1)}, bf16[8192,2048]{1,0:T(8,128)(2,1)}, bf16[5120,2048]{1,0:T(8,128)(2,1)...) custom-call(bf16[256,2048]{1,0:T(8,128)(2,1)} %copy-done.7, ...), custom_call_target="tpu_custom_call" | custom-call | tf_op jit(solution)/shard_map/feed_forward/pallas_call | solution.py:1882
  708.2 158.0 %sum_rows.1 = (f32[256,2048]{1,0:T(8,128)}, f32[704,2048]{1,0:T(8,128)}, f32[704,2048]{1,0:T(8,128)}, f32[704,2048]{1,0:T(8,128)}) custom-call(bf16[8192,2048]{1,0:T(8,128)(2,1)} %get-tuple-element.52.source, bf16[5120,1536]{1,0:T(8,128)(2,1)} %get-tuple-element.53.refs_0_, bf16[5120,2048]{1,0:T(8,128)(2,1)} %get-tuple-element.54.refs_1_, ...), custom_call_target="tpu_custom_call" | custom-call | tf_op jit(solution)/shard_map/sum_rows/pallas_call | solution.py:1036
  868.9 4.0 multiply_reduce_fusion
  875.8 38.0 %gather_cotangents.1.refs_5_ = bf16[1024,2048]{1,0:T(8,128)(2,1)} custom-call(bf16[256,2048]{1,0:T(8,128)(2,1)} %fusion.28.refs_0_), custom_call_target="tpu_custom_call" | custom-call | tf_op jit(solution)/shard_map/gather_cotangents/pallas_call | solution.py:610
  913.8 13.9 convolution_convert_fusion.2.refs_3_
  927.7 96.4 %sum_output_left.1 = (f32[256,1024]{1,0:T(8,128)}, bf16[1024,3072]{1,0:T(8,128)(2,1)}, f32[1024,128]{1,0:T(8,128)}, bf16[2048,2048]{1,0:T(8,128)(2,1)}) custom-call(bf16[8192,2048]{1,0:T(8,128)(2,1)} %get-tuple-element.50.source, bf16[1024,3072]{1,0:T(8,128)(2,1)} %convolution_convert_fusion.q.k.v.refs_0_, f32[1024,128]{1,0:T(8,128)} %copy-done, ...), custom_call_target="tpu_custom_call" | custom-call | tf_op jit(solution)/shard_map/sum_output_left/pallas_call | solution.py:1036
  1024.1 17.6 %convolution_convert_fusion.1 = bf16[1024,2048]{1,0:T(8,128)(2,1)S(1)} fusion(bf16[1024,3072]{1,0:T(8,128)(2,1)} %get-tuple-element.61.refs_1_, bf16[2048,3072]{1,0:T(8,128)(2,1)} %get-tuple-element.43), kind=kOutput, calls=%fused_computation.2 | convolution fusion | flops 12886999040 | bytes 23068672 | tf_op jit(solution)/shard_map/dot_general | solution.py:2075
  1044.3 30.4 %sum_attention_back.1 = f32[256,2176]{1,0:T(8,128)} custom-call(bf16[1024,2176]{1,0:T(8,128)(2,1)} %pad_maximum_fusion.source), custom_call_target="tpu_custom_call" | custom-call | tf_op jit(solution)/shard_map/sum_attention_back/pallas_call | solution.py:1036
  1076.9 4.8 fusion.10
  1082.3 205.2 %sum_output_right.1 = (f32[256,1024]{1,0:T(8,128)}, f32[256,2048]{1,0:T(8,128)}, bf16[2048,3072]{1,0:T(8,128)(2,1)}) custom-call(bf16[8192,2048]{1,0:T(8,128)(2,1)} %get-tuple-element.50.source, bf16[2048,2048]{1,0:T(8,128)(2,1)} %get-tuple-element.60.out_grad, bf16[1024,2048]{1,0:T(8,128)(2,1)} %get-tuple-element.42.refs_0_, ...), custom_call_target="tpu_custom_call" | custom-call | tf_op jit(solution)/shard_map/sum_output_right/pallas_call | solution.py:1121
  1288.2 5.9 fusion.9
  1294.1 167.1 %sum_weights.1 = (f32[256,2048]{1,0:T(8,128)}, f32[256,4096]{1,0:T(8,128)}) custom-call(bf16[2048,3072]{1,0:T(8,128)(2,1)} %get-tuple-element.64.in_grad), custom_call_target="tpu_custom_call" | custom-call | tf_op jit(solution)/shard_map/sum_weights/pallas_call | solution.py:1222
  1464.0 4.9 copy.76
  1468.9 3.6 copy.77
  1473.9 2.9 copy.79
  1476.8 2.9 copy.80
  1480.7 2.5 copy.81
  (136 shorter events, 37.3 us)
Async XLA Ops:
  7.2 5.2 copy-start.4
  7.2 4.5 copy-start.22
  7.2 5.1 copy-start.15
  7.2 435.9 %all-gather.2.cloned.1.call-start = ((), (), s32[]{:S(2)}) async-start(), calls=%async_computation | async-start | bytes 17301504 | tf_op jit(solution)/shard_map/all_gather | solution.py:1987
  8.9 4.8 copy-start.18
  13.6 295.3 %copy-start.21 = (s32[1,1024,2]{1,2,0:T(2,128)S(1)}, s32[1,1024,2]{1,2,0:T(2,128)}, u32[]{:S(2)}) copy-start(s32[1,1024,2]{1,2,0:T(2,128)} %param.16) | copy-start | bytes 24580
  308.1 558.2 %all-reduce.8.cloned.1.call-start = ((), (), s32[]{:S(2)}) async-start(), calls=%async_computation.2 | async-start | bytes 262144
  314.9 50.5 %slice-start.6 = ((s8[8388608]{0:T(1024)(128)(4,1)}), s8[4194304]{0:T(1024)(128)(4,1)S(1)}, s32[]{:S(2)}) async-start(s8[8388608]{0:T(1024)(128)(4,1)} %bitcast.117), calls=%async_computation.9 | async-start | bytes 8388608
  315.1 19.4 %copy-start = (f32[1024,128]{1,0:T(8,128)}, f32[1024,128]{1,0:T(8,128)S(1)}, u32[]{:S(2)}) copy-start(f32[1024,128]{1,0:T(8,128)S(1)} %pad.8.side.refs_1_) | copy-start | bytes 1572868
  316.5 48.9 %slice-start.7 = ((s8[8388608]{0:T(1024)(128)(4,1)}), s8[4194304]{0:T(1024)(128)(4,1)S(1)}, s32[]{:S(2)}) async-start(s8[8388608]{0:T(1024)(128)(4,1)} %bitcast.117), calls=%async_computation.10 | async-start | bytes 8388608
  375.7 49.6 %copy-start.17 = (bf16[128,128]{1,0:T(8,128)(2,1)S(1)}, bf16[128,128]{1,0:T(8,128)(2,1)}, u32[]{:S(2)}) copy-start(bf16[128,128]{1,0:T(8,128)(2,1)} %get-tuple-element.49) | copy-start | bytes 98308
  431.5 11.6 copy-start.7
  708.2 753.1 %all-reduce.6.cloned.1.call-start = ((), (), s32[]{:S(2)}) async-start(), calls=%async_computation.1 | async-start | bytes 262144 | tf_op jit(solution)/shard_map/psum | solution.py:2111
  868.9 5.3 copy-start.3
  868.9 5.3 copy-start.8
  1024.1 17.6 %copy-start.13 = (f32[1024,128]{1,0:T(8,128)S(1)}, f32[1024,128]{1,0:T(8,128)}, u32[]{:S(2)}) copy-start(f32[1024,128]{1,0:T(8,128)} %get-tuple-element.63) | copy-start | bytes 1572868
  1044.3 30.5 %copy-start.11 = (f32[1024,2]{1,0:T(8,128)S(1)}, f32[1024,2]{1,0:T(8,128)}, u32[]{:S(2)}) copy-start(f32[1024,2]{1,0:T(8,128)} %copy-done.10) | copy-start | bytes 24580
  1044.3 32.6 %copy-start.16 = (f32[2048]{0:T(1024)S(1)}, f32[2048]{0:T(1024)}, u32[]{:S(2)}) copy-start(f32[2048]{0:T(1024)} %param.19) | copy-start | bytes 24580
  1044.3 32.6 %copy-start.19 = (f32[256]{0:T(256)S(1)}, f32[256]{0:T(256)}, u32[]{:S(2)}) copy-start(f32[256]{0:T(256)} %copy-done.18) | copy-start | bytes 3076
  1076.9 4.9 copy-start.9
  1464.0 9.8 slice-start.4
  1464.0 12.8 slice-start.2
  1468.9 4.9 slice-start.5
  1473.8 5.8 slice-start
  (10 other events, 27.5 us)
Sparse Core Ops, SparseCore 0:
  308.2 134.8 all-gather.1
  708.3 123.7 all-reduce.7
  1288.4 121.8 all-reduce.5

commit v7 on v6

--- a/solution.py
+++ b/solution.py
@@ -562,21 +562,28 @@
     return starts, waves, owns
 
 
-def gather_kernel(jobs, axes, *refs):
+def gather_kernel(jobs, axes, filler, *refs):
     count = len(jobs)
-    sources, targets = refs[:count], refs[count : 2 * count]
-    send_sems, arrive_sems, own_sems = refs[2 * count :]
+    sources, given, refs = refs[:count], refs[count : count + filler.operands], refs[count + filler.operands :]
+    targets, made, refs = refs[:count], refs[count : count + filler.results], refs[count + filler.results :]
+    send_sems, arrive_sems, own_sems = refs[:3]
+    own = refs[3:]
     place = Place()
     enter(place, axes)
     post = Post(send_sems, place)
     starts, waves, owns = gather_plan(jobs, place, post, sources, targets, arrive_sems, own_sems)
     for act in sum(starts, []):
         act()
-    for wave in sorted(waves):
+    steps, done = filler.start(given, made, own), 0
+    for number, wave in enumerate(sorted(waves)):
+        share = steps * (number + 1) // len(waves)
+        filler.run(given, made, own, done, share)
+        done = share
         for act in waves[wave]:
             act()
-    for own in owns:
-        own.wait()
+    for copy in owns:
+        copy.wait()
+    filler.end(given, made, own)
     post.close()
 
 
@@ -600,31 +607,48 @@
             come(z, seen, later, 0, 0, wave + 1, condition)
 
 
-def gather(jobs, collective_id, name):
+class Nothing:
+    operands = results = rooms = 0
+    turns = 12
+    shapes, scratch = [], []
+
+    def start(self, given, made, own):
+        return 0
+
+    def run(self, given, made, own, first, last):
+        pass
+
+    def end(self, given, made, own):
+        pass
+
+
+def gather(jobs, collective_id, name, filler=Nothing(), operands=()):
     arrays = [rows for rows, _, _ in jobs]
     sizes = {"all": 32, "dp": 8, "expert": 4}
     plan = tuple((whose, rows.shape[0], pieces) for rows, whose, pieces in jobs)
     axes = "".join(a for a in "cxyz" if any(a in order for _, _, ps in plan for _, _, order in ps))
     lines = sum(len(ps) for _, _, ps in plan)
-    any_spec = pl.BlockSpec(memory_space=pltpu.HBM)
+    hbm = pl.BlockSpec(memory_space=pltpu.HBM)
     return pl.pallas_call(
-        functools.partial(gather_kernel, plan, axes),
+        functools.partial(gather_kernel, plan, axes, filler),
         out_shape=[
             jax.ShapeDtypeStruct((sizes[whose] * r.shape[0], r.shape[1]), r.dtype)
             for r, whose, _ in jobs
-        ],
-        in_specs=[any_spec] * len(jobs),
-        out_specs=[any_spec] * len(jobs),
+        ]
+        + filler.shapes,
+        in_specs=[hbm] * (len(jobs) + len(operands)),
+        out_specs=[hbm] * (len(jobs) + filler.results),
         scratch_shapes=[
             pltpu.SemaphoreType.DMA((110 * lines,)),
             pltpu.SemaphoreType.DMA((lines, 32)),
             pltpu.SemaphoreType.DMA((len(jobs),)),
-        ],
+        ]
+        + filler.scratch,
         compiler_params=pltpu.CompilerParams(
-            collective_id=collective_id, has_side_effects=True
+            collective_id=collective_id, has_side_effects=True, vmem_limit_bytes=48 * 2**20
         ),
         name=name,
-    )(*arrays)
+    )(*arrays, *operands)
 
 
 def add_into(target, terms, length):
@@ -811,21 +835,6 @@
     post.close()
 
 
-class Nothing:
-    operands = results = rooms = 0
-    turns = 12
-    shapes, scratch = [], []
-
-    def start(self, given, made, own):
-        return 0
-
-    def run(self, given, made, own, first, last):
-        pass
-
-    def end(self, given, made, own):
-        pass
-
-
 class WeightGrads(Nothing):
     operands, results, rooms = 4, 3, 6
     TILE, CHUNK = 256, 512
@@ -930,10 +939,10 @@
 
 class LowGrad(Nothing):
     operands, results, rooms = 2, 1, 5
-    TILE, turns = 256, 4
-
-    def __init__(self, rows, left, width):
-        self.tiles, self.width = left // self.TILE, width
+    TILE = 256
+
+    def __init__(self, rows, left, width, turns):
+        self.tiles, self.width, self.turns = left // self.TILE, width, turns
         low = jnp.bfloat16
         self.shapes = [jax.ShapeDtypeStruct((left, width), low)]
         self.scratch = [
@@ -989,6 +998,81 @@
             self.put(made, own, tile).start()
 
     def end(self, given, made, own):
+        for tile in (self.tiles - 2, self.tiles - 1):
+            self.put(made, own, jnp.int32(tile)).wait()
+
+
+class RowGrads(Nothing):
+    operands, results, rooms = 3, 1, 7
+    TILE, turns = 256, 4
+
+    def __init__(self, rows, depth, width):
+        self.tiles, self.width = width // self.TILE, width
+        low = jnp.bfloat16
+        self.shapes = [jax.ShapeDtypeStruct((rows, width + 128), low)]
+        self.scratch = [
+            pltpu.VMEM((rows, depth), low),
+            pltpu.VMEM((2, self.TILE, depth), low),
+            pltpu.VMEM((2, rows, self.TILE), low),
+            pltpu.VMEM((rows, 128), jnp.float32),
+            pltpu.VMEM((rows, 128), low),
+            pltpu.SemaphoreType.DMA((4,)),
+            pltpu.SemaphoreType.DMA((3,)),
+        ]
+
+    def whole(self, given, own):
+        return [
+            pltpu.make_async_copy(given[0], own[0], own[5].at[2]),
+            pltpu.make_async_copy(given[2], own[3], own[5].at[3]),
+        ]
+
+    def right(self, given, own, tile):
+        at = pl.ds(pl.multiple_of(tile * self.TILE, self.TILE), self.TILE)
+        return pltpu.make_async_copy(given[1].at[at], own[1].at[tile % 2], own[5].at[tile % 2])
+
+    def put(self, made, own, tile):
+        at = pl.ds(pl.multiple_of(tile * self.TILE, self.TILE), self.TILE)
+        return pltpu.make_async_copy(own[2].at[tile % 2], made[0].at[:, at], own[6].at[tile % 2])
+
+    def extra(self, made, own):
+        return pltpu.make_async_copy(own[4], made[0].at[:, pl.ds(self.width, 128)], own[6].at[2])
+
+    def start(self, given, made, own):
+        for copy in self.whole(given, own):
+            copy.start()
+        self.right(given, own, jnp.int32(0)).start()
+        return self.tiles
+
+    def run(self, given, made, own, first, last):
+        if first == last:
+            return
+        if first == 0:
+            for copy in self.whole(given, own):
+                copy.wait()
+            own[4][...] = own[3][...].astype(jnp.bfloat16)
+            self.extra(made, own).start()
+
+        @pl.loop(first, last)
+        def _(tile):
+            slot = tile % 2
+
+            @pl.when(tile + 1 < self.tiles)
+            def _():
+                self.right(given, own, tile + 1).start()
+
+            self.right(given, own, tile).wait()
+
+            @pl.when(tile >= 2)
+            def _():
+                self.put(made, own, tile - 2).wait()
+
+            own[2][slot] = lax.dot_general(
+                own[0][...], own[1][slot], ACROSS, preferred_element_type=jnp.float32
+            ).astype(jnp.bfloat16)
+            self.put(made, own, tile).start()
+
+    def end(self, given, made, own):
+        self.extra(made, own).wait()
         for tile in (self.tiles - 2, self.tiles - 1):
             self.put(made, own, jnp.int32(tile)).wait()
 
@@ -1546,6 +1630,113 @@
             copy.wait()
 
 
+def chip_in_turn(u, z_here):
+    u = jnp.asarray(u, jnp.int32)
+    turn, q = u // 4, u % 4
+    flip = lambda *at: ((q == at[0]) | (q == at[1])).astype(jnp.int32)
+    k, xr, yr = turn + (q == 3) - (q == 0), flip(0, 1), flip(0, 2)
+    k = jnp.where(u == 0, 0, jnp.minimum(k, CHIPS_Z - 1))
+    last = 4 * CHIPS_Z - 1
+    xr = jnp.where(u == 0, 0, jnp.where(u == last, 1, xr))
+    yr = jnp.where(u == 0, 0, jnp.where(u == last, 1, yr))
+    inner = (z_here == 1) | (z_here == 2)
+    near = jnp.where(inner, jnp.where(k == 3, 3, jnp.where(k == 2, 0, k + 1)), k)
+    return jnp.where(z_here < 2, near, CHIPS_Z - 1 - near), xr, yr
+
+
+def block_in_turn(u, place):
+    z, xr, yr = chip_in_turn(u, place.at["z"])
+    x = place.at["x"] + xr * (1 - 2 * place.at["x"])
+    y = place.at["y"] + yr * (1 - 2 * place.at["y"])
+    return (z * 2 + y) * 4 + x * 2
+
+
+class BranchRows(Nothing):
+    operands, results, rooms = 3, 1, 8
+
+    def __init__(self, tok, slot_count, blocks, hidden, padded, width):
+        self.tok, self.slot_count, self.hidden = tok, slot_count, hidden
+        low = jnp.bfloat16
+        self.chips = blocks // 2
+        self.shapes = [jax.ShapeDtypeStruct((blocks * tok, width), low)]
+        self.scratch = [
+            pltpu.VMEM((padded, width), low),
+            pltpu.VMEM((blocks, tok), jnp.int32),
+            pltpu.VMEM((2, 2 * slot_count, padded), low),
+            pltpu.VMEM((2 * slot_count, width), low),
+            pltpu.VMEM((2, 2 * tok, width), low),
+            pltpu.SemaphoreType.DMA((2,)),
+            pltpu.SemaphoreType.DMA((2,)),
+            pltpu.SemaphoreType.DMA((2,)),
+        ]
+
+    def whole(self, given, own):
+        return [
+            pltpu.make_async_copy(given[1], own[0].at[pl.ds(0, self.hidden)], own[5].at[0]),
+            pltpu.make_async_copy(given[2], own[1], own[5].at[1]),
+        ]
+
+    def take(self, given, own, u):
+        rows = pl.ds(pl.multiple_of(u * 2 * self.slot_count, 64), 2 * self.slot_count)
+        return pltpu.make_async_copy(given[0].at[rows], own[2].at[u % 2], own[6].at[u % 2])
+
+    def put(self, made, own, u):
+        rows = pl.ds(block_in_turn(u, Place()) * self.tok, 2 * self.tok)
+        return pltpu.make_async_copy(own[4].at[u % 2], made[0].at[rows], own[7].at[u % 2])
+
+    def start(self, given, made, own):
+        for copy in self.whole(given, own):
+            copy.start()
+        self.take(given, own, jnp.int32(0)).start()
+        own[0][self.hidden :, :] = jnp.zeros_like(own[0][self.hidden :, :])
+        return self.chips
+
+    def run(self, given, made, own, first, last):
+        if first == last:
+            return
+        if first == 0:
+            for copy in self.whole(given, own):
+                copy.wait()
+        w_down, slots, acts, outs, placed = own[:5]
+
+        @pl.loop(first, last)
+        def _(u):
+            s = u % 2
+
+            @pl.when(u + 1 < self.chips)
+            def _():
+                self.take(given, own, u + 1).start()
+
+            self.take(given, own, u).wait()
+
+            @pl.when(u >= 2)
+            def _():
+                self.put(made, own, u - 2).wait()
+
+            @pl.loop(0, outs.shape[1] // 256)
+            def _(n):
+                cols = pl.ds(pl.multiple_of(n * 256, 256), 256)
+                outs[:, cols] = jnp.dot(
+                    acts[s], w_down[:, cols], preferred_element_type=jnp.float32
+                ).astype(jnp.bfloat16)
+
+            block = block_in_turn(u, Place())
+            for b in range(2):
+                row = slots[pl.ds(block + b, 1), :]
+                number = lax.broadcasted_iota(jnp.int32, (self.slot_count, self.tok), 0)
+                table = (number == row).astype(jnp.float32).T.astype(jnp.bfloat16)
+                placed[s, pl.ds(b * self.tok, self.tok), :] = jnp.dot(
+                    table,
+                    outs[pl.ds(b * self.slot_count, self.slot_count), :],
+                    preferred_element_type=jnp.float32,
+                ).astype(jnp.bfloat16)
+            self.put(made, own, u).start()
+
+    def end(self, given, made, own):
+        for u in (self.chips - 2, self.chips - 1):
+            self.put(made, own, jnp.int32(u)).wait()
+
+
 def expert_slots(first, second, my_index):
     tok_rows = first.shape[1]
     chosen = ((first == my_index) | (second == my_index)).astype(jnp.float32)
@@ -1568,7 +1759,6 @@
     others,
     everyone,
     dx_part,
-    out_part,
     x_kept,
     g_kept,
     d_kept,
@@ -1585,9 +1775,7 @@
     ds,
     acts,
     dx_buf,
-    out_buf,
     dxs,
-    outs,
     send_sems,
     arrive_sems,
     own_sem,
@@ -1623,22 +1811,10 @@
     enter(place, "cxyz")
 
     def chip(u):
-        u = jnp.asarray(u, jnp.int32)
-        turn, q = u // 4, u % 4
-        flip = lambda *at: ((q == at[0]) | (q == at[1])).astype(jnp.int32)
-        k, xr, yr = turn + (q == 3) - (q == 0), flip(0, 1), flip(0, 2)
-        k = jnp.where(u == 0, 0, jnp.minimum(k, CHIPS_Z - 1))
-        xr = jnp.where(u == 0, 0, jnp.where(u == chips - 1, 1, xr))
-        yr = jnp.where(u == 0, 0, jnp.where(u == chips - 1, 1, yr))
-        inner = (z_here == 1) | (z_here == 2)
-        near = jnp.where(inner, jnp.where(k == 3, 3, jnp.where(k == 2, 0, k + 1)), k)
-        return jnp.where(z_here < 2, near, CHIPS_Z - 1 - near), xr, yr
+        return chip_in_turn(u, z_here)
 
     def first_block(u):
-        z, xr, yr = chip(u)
-        x = place.at["x"] + xr * (1 - 2 * place.at["x"])
-        y = place.at["y"] + yr * (1 - 2 * place.at["y"])
-        return (z * 2 + y) * 4 + x * 2
+        return block_in_turn(u, place)
 
     def part(p, u, core):
         return everyone.at[pl.ds((first_block(u) + core) * tok + p * half, half)]
@@ -1722,7 +1898,6 @@
             pltpu.make_async_copy(ds.at[s], d_kept.at[rows], keep_sems.at[s, 2]),
             pltpu.make_async_copy(acts.at[s], a_kept.at[rows], keep_sems.at[s, 3]),
             pltpu.make_async_copy(dx_buf.at[s], dx_part.at[blocks], keep_sems.at[s, 4]),
-            pltpu.make_async_copy(out_buf.at[s], out_part.at[blocks], keep_sems.at[s, 5]),
         ]
 
     hand_on(0, [own_rows.at[pl.ds(0, half)], own_rows.at[pl.ds(half, half)]])
@@ -1800,9 +1975,6 @@
         def _(n):
             cols = pl.ds(pl.multiple_of(n * 256, 256), 256)
             dxs[:, cols] = jnp.dot(ds[s], w_in[:, cols], preferred_element_type=f32).astype(low)
-            outs[:, cols] = jnp.dot(acts[s], w_down[:, cols], preferred_element_type=f32).astype(
-                low
-            )
 
         for b in range(2):
             at = pl.ds(b * slot_count, slot_count)
@@ -1810,9 +1982,6 @@
             to = pl.ds(b * tok, tok)
             dx_buf[s, to, :] = jnp.dot(
                 back_table, dxs[at, :], preferred_element_type=f32
-            ).astype(low)
-            out_buf[s, to, :] = jnp.dot(
-                back_table, outs[at, :], preferred_element_type=f32
             ).astype(low)
 
     @pl.loop(0, chips)
@@ -1882,9 +2051,8 @@
     return pl.pallas_call(
         functools.partial(feed_kernel, tok, slot_count),
         in_specs=[hbm] * 7 + [vmem] * 2,
-        out_specs=[hbm] * 7 + [vmem],
+        out_specs=[hbm] * 6 + [vmem],
         out_shape=[
-            shape((total, width), low),
             shape((total, width), low),
             shape((total, width), low),
             shape((kept, width), low),
@@ -1905,8 +2073,6 @@
             pltpu.VMEM((2, pair, 2 * padded), low),
             pltpu.VMEM((2, pair, padded), low),
             pltpu.VMEM((2, 2 * tok, width), low),
-            pltpu.VMEM((2, 2 * tok, width), low),
-            pltpu.VMEM((pair, width), low),
             pltpu.VMEM((pair, width), low),
             pltpu.SemaphoreType.DMA((10 * chips,)),
             pltpu.SemaphoreType.DMA((16 * CHIPS_Z,)),
@@ -2019,7 +2185,7 @@
     router_rows = jnp.pad(
         feedforward_cols.T, ((0, padded - hidden_rows - group_size), (0, 0))
     )
-    _, dx_part, out_part, kept_rows, kept_cots, kept_back, kept_act, token_dgate = feed(
+    _, dx_part, kept_rows, kept_cots, kept_back, kept_act, token_dgate = feed(
         feed_in,
         cots_left,
         cots_right,
@@ -2053,8 +2219,12 @@
     grad_gain_feed = jnp.sum(feed_dnorm * unit_feed, axis=0)
     hidden_grad = gradient + norm_back(feed_dnorm, gain_feedforward, unit_feed, factor_feed)
 
-    (sequence_grad,) = gather(
-        [(hidden_grad.astype(low), "expert", quarters("xc"))], 5, "gather_cotangents"
+    sequence_grad, out_part = gather(
+        [(hidden_grad.astype(low), "expert", quarters("xc"))],
+        5,
+        "gather_cotangents",
+        BranchRows(tok_rows, slot_count, slots.shape[0], hidden_rows, padded, model_width),
+        (kept_act, down_weight[0], slots),
     )
     dmix = lax.dot_general(sequence_grad, out_weight, ACROSS, preferred_element_type=f32).astype(low)
     length, total = projected.shape
@@ -2067,26 +2237,32 @@
         "sum_output_left",
         InTurn(
             AttentionBack(length, total, group_size, tok_rows),
-            LowGrad(length, query_width, model_width),
+            LowGrad(length, query_width, model_width, 4),
         ),
         (projected, side, log_total, dmix, mixed, sequence_grad),
         (0, columns),
     )
-    attend_dx = lax.dot_general(dprojected, in_weight, ACROSS, preferred_element_type=f32)
-    attend_dx = jnp.concatenate([attend_dx.astype(low), gate_parts.astype(low)], axis=1)
-    attend_home = scatter(attend_dx, "expert", quarters("cx"), 9, "sum_attention_back")
-    pair_dgate = attend_home[:, model_width : model_width + 2]
-    attend_home = attend_home[:, :model_width]
-    second_sum, grad_projection, grad_in = sum_right(
+    second_sum, grad_projection, attend_dx = sum_right(
         out_part,
         (columns, model_width - columns),
         everywhere("cxyz", "cxyz"),
         grad_out,
         ((0, rows_in, "yz"),),
         8,
-        LowGrad(length, model_width, total),
+        RowGrads(length, total, model_width),
+        (dprojected, in_weight, gate_parts),
+    )
+    attend_home, grad_in = scatter(
+        attend_dx,
+        "expert",
+        quarters("cx"),
+        9,
+        "sum_attention_back",
+        LowGrad(length, model_width, total, 1),
         (sequence_in, dprojected),
     )
+    pair_dgate = attend_home[:, model_width : model_width + 2]
+    attend_home = attend_home[:, :model_width]
     layer_output = hidden + jnp.concatenate([first_sum, second_sum], axis=1)
     matches = mine(attend_matches_all)
     weights = mine(attend_weights_all)

time: 1500 us -> 1470 us (0.980)
  matrix products: 75.5 us -> 55 us
    pallas_call x1, Pallas kernels: 38 us -> 60.4 us  [gather(): pl.pallas_call(functools.partial(gather_kernel, plan, axes, filler), out_...]
    pallas_call x1, Pallas kernels: 263 us -> 241 us  [feed(): pl.pallas_call(functools.partial(feed_kernel, tok, slot_count), in_specs=...]
    dot_general x1 -> x0, matrix products: 17.6 us -> none  [per_device_torus(): lax.dot_general(dprojected, in_weight, ACROSS, preferred_element_type=f32)]
  transfers between devices with their start and end apart: 3 -> 3, of which waited for: 1 -> 0; matrix products, arithmetic and copies ran while one was open for 3% -> 3% of each run, Pallas kernels for 27% -> 28%
where the time goes in v7:
time: 1470 us; the launch traced here: 1460 us
  Pallas kernels  1330 us (90%)
  matrix products  55 us (4%)
  local copies, waits for them, and re-layouts  38.7 us (3%)
  between operations  15.2 us (1%)
  other arithmetic  15 us (1%)
    pallas_call x4, Pallas kernels, scatter(): pl.pallas_call(functools.partial(scatter_kernel, whose, rows, pieces, col...  345 us
    pallas_call x1, Pallas kernels, gather_weights(): pl.pallas_call(functools.partial(weights_kernel, plan), out_shape=shards...  294 us
    pallas_call x1, Pallas kernels, feed(): pl.pallas_call(functools.partial(feed_kernel, tok, slot_count), in_specs=...  241 us
    pallas_call x1, Pallas kernels, sum_right(): pl.pallas_call(functools.partial(sum_right_kernel, rows, pieces, columns,...  198 us
    pallas_call x1, Pallas kernels, sum_weights(): pl.pallas_call(functools.partial(sum_weights_kernel, rows, pieces), out_s...  167 us
    pallas_call x1, Pallas kernels, gather(): pl.pallas_call(functools.partial(gather_kernel, plan, axes, filler), out_...  60.4 us
  transfers between devices with their start and end apart: 3, of which 0 were waited for; matrix products, arithmetic and copies ran while one was open for 3% of the time, Pallas kernels for 28%

profile of v7, /device:TPU:2, one launch (start us, length us, event | category | flops | bytes accessed | tf_op | source)
XLA Modules:
  0.0 1458.3 jit_solution(308248684348735203)
XLA Ops:
  8.9 2.2 slice_bitcast_fusion
  13.6 294.4 %gather_weights.1 = (bf16[256,3072]{1,0:T(8,128)(2,1)}, bf16[256,2048]{1,0:T(8,128)(2,1)}, bf16[1024,2048]{1,0:T(8,128)(2,1)}, bf16[8192,1024]{1,0:T(8,128)(2,1)...) custom-call(bf16[256,2048]{1,0:T(8,128)(2,1)} %fusion.4.refs_0_, ...), custom_call_target="tpu_custom_call" | custom-call | tf_op jit(solution)/shard_map/gather_weights/pallas_call | solution.py:1407
  309.4 3.4 fusion.19
  316.5 18.3 %convolution_convert_fusion.q.k.v.refs_0_ = bf16[1024,3072]{1,0:T(8,128)(2,1)} fusion(bf16[1024,2048]{1,0:T(8,128)(2,1)S(1)} %copy-done.9, bf16[2048,3072]{1,0:T(8,128)(2,1)} %get-tuple-element.46.refs_1_), kind=kOutput, calls=%fused_computation | convolution fusion | flops 12888047616 | bytes 23068672 | tf_op jit(solution)/shard_map/dot_general | solution.py:2162
  334.8 28.9 %attention.1 = (bf16[1024,2048]{1,0:T(8,128)(2,1)S(1)}, f32[1024,1024]{1,0:T(8,128)}) custom-call(s32[1]{0:T(128)S(6)} %copy.75.prefix, bf16[1024,3072]{1,0:T(8,128)(2,1)} %convolution_convert_fusion.q.k.v.refs_0_, bf16[1024,3072]{1,0:T(8,128)(2,1)} %convolution_convert_fusion.q.k.v.refs_0_, bf16[1024,3072]{1,0:T(8,128)(2,1)} %convolution_convert_fusion.q.k.v.refs_0_, ...), custom_call_target="tpu_custom_call" | custom-call | tf_op jit(solution)/shard_map/attention/pallas_call | solution.py:1496
  365.7 10.3 convolution_convert_fusion.2.source
  376.0 61.2 %sum_attention.1 = f32[256,2048]{1,0:T(8,128)} custom-call(bf16[1024,2048]{1,0:T(8,128)(2,1)} %convolution_convert_fusion.2.source), custom_call_target="tpu_custom_call" | custom-call | tf_op jit(solution)/shard_map/sum_attention/pallas_call | solution.py:1120
  439.6 2.3 multiply_reduce_fusion.2
  444.4 241.1 %feed_forward.1 = (bf16[8192,2048]{1,0:T(8,128)(2,1)}, bf16[8192,2048]{1,0:T(8,128)(2,1)}, bf16[5120,2048]{1,0:T(8,128)(2,1)}, bf16[5120,2048]{1,0:T(8,128)(2,1)...) custom-call(bf16[256,2048]{1,0:T(8,128)(2,1)} %copy-done.11, ...), custom_call_target="tpu_custom_call" | custom-call | tf_op jit(solution)/shard_map/feed_forward/pallas_call | solution.py:2051
  687.3 158.1 %sum_rows.1 = (f32[256,2048]{1,0:T(8,128)}, f32[704,2048]{1,0:T(8,128)}, f32[704,2048]{1,0:T(8,128)}, f32[704,2048]{1,0:T(8,128)}) custom-call(bf16[8192,2048]{1,0:T(8,128)(2,1)} %get-tuple-element.53.source, bf16[5120,1536]{1,0:T(8,128)(2,1)} %get-tuple-element.54.refs_0_, bf16[5120,2048]{1,0:T(8,128)(2,1)} %get-tuple-element.55.refs_1_, ...), custom_call_target="tpu_custom_call" | custom-call | tf_op jit(solution)/shard_map/sum_rows/pallas_call | solution.py:1120
  846.3 4.0 multiply_reduce_fusion
  853.4 60.4 %gather_cotangents.1 = (bf16[1024,2048]{1,0:T(8,128)(2,1)}, bf16[8192,2048]{1,0:T(8,128)(2,1)}) custom-call(bf16[256,2048]{1,0:T(8,128)(2,1)S(1)} %fusion.28.refs_0_, bf16[5120,768]{1,0:T(8,128)(2,1)} %get-tuple-element.56.refs_2_.refs_1_, bf16[704,2048]{1,0:T(8,128)(2,1)S(1)} %bitcast.89, s32[32,256]{1,0:T(8,128)S(1)} %copy-done.3), custom_call_target="tpu_custom_call" | custom-call | tf_op jit(solution)/shard_map/gather_cotangents/pallas_call | solution.py:632
  913.9 12.0 convolution_convert_fusion.1.refs_3_
  925.9 96.4 %sum_output_left.1 = (f32[256,1024]{1,0:T(8,128)}, bf16[1024,3072]{1,0:T(8,128)(2,1)}, f32[1024,128]{1,0:T(8,128)}, bf16[2048,2048]{1,0:T(8,128)(2,1)}) custom-call(bf16[8192,2048]{1,0:T(8,128)(2,1)} %get-tuple-element.60.source, bf16[1024,3072]{1,0:T(8,128)(2,1)} %convolution_convert_fusion.q.k.v.refs_0_, f32[1024,128]{1,0:T(8,128)} %copy-done.1, ...), custom_call_target="tpu_custom_call" | custom-call | tf_op jit(solution)/shard_map/sum_output_left/pallas_call | solution.py:1120
  1022.3 198.0 %sum_output_right.1 = (f32[256,1024]{1,0:T(8,128)}, f32[256,2048]{1,0:T(8,128)}, bf16[1024,2176]{1,0:T(8,128)(2,1)}) custom-call(bf16[8192,2048]{1,0:T(8,128)(2,1)} %get-tuple-element.60.source, bf16[2048,2048]{1,0:T(8,128)(2,1)} %get-tuple-element.64.out_grad, bf16[1024,3072]{1,0:T(8,128)(2,1)} %get-tuple-element.65.refs_0_.refs_1_, ...), custom_call_target="tpu_custom_call" | custom-call | tf_op jit(solution)/shard_map/sum_output_right/pallas_call | solution.py:1205
  1220.3 29.0 %sum_attention_back.1 = (f32[256,2176]{1,0:T(8,128)}, bf16[2048,3072]{1,0:T(8,128)(2,1)}) custom-call(bf16[1024,2176]{1,0:T(8,128)(2,1)} %get-tuple-element.68.source, bf16[1024,2048]{1,0:T(8,128)(2,1)} %get-tuple-element.45.refs_0_, bf16[1024,3072]{1,0:T(8,128)(2,1)} %get-tuple-element.65.refs_0_.refs_1_), custom_call_target="tpu_custom_call" | custom-call | tf_op jit(solution)/shard_map/sum_attention_back/pallas_call | solution.py:1120
  1251.5 4.9 fusion.10
  1258.2 4.8 fusion.9
  1263.0 166.6 %sum_weights.1 = (f32[256,2048]{1,0:T(8,128)}, f32[256,4096]{1,0:T(8,128)}) custom-call(bf16[2048,3072]{1,0:T(8,128)(2,1)} %get-tuple-element.70.in_grad), custom_call_target="tpu_custom_call" | custom-call | tf_op jit(solution)/shard_map/sum_weights/pallas_call | solution.py:1306
  1432.3 4.9 copy.76
  1437.3 3.6 copy.77
  1442.2 2.9 copy.79
  1445.1 2.9 copy.80
  1449.1 2.5 copy.81
  (146 shorter events, 29.9 us)
Async XLA Ops:
  7.2 5.2 copy-start.7
  7.2 5.1 copy-start.19
  7.2 436.6 %all-gather.2.cloned.1.call-start = ((), (), s32[]{:S(2)}) async-start(), calls=%async_computation | async-start | bytes 17301504 | tf_op jit(solution)/shard_map/all_gather | solution.py:2153
  13.6 295.3 %copy-start.25 = (s32[1,1024,2]{1,2,0:T(2,128)S(1)}, s32[1,1024,2]{1,2,0:T(2,128)}, u32[]{:S(2)}) copy-start(s32[1,1024,2]{1,2,0:T(2,128)} %param.16) | copy-start | bytes 24580
  308.1 537.3 %all-reduce.8.cloned.1.call-start = ((), (), s32[]{:S(2)}) async-start(), calls=%async_computation.2 | async-start | bytes 262144
  314.9 50.8 %slice-start.6 = ((s8[8388608]{0:T(1024)(128)(4,1)}), s8[4194304]{0:T(1024)(128)(4,1)S(1)}, s32[]{:S(2)}) async-start(s8[8388608]{0:T(1024)(128)(4,1)} %bitcast.116), calls=%async_computation.9 | async-start | bytes 8388608
  315.1 19.7 %copy-start.1 = (f32[1024,128]{1,0:T(8,128)}, f32[1024,128]{1,0:T(8,128)S(1)}, u32[]{:S(2)}) copy-start(f32[1024,128]{1,0:T(8,128)S(1)} %pad.8.side.refs_1_) | copy-start | bytes 1572868
  316.5 49.2 %slice-start.7 = ((s8[8388608]{0:T(1024)(128)(4,1)}), s8[4194304]{0:T(1024)(128)(4,1)S(1)}, s32[]{:S(2)}) async-start(s8[8388608]{0:T(1024)(128)(4,1)} %bitcast.116), calls=%async_computation.10 | async-start | bytes 8388608
  376.0 61.3 %copy-start.21 = (bf16[128,128]{1,0:T(8,128)(2,1)S(1)}, bf16[128,128]{1,0:T(8,128)(2,1)}, u32[]{:S(2)}) copy-start(bf16[128,128]{1,0:T(8,128)(2,1)} %get-tuple-element.52) | copy-start | bytes 98308
  687.2 742.4 %all-reduce.6.cloned.1.call-start = ((), (), s32[]{:S(2)}) async-start(), calls=%async_computation.1 | async-start | bytes 262144 | tf_op jit(solution)/shard_map/psum | solution.py:2287
  846.3 5.4 copy-start.5
  846.3 5.3 copy-start.13
  851.6 62.3 %slice-start.8 = ((s8[8388608]{0:T(1024)(128)(4,1)}), s8[4194304]{0:T(1024)(128)(4,1)S(1)}, s32[]{:S(2)}) async-start(s8[8388608]{0:T(1024)(128)(4,1)} %bitcast.118), calls=%async_computation.11 | async-start | bytes 8388608
  853.4 60.5 %slice-start.9 = ((s8[8388608]{0:T(1024)(128)(4,1)}), s8[4194304]{0:T(1024)(128)(4,1)S(1)}, s32[]{:S(2)}) async-start(s8[8388608]{0:T(1024)(128)(4,1)} %bitcast.118), calls=%async_computation.12 | async-start | bytes 8388608
  1220.3 29.1 %copy-start.16 = (f32[1024,2]{1,0:T(8,128)S(1)}, f32[1024,2]{1,0:T(8,128)}, u32[]{:S(2)}) copy-start(f32[1024,2]{1,0:T(8,128)} %copy-done.15) | copy-start | bytes 24580
  1220.3 31.2 %copy-start.20 = (f32[2048]{0:T(1024)S(1)}, f32[2048]{0:T(1024)}, u32[]{:S(2)}) copy-start(f32[2048]{0:T(1024)} %param.19) | copy-start | bytes 24580
  1220.3 31.2 %copy-start.23 = (f32[256]{0:T(256)S(1)}, f32[256]{0:T(256)}, u32[]{:S(2)}) copy-start(f32[256]{0:T(256)} %copy-done.22) | copy-start | bytes 3076
  1251.5 4.9 copy-start.14
  1251.5 5.5 copy-start.12
  1251.5 6.7 copy-start.8
  1432.3 9.8 slice-start.4
  1432.3 12.8 slice-start.2
  1437.3 4.9 slice-start.5
  1442.2 5.8 slice-start
  (16 other events, 43.1 us)
Sparse Core Ops, SparseCore 0:
  308.2 134.8 all-gather.1
  687.3 123.6 all-reduce.7
  1258.3 127.3 all-reduce.5

commit v8 on v7

--- a/solution.py
+++ b/solution.py
@@ -1134,8 +1134,7 @@
     return out if filler.results else out[0]
 
 
-def sum_right_kernel(rows, pieces, columns, out_rows, out_pieces, filler, source, out_grad, *refs):
-    source = source.at[:, pl.ds(*columns)]
+def sum_with_output_kernel(rows, pieces, out_rows, out_pieces, filler, source, out_grad, *refs):
     given, refs = refs[: filler.operands], refs[filler.operands :]
     result, output, refs = refs[0], refs[1], refs[2:]
     made, refs = refs[: filler.results], refs[filler.results :]
@@ -1150,7 +1149,7 @@
     z, e = place.at["z"], place.expert
     partner, moves = (e * 2 + place.at["y"], z), z != e
     loads, works, finish = scatter_plan(
-        "all", rows, pieces, place, post, source, rooms, sems
+        "expert", rows, pieces, place, post, source, rooms, sems
     )
     out_loads, out_works, out_finish = scatter_plan(
         "dp", out_rows, out_pieces, place, post, out_grad, out_rooms, out_sems
@@ -1163,7 +1162,7 @@
     turns = [time for time in times if time >= 0]
     done = 0
     for time in times:
-        for plan in (out_works, works):
+        for plan in (works, out_works):
             for at, act in plan:
                 if at == time:
                     act()
@@ -1194,8 +1193,8 @@
     post.close()
 
 
-def sum_right(array, columns, pieces, out_grad, out_pieces, collective_id, filler, operands):
-    rows, width = array.shape[0] // 32, columns[1]
+def sum_with_output(array, pieces, out_grad, out_pieces, collective_id, filler, operands):
+    rows, width = array.shape[0] // 4, array.shape[1]
     out_rows, out_width = out_grad.shape[0] // 8, out_grad.shape[1]
     order, out_order = pieces[0][2], out_pieces[0][2]
     hbm = pl.BlockSpec(memory_space=pltpu.HBM)
@@ -1204,7 +1203,7 @@
     sends = sends_of(order, len(pieces)) + sends_of(out_order, len(out_pieces)) + len(out_pieces)
     return pl.pallas_call(
         functools.partial(
-            sum_right_kernel, rows, pieces, columns, out_rows, out_pieces, filler
+            sum_with_output_kernel, rows, pieces, out_rows, out_pieces, filler
         ),
         out_shape=[
             shape((rows, width), jnp.float32),
@@ -1226,7 +1225,7 @@
         compiler_params=pltpu.CompilerParams(
             collective_id=collective_id, has_side_effects=True, vmem_limit_bytes=63 * 2**20
         ),
-        name="sum_output_right",
+        name="sum_attention_back",
     )(array, out_grad, *operands)
 
 
@@ -1787,7 +1786,7 @@
     z_here = place.at["z"]
     hidden = gate_weight.shape[0]
     padded = w_down.shape[0]
-    width = own_rows.shape[1]
+    width, cut = own_rows.shape[1], cots_left.shape[1]
     half = tok // 2
     chips = 4 * CHIPS_Z
     pair = 2 * slot_count
@@ -1879,11 +1878,11 @@
         return [
             pltpu.make_async_copy(everyone.at[at], rows_buf.at[u % 2], load_sems.at[u % 2, 0]),
             pltpu.make_async_copy(
-                cots_left.at[at], cots_buf.at[u % 2, :, pl.ds(0, width // 2)], load_sems.at[u % 2, 1]
+                cots_left.at[at], cots_buf.at[u % 2, :, pl.ds(0, cut)], load_sems.at[u % 2, 1]
             ),
             pltpu.make_async_copy(
                 cots_right.at[at],
-                cots_buf.at[u % 2, :, pl.ds(width // 2, width // 2)],
+                cots_buf.at[u % 2, :, pl.ds(cut, width - cut)],
                 load_sems.at[u % 2, 2],
             ),
         ]
@@ -2132,14 +2131,14 @@
     )
     rows_in = keyvalue_weight.shape[0]
     route_shard = feedforward_routes[0].T.astype(low).reshape(-1, 128)
-    half_model = model_width // 2
+    early = model_width * 5 // 8
     router_shard = router_weight.T.reshape(-1, 128)
     whole = lambda a: ((0, a.shape[0], "zy"),)
     cut = rows_in * 13 // 16
     sequence_in, cots_left, every_route, router_full, in_weight, out_weight = gather_weights(
         [
             (attention_in, "expert", quarters("xc")),
-            (cotangent[0, :, :half_model], "all", quarters("zyxc")),
+            (cotangent[0, :, :early], "all", quarters("zyxc")),
             (route_shard, "dp", whole(route_shard)),
             (router_shard, "dp", whole(router_shard)),
         ],
@@ -2149,7 +2148,7 @@
         ((0, cut, "zy"), (cut, rows_in - cut, "yz")),
         1,
     )
-    cots_late, sequence_in = lax.optimization_barrier((cotangent[0, :, half_model:], sequence_in))
+    cots_late, sequence_in = lax.optimization_barrier((cotangent[0, :, early:], sequence_in))
     cots_right = lax.all_gather(cots_late, ("dp", "expert"), axis=0, tiled=True)
     every_route = every_route.reshape(dp_size, 2, group_size, tok_rows).astype(jnp.int32)
     router_full = (
@@ -2242,23 +2241,23 @@
         (projected, side, log_total, dmix, mixed, sequence_grad),
         (0, columns),
     )
-    second_sum, grad_projection, attend_dx = sum_right(
+    second_sum, attend_dx = scatter(
         out_part,
+        "all",
+        everywhere("cxyz", "cyxz"),
+        8,
+        "sum_output_right",
+        RowGrads(length, total, model_width),
+        (dprojected, in_weight, gate_parts),
         (columns, model_width - columns),
-        everywhere("cxyz", "cxyz"),
+    )
+    attend_home, grad_projection, grad_in = sum_with_output(
+        attend_dx,
+        quarters("cx"),
         grad_out,
         ((0, rows_in, "yz"),),
-        8,
-        RowGrads(length, total, model_width),
-        (dprojected, in_weight, gate_parts),
-    )
-    attend_home, grad_in = scatter(
-        attend_dx,
-        "expert",
-        quarters("cx"),
         9,
-        "sum_attention_back",
-        LowGrad(length, model_width, total, 1),
+        LowGrad(length, model_width, total, 4),
         (sequence_in, dprojected),
     )
     pair_dgate = attend_home[:, model_width : model_width + 2]

time: 1470 us -> 1490 us (1.014)
  Pallas kernels: 1330 us -> 1350 us
    pallas_call x4, Pallas kernels: 345 us -> 390 us  [scatter(): pl.pallas_call(functools.partial(scatter_kernel, whose, rows, pieces, col...]
    pallas_call x1, Pallas kernels: 198 us -> 154 us  [sum_with_output(): pl.pallas_call(functools.partial(sum_with_output_kernel, rows, pieces, ou...]
  transfers between devices with their start and end apart: 3 -> 3, of which waited for: 0 -> 0; matrix products, arithmetic and copies ran while one was open for 3% -> 3% of each run, Pallas kernels for 28% -> 27%
where the time goes in v8:
time: 1490 us; the launch traced here: 1480 us
  Pallas kernels  1350 us (91%)
  matrix products  55 us (4%)
  local copies, waits for them, and re-layouts  40.2 us (3%)
  between operations  15.2 us (1%)
    pallas_call x4, Pallas kernels, scatter(): pl.pallas_call(functools.partial(scatter_kernel, whose, rows, pieces, col...  390 us
    pallas_call x1, Pallas kernels, gather_weights(): pl.pallas_call(functools.partial(weights_kernel, plan), out_shape=shards...  304 us
    pallas_call x1, Pallas kernels, feed(): pl.pallas_call(functools.partial(feed_kernel, tok, slot_count), in_specs=...  244 us
    pallas_call x1, Pallas kernels, sum_weights(): pl.pallas_call(functools.partial(sum_weights_kernel, rows, pieces), out_s...  171 us
    pallas_call x1, Pallas kernels, sum_with_output(): pl.pallas_call(functools.partial(sum_with_output_kernel, rows, pieces, ou...  154 us
    pallas_call x1, Pallas kernels, gather(): pl.pallas_call(functools.partial(gather_kernel, plan, axes, filler), out_...  61.9 us
  transfers between devices with their start and end apart: 3, of which 0 were waited for; matrix products, arithmetic and copies ran while one was open for 3% of the time, Pallas kernels for 27%

profile of v8, /device:TPU:2, one launch (start us, length us, event | category | flops | bytes accessed | tf_op | source)
XLA Modules:
  0.0 1478.8 jit_solution(4643174040580277641)
XLA Ops:
  7.3 2.0 slice_bitcast_fusion.refs_1_
  13.9 304.3 %gather_weights.1 = (bf16[256,3072]{1,0:T(8,128)(2,1)}, bf16[256,2048]{1,0:T(8,128)(2,1)}, bf16[1024,2048]{1,0:T(8,128)(2,1)}, bf16[8192,1280]{1,0:T(8,128)(2,1)...) custom-call(bf16[256,2048]{1,0:T(8,128)(2,1)} %fusion.4.refs_0_, ...), custom_call_target="tpu_custom_call" | custom-call | tf_op jit(solution)/shard_map/gather_weights/pallas_call | solution.py:1406
  319.5 3.4 fusion.19
  326.6 18.2 %convolution_convert_fusion.q.k.v.refs_0_ = bf16[1024,3072]{1,0:T(8,128)(2,1)} fusion(bf16[1024,2048]{1,0:T(8,128)(2,1)S(1)} %copy-done.9, bf16[2048,3072]{1,0:T(8,128)(2,1)} %get-tuple-element.46.refs_1_), kind=kOutput, calls=%fused_computation | convolution fusion | flops 12888047616 | bytes 23068672 | tf_op jit(solution)/shard_map/dot_general | solution.py:2161
  344.9 29.2 %attention.1 = (bf16[1024,2048]{1,0:T(8,128)(2,1)S(1)}, f32[1024,1024]{1,0:T(8,128)}) custom-call(s32[1]{0:T(128)S(6)} %copy.75.prefix, bf16[1024,3072]{1,0:T(8,128)(2,1)} %convolution_convert_fusion.q.k.v.refs_0_, bf16[1024,3072]{1,0:T(8,128)(2,1)} %convolution_convert_fusion.q.k.v.refs_0_, bf16[1024,3072]{1,0:T(8,128)(2,1)} %convolution_convert_fusion.q.k.v.refs_0_, ...), custom_call_target="tpu_custom_call" | custom-call | tf_op jit(solution)/shard_map/attention/pallas_call | solution.py:1495
  376.1 10.3 convolution_convert_fusion.2.source
  386.4 46.3 %sum_attention.1 = f32[256,2048]{1,0:T(8,128)} custom-call(bf16[1024,2048]{1,0:T(8,128)(2,1)} %convolution_convert_fusion.2.source), custom_call_target="tpu_custom_call" | custom-call | tf_op jit(solution)/shard_map/sum_attention/pallas_call | solution.py:1120
  435.1 2.2 multiply_reduce_fusion.2
  439.9 244.1 %feed_forward.1 = (bf16[8192,2048]{1,0:T(8,128)(2,1)}, bf16[8192,2048]{1,0:T(8,128)(2,1)}, bf16[5120,2048]{1,0:T(8,128)(2,1)}, bf16[5120,2048]{1,0:T(8,128)(2,1)...) custom-call(bf16[256,2048]{1,0:T(8,128)(2,1)} %copy-done.11, ...), custom_call_target="tpu_custom_call" | custom-call | tf_op jit(solution)/shard_map/feed_forward/pallas_call | solution.py:2050
  685.6 157.3 %sum_rows.1 = (f32[256,2048]{1,0:T(8,128)}, f32[704,2048]{1,0:T(8,128)}, f32[704,2048]{1,0:T(8,128)}, f32[704,2048]{1,0:T(8,128)}) custom-call(bf16[8192,2048]{1,0:T(8,128)(2,1)} %get-tuple-element.53.source, bf16[5120,1536]{1,0:T(8,128)(2,1)} %get-tuple-element.54.refs_0_, bf16[5120,2048]{1,0:T(8,128)(2,1)} %get-tuple-element.55.refs_1_, ...), custom_call_target="tpu_custom_call" | custom-call | tf_op jit(solution)/shard_map/sum_rows/pallas_call | solution.py:1120
  843.8 4.0 multiply_reduce_fusion
  851.0 61.9 %gather_cotangents.1 = (bf16[1024,2048]{1,0:T(8,128)(2,1)}, bf16[8192,2048]{1,0:T(8,128)(2,1)}) custom-call(bf16[256,2048]{1,0:T(8,128)(2,1)S(1)} %fusion.28.refs_0_, bf16[5120,768]{1,0:T(8,128)(2,1)} %get-tuple-element.56.refs_2_.refs_1_, bf16[704,2048]{1,0:T(8,128)(2,1)S(1)} %bitcast.89, s32[32,256]{1,0:T(8,128)S(1)} %copy-done.3), custom_call_target="tpu_custom_call" | custom-call | tf_op jit(solution)/shard_map/gather_cotangents/pallas_call | solution.py:632
  912.9 12.0 convolution_convert_fusion.1.refs_3_
  924.9 95.4 %sum_output_left.1 = (f32[256,1024]{1,0:T(8,128)}, bf16[1024,3072]{1,0:T(8,128)(2,1)}, f32[1024,128]{1,0:T(8,128)}, bf16[2048,2048]{1,0:T(8,128)(2,1)}) custom-call(bf16[8192,2048]{1,0:T(8,128)(2,1)} %get-tuple-element.60.source, bf16[1024,3072]{1,0:T(8,128)(2,1)} %convolution_convert_fusion.q.k.v.refs_0_, f32[1024,128]{1,0:T(8,128)} %copy-done.1, ...), custom_call_target="tpu_custom_call" | custom-call | tf_op jit(solution)/shard_map/sum_output_left/pallas_call | solution.py:1120
  1020.4 90.7 %sum_output_right.1 = (f32[256,1024]{1,0:T(8,128)}, bf16[1024,2176]{1,0:T(8,128)(2,1)}) custom-call(bf16[8192,2048]{1,0:T(8,128)(2,1)} %get-tuple-element.60.source, bf16[1024,3072]{1,0:T(8,128)(2,1)} %get-tuple-element.64.refs_0_.refs_1_, bf16[2048,3072]{1,0:T(8,128)(2,1)} %get-tuple-element.46.refs_1_, f32[1024,128]{1,0:T(8,128)} %get-tuple-element.65.refs_2_), custom_call_target="tpu_custom_call" | custom-call | tf_op jit(solution)/shard_map/sum_output_right/pallas_call | solution.py:1120
  1111.1 153.9 %sum_attention_back.1 = (f32[256,2176]{1,0:T(8,128)}, f32[256,2048]{1,0:T(8,128)}, bf16[2048,3072]{1,0:T(8,128)(2,1)}) custom-call(bf16[1024,2176]{1,0:T(8,128)(2,1)} %get-tuple-element.67.source, bf16[2048,2048]{1,0:T(8,128)(2,1)} %get-tuple-element.68.out_grad, bf16[1024,2048]{1,0:T(8,128)(2,1)} %get-tuple-element.45.refs_0_, ...), custom_call_target="tpu_custom_call" | custom-call | tf_op jit(solution)/shard_map/sum_attention_back/pallas_call | solution.py:1204
  1267.2 4.9 fusion.10
  1273.9 4.8 fusion.9
  1278.7 171.4 %sum_weights.1 = (f32[256,2048]{1,0:T(8,128)}, f32[256,4096]{1,0:T(8,128)}) custom-call(bf16[2048,3072]{1,0:T(8,128)(2,1)} %get-tuple-element.70.in_grad), custom_call_target="tpu_custom_call" | custom-call | tf_op jit(solution)/shard_map/sum_weights/pallas_call | solution.py:1305
  1452.8 4.9 copy.76
  1457.8 3.6 copy.77
  1462.7 2.9 copy.79
  1465.6 2.9 copy.80
  1469.6 2.5 copy.81
  (147 shorter events, 30.4 us)
Async XLA Ops:
  7.2 5.4 copy-start.19
  7.2 432.1 %all-gather.2.cloned.1.call-start = ((), (), s32[]{:S(2)}) async-start(), calls=%async_computation | async-start | bytes 12976128 | tf_op jit(solution)/shard_map/all_gather | solution.py:2152
  11.4 306.8 %copy-start.22 = (f32[256]{0:T(256)}, f32[256]{0:T(256)S(1)}, u32[]{:S(2)}) copy-start(f32[256]{0:T(256)S(1)} %add_rsqrt_fusion.1) | copy-start | bytes 3076
  13.9 305.2 %copy-start.25 = (s32[1,1024,2]{1,2,0:T(2,128)S(1)}, s32[1,1024,2]{1,2,0:T(2,128)}, u32[]{:S(2)}) copy-start(s32[1,1024,2]{1,2,0:T(2,128)} %param.16) | copy-start | bytes 24580
  318.3 524.7 %all-reduce.8.cloned.1.call-start = ((), (), s32[]{:S(2)}) async-start(), calls=%async_computation.2 | async-start | bytes 262144
  325.0 51.1 %slice-start.6 = ((s8[8388608]{0:T(1024)(128)(4,1)}), s8[4194304]{0:T(1024)(128)(4,1)S(1)}, s32[]{:S(2)}) async-start(s8[8388608]{0:T(1024)(128)(4,1)} %bitcast.116), calls=%async_computation.9 | async-start | bytes 8388608
  325.3 19.6 %copy-start.1 = (f32[1024,128]{1,0:T(8,128)}, f32[1024,128]{1,0:T(8,128)S(1)}, u32[]{:S(2)}) copy-start(f32[1024,128]{1,0:T(8,128)S(1)} %pad.8.side.refs_1_) | copy-start | bytes 1572868
  326.6 49.5 %slice-start.7 = ((s8[8388608]{0:T(1024)(128)(4,1)}), s8[4194304]{0:T(1024)(128)(4,1)S(1)}, s32[]{:S(2)}) async-start(s8[8388608]{0:T(1024)(128)(4,1)} %bitcast.116), calls=%async_computation.10 | async-start | bytes 8388608
  386.4 46.3 %copy-start.21 = (bf16[128,128]{1,0:T(8,128)(2,1)S(1)}, bf16[128,128]{1,0:T(8,128)(2,1)}, u32[]{:S(2)}) copy-start(bf16[128,128]{1,0:T(8,128)(2,1)} %get-tuple-element.52) | copy-start | bytes 98308
  685.5 764.6 %all-reduce.6.cloned.1.call-start = ((), (), s32[]{:S(2)}) async-start(), calls=%async_computation.1 | async-start | bytes 262144 | tf_op jit(solution)/shard_map/psum | solution.py:2286
  843.8 5.4 copy-start.5
  843.8 5.4 copy-start.13
  849.2 63.7 %slice-start.8 = ((s8[8388608]{0:T(1024)(128)(4,1)}), s8[4194304]{0:T(1024)(128)(4,1)S(1)}, s32[]{:S(2)}) async-start(s8[8388608]{0:T(1024)(128)(4,1)} %bitcast.118), calls=%async_computation.11 | async-start | bytes 8388608
  851.0 61.9 %slice-start.9 = ((s8[8388608]{0:T(1024)(128)(4,1)}), s8[4194304]{0:T(1024)(128)(4,1)S(1)}, s32[]{:S(2)}) async-start(s8[8388608]{0:T(1024)(128)(4,1)} %bitcast.118), calls=%async_computation.12 | async-start | bytes 8388608
  1111.1 154.0 %copy-start.16 = (f32[1024,2]{1,0:T(8,128)S(1)}, f32[1024,2]{1,0:T(8,128)}, u32[]{:S(2)}) copy-start(f32[1024,2]{1,0:T(8,128)} %copy-done.15) | copy-start | bytes 24580
  1111.1 156.1 %copy-start.20 = (f32[2048]{0:T(1024)S(1)}, f32[2048]{0:T(1024)}, u32[]{:S(2)}) copy-start(f32[2048]{0:T(1024)} %param.19) | copy-start | bytes 24580
  1111.1 156.1 %copy-start.23 = (f32[256]{0:T(256)S(1)}, f32[256]{0:T(256)}, u32[]{:S(2)}) copy-start(f32[256]{0:T(256)} %copy-done.22) | copy-start | bytes 3076
  1267.2 4.9 copy-start.14
  1267.2 5.5 copy-start.12
  1267.2 6.7 copy-start.8
  1452.8 9.8 slice-start.4
  1452.8 12.8 slice-start.2
  1457.8 4.9 slice-start.5
  1462.7 5.8 slice-start
  (16 other events, 42.8 us)
Sparse Core Ops, SparseCore 0:
  318.4 107.7 all-gather.1
  685.7 124.3 all-reduce.7
  1274.0 126.3 all-reduce.5

commit v9 on v8

--- a/solution.py
+++ b/solution.py
@@ -1142,12 +1142,10 @@
     rooms, refs = refs[:count], refs[count:]
     count = len(scatter_rooms(rows, 128, out_pieces[0][2]))
     out_rooms, refs = refs[:count], refs[count:]
-    dealt, send_sems, deal_sems = refs[:3]
-    sems, out_sems, own = refs[3:6], refs[6:9], refs[9:]
+    send_sems = refs[0]
+    sems, out_sems, own = refs[1:4], refs[4:7], refs[7:]
     place = Place()
     post = Post(send_sems, place)
-    z, e = place.at["z"], place.expert
-    partner, moves = (e * 2 + place.at["y"], z), z != e
     loads, works, finish = scatter_plan(
         "expert", rows, pieces, place, post, source, rooms, sems
     )
@@ -1156,7 +1154,7 @@
     )
     for load in loads + out_loads:
         load.start()
-    enter(place, "cxyz", [(partner, moves)])
+    enter(place, "cxyz")
     steps = filler.start(given, made, own)
     times = sorted({time for time, _ in works + out_works})
     turns = [time for time in times if time >= 0]
@@ -1172,24 +1170,11 @@
             done = share
     for p in range(len(out_pieces)):
         first, length, _ = out_pieces[p]
-        at = pl.ds(first, length)
-        post.send(out_finish(p), dealt.at[at], deal_sems.at[p], partner, moves)
+        output[pl.ds(first, length), :] = out_finish(p)[...]
     for p in range(len(pieces)):
         first, length, _ = pieces[p]
         widen(result.at[pl.ds(first, length)], finish(p), length)
     filler.end(given, made, own)
-    for p in range(len(out_pieces)):
-        first, length, _ = out_pieces[p]
-        at = pl.ds(first, length)
-
-        def came(p=p, at=at, length=length):
-            post.arrived(dealt.at[at], deal_sems.at[p])
-            widen(output.at[at], dealt.at[at], length)
-
-        pl.when(moves)(came)
-        pl.when(~moves)(
-            lambda at=at, length=length: widen(output.at[at], out_rooms[0].at[z, at], length)
-        )
     post.close()
 
 
@@ -1200,14 +1185,14 @@
     hbm = pl.BlockSpec(memory_space=pltpu.HBM)
     vmem = pl.BlockSpec(memory_space=pltpu.VMEM)
     shape = jax.ShapeDtypeStruct
-    sends = sends_of(order, len(pieces)) + sends_of(out_order, len(out_pieces)) + len(out_pieces)
+    sends = sends_of(order, len(pieces)) + sends_of(out_order, len(out_pieces))
     return pl.pallas_call(
         functools.partial(
             sum_with_output_kernel, rows, pieces, out_rows, out_pieces, filler
         ),
         out_shape=[
             shape((rows, width), jnp.float32),
-            shape((out_rows, out_width), jnp.float32),
+            shape((out_rows, out_width), jnp.bfloat16),
         ]
         + filler.shapes,
         in_specs=[hbm] * (2 + len(operands)),
@@ -1215,9 +1200,7 @@
         scratch_shapes=scatter_rooms(rows, width, order)
         + scatter_rooms(out_rows, out_width, out_order)
         + [
-            pltpu.VMEM((out_rows, out_width), jnp.bfloat16),
             pltpu.SemaphoreType.DMA((sends,)),
-            pltpu.SemaphoreType.DMA((len(out_pieces),)),
         ]
         + scatter_sems(order, len(pieces))
         + scatter_sems(out_order, len(out_pieces))
@@ -1229,10 +1212,10 @@
     )(array, out_grad, *operands)
 
 
-def sum_weights_kernel(rows, pieces, in_grad, query, keyvalue, *refs):
+def sum_weights_kernel(rows, pieces, in_grad, out_rows, query, keyvalue, output, *refs):
     count = len(scatter_rooms(rows, 128, pieces[0][2]))
     rooms = refs[:count]
-    dealt, shared, send_sems, deal_sems = refs[count : count + 4]
+    dealt, shared, out_dealt, send_sems, deal_sems = refs[count : count + 5]
     place = Place()
     post = Post(send_sems, place)
     z, e = place.at["z"], place.expert
@@ -1244,13 +1227,22 @@
         core = place.at["c"] + flip_c * (1 - 2 * place.at["c"])
         peers.append((x * 2 + core, flip_x * 2 + flip_c))
     loads, works, finish = scatter_plan(
-        "dp", rows, pieces, place, post, in_grad, rooms, refs[count + 4 :]
+        "dp", rows, pieces, place, post, in_grad, rooms, refs[count + 5 :]
     )
     for load in loads:
         load.start()
-    enter(place, "cxyz", [((place.dp, peers[0][0]), None)])
-    for _, act in works:
+    partner, moves = (e * 2 + place.at["y"], z), z != e
+    enter(place, "cxyz", [((place.dp, peers[0][0]), None), (partner, moves)])
+    stay = pltpu.make_async_copy(out_rows, out_dealt, deal_sems.at[0, 0])
+    pl.when(~moves)(stay.start)
+    for time, act in works:
+        if time == 0:
+            break
         act()
+    post.send(out_rows, out_dealt, deal_sems.at[0, 7], partner, moves)
+    for time, act in works:
+        if time >= 0:
+            act()
     cols = lambda block: pl.ds(pl.multiple_of(block * span, span), span)
     keep = slice(wide, wide + 2 * span)
     for p in range(len(pieces)):
@@ -1294,10 +1286,14 @@
             widen(query.at[at, cols(peer)], dealt.at[at, cols(peer)], length)
         post.arrived(shared.at[3, at], deal_sems.at[p, 6])
         place_keys(p, 3, shared.at[3, at])
+    pl.when(~moves)(stay.wait)
+    pl.when(moves)(lambda: post.arrived(out_dealt, deal_sems.at[0, 7]))
+    widen(output, out_dealt, rows)
     post.close()
 
 
-def sum_weights(in_grad, wide, pieces, collective_id):
+def sum_weights(in_grad, out_rows, pieces, collective_id):
+    wide = out_rows.shape[1]
     rows, total = in_grad.shape[0] // 8, in_grad.shape[1]
     order, count = pieces[0][2], len(pieces)
     vmem = pl.BlockSpec(memory_space=pltpu.VMEM)
@@ -1307,22 +1303,24 @@
         out_shape=[
             shape((rows, wide), jnp.float32),
             shape((rows, 2 * wide), jnp.float32),
+            shape((rows, wide), jnp.float32),
         ],
-        in_specs=[pl.BlockSpec(memory_space=pltpu.HBM)],
-        out_specs=[vmem] * 2,
+        in_specs=[pl.BlockSpec(memory_space=pltpu.HBM)] * 2,
+        out_specs=[vmem] * 3,
         scratch_shapes=scatter_rooms(rows, total, order)
         + [
             pltpu.VMEM((rows, wide), jnp.bfloat16),
             pltpu.VMEM((4, rows, total - wide), jnp.bfloat16),
-            pltpu.SemaphoreType.DMA((sends_of(order, count) + 7 * count,)),
-            pltpu.SemaphoreType.DMA((count, 7)),
+            pltpu.VMEM((rows, wide), jnp.bfloat16),
+            pltpu.SemaphoreType.DMA((sends_of(order, count) + 7 * count + 1,)),
+            pltpu.SemaphoreType.DMA((count, 8)),
         ]
         + scatter_sems(order, count),
         compiler_params=pltpu.CompilerParams(
             collective_id=collective_id, has_side_effects=True, vmem_limit_bytes=63 * 2**20
         ),
         name="sum_weights",
-    )(in_grad)
+    )(in_grad, out_rows)
 
 
 def weights_kernel(jobs, *refs):
@@ -2251,7 +2249,7 @@
         (dprojected, in_weight, gate_parts),
         (columns, model_width - columns),
     )
-    attend_home, grad_projection, grad_in = sum_with_output(
+    attend_home, out_rows, grad_in = sum_with_output(
         attend_dx,
         quarters("cx"),
         grad_out,
@@ -2286,7 +2284,9 @@
     small = lax.psum(small.astype(f32), ("dp", "expert"))
     small = lax.dynamic_slice_in_dim(small, lax.axis_index("dp") * rows_in, rows_in, 1)
 
-    grad_query, grad_keyvalue = sum_weights(grad_in, query_width, ((0, rows_in, "yz"),), 6)
+    grad_query, grad_keyvalue, grad_projection = sum_weights(
+        grad_in, out_rows, ((0, rows_in, "yz"),), 6
+    )
     return (
         layer_output.astype(low)[None],
         grad_tokens[None],

time: 1490 us -> 1440 us (0.966)
  Pallas kernels: 1350 us -> 1310 us
    pallas_call x1, Pallas kernels: 154 us -> 106 us  [sum_with_output(): pl.pallas_call(functools.partial(sum_with_output_kernel, rows, pieces, ou...]
  transfers between devices with their start and end apart: 3 -> 3, of which waited for: 0 -> 0; matrix products, arithmetic and copies ran while one was open for 3% -> 3% of each run, Pallas kernels for 27% -> 28%
where the time goes in v9:
time: 1440 us; the launch traced here: 1430 us
  Pallas kernels  1310 us (91%)
  matrix products  55 us (4%)
  local copies, waits for them, and re-layouts  40.2 us (3%)
  between operations  15.2 us (1%)
    pallas_call x4, Pallas kernels, scatter(): pl.pallas_call(functools.partial(scatter_kernel, whose, rows, pieces, col...  390 us
    pallas_call x1, Pallas kernels, gather_weights(): pl.pallas_call(functools.partial(weights_kernel, plan), out_shape=shards...  304 us
    pallas_call x1, Pallas kernels, feed(): pl.pallas_call(functools.partial(feed_kernel, tok, slot_count), in_specs=...  244 us
    pallas_call x1, Pallas kernels, sum_weights(): pl.pallas_call(functools.partial(sum_weights_kernel, rows, pieces), out_s...  174 us
    pallas_call x1, Pallas kernels, sum_with_output(): pl.pallas_call(functools.partial(sum_with_output_kernel, rows, pieces, ou...  106 us
    pallas_call x1, Pallas kernels, gather(): pl.pallas_call(functools.partial(gather_kernel, plan, axes, filler), out_...  61.9 us
    pallas_call x1, Pallas kernels, attention(): pl.pallas_call(functools.partial(attention_kernel, experts), grid=(length...  29.2 us
  transfers between devices with their start and end apart: 3, of which 0 were waited for; matrix products, arithmetic and copies ran while one was open for 3% of the time, Pallas kernels for 28%

profile of v9, /device:TPU:2, one launch (start us, length us, event | category | flops | bytes accessed | tf_op | source)
XLA Modules:
  0.0 1433.1 jit_solution(12547110398415483645)
XLA Ops:
  7.3 2.0 slice_bitcast_fusion.refs_1_
  13.9 304.3 %gather_weights.1 = (bf16[256,3072]{1,0:T(8,128)(2,1)}, bf16[256,2048]{1,0:T(8,128)(2,1)}, bf16[1024,2048]{1,0:T(8,128)(2,1)}, bf16[8192,1280]{1,0:T(8,128)(2,1)...) custom-call(bf16[256,2048]{1,0:T(8,128)(2,1)} %fusion.4.refs_0_, ...), custom_call_target="tpu_custom_call" | custom-call | tf_op jit(solution)/shard_map/gather_weights/pallas_call | solution.py:1404
  319.5 3.4 fusion.19
  326.6 18.2 %convolution_convert_fusion.q.k.v.refs_0_ = bf16[1024,3072]{1,0:T(8,128)(2,1)} fusion(bf16[1024,2048]{1,0:T(8,128)(2,1)S(1)} %copy-done.9, bf16[2048,3072]{1,0:T(8,128)(2,1)} %get-tuple-element.47.refs_1_), kind=kOutput, calls=%fused_computation | convolution fusion | flops 12888047616 | bytes 23068672 | tf_op jit(solution)/shard_map/dot_general | solution.py:2159
  344.9 29.2 %attention.1 = (bf16[1024,2048]{1,0:T(8,128)(2,1)S(1)}, f32[1024,1024]{1,0:T(8,128)}) custom-call(s32[1]{0:T(128)S(6)} %copy.75.prefix, bf16[1024,3072]{1,0:T(8,128)(2,1)} %convolution_convert_fusion.q.k.v.refs_0_, bf16[1024,3072]{1,0:T(8,128)(2,1)} %convolution_convert_fusion.q.k.v.refs_0_, bf16[1024,3072]{1,0:T(8,128)(2,1)} %convolution_convert_fusion.q.k.v.refs_0_, ...), custom_call_target="tpu_custom_call" | custom-call | tf_op jit(solution)/shard_map/attention/pallas_call | solution.py:1493
  376.1 10.3 convolution_convert_fusion.2.source
  386.4 46.3 %sum_attention.1 = f32[256,2048]{1,0:T(8,128)} custom-call(bf16[1024,2048]{1,0:T(8,128)(2,1)} %convolution_convert_fusion.2.source), custom_call_target="tpu_custom_call" | custom-call | tf_op jit(solution)/shard_map/sum_attention/pallas_call | solution.py:1120
  435.1 2.2 multiply_reduce_fusion.2
  439.9 244.1 %feed_forward.1 = (bf16[8192,2048]{1,0:T(8,128)(2,1)}, bf16[8192,2048]{1,0:T(8,128)(2,1)}, bf16[5120,2048]{1,0:T(8,128)(2,1)}, bf16[5120,2048]{1,0:T(8,128)(2,1)...) custom-call(bf16[256,2048]{1,0:T(8,128)(2,1)} %copy-done.11, ...), custom_call_target="tpu_custom_call" | custom-call | tf_op jit(solution)/shard_map/feed_forward/pallas_call | solution.py:2048
  685.6 157.3 %sum_rows.1 = (f32[256,2048]{1,0:T(8,128)}, f32[704,2048]{1,0:T(8,128)}, f32[704,2048]{1,0:T(8,128)}, f32[704,2048]{1,0:T(8,128)}) custom-call(bf16[8192,2048]{1,0:T(8,128)(2,1)} %get-tuple-element.54.source, bf16[5120,1536]{1,0:T(8,128)(2,1)} %get-tuple-element.55.refs_0_, bf16[5120,2048]{1,0:T(8,128)(2,1)} %get-tuple-element.56.refs_1_, ...), custom_call_target="tpu_custom_call" | custom-call | tf_op jit(solution)/shard_map/sum_rows/pallas_call | solution.py:1120
  843.8 4.0 multiply_reduce_fusion
  851.0 61.9 %gather_cotangents.1 = (bf16[1024,2048]{1,0:T(8,128)(2,1)}, bf16[8192,2048]{1,0:T(8,128)(2,1)}) custom-call(bf16[256,2048]{1,0:T(8,128)(2,1)S(1)} %fusion.28.refs_0_, bf16[5120,768]{1,0:T(8,128)(2,1)} %get-tuple-element.57.refs_2_.refs_1_, bf16[704,2048]{1,0:T(8,128)(2,1)S(1)} %bitcast.89, s32[32,256]{1,0:T(8,128)S(1)} %copy-done.3), custom_call_target="tpu_custom_call" | custom-call | tf_op jit(solution)/shard_map/gather_cotangents/pallas_call | solution.py:632
  912.9 12.0 convolution_convert_fusion.1.refs_3_
  924.9 95.4 %sum_output_left.1 = (f32[256,1024]{1,0:T(8,128)}, bf16[1024,3072]{1,0:T(8,128)(2,1)}, f32[1024,128]{1,0:T(8,128)}, bf16[2048,2048]{1,0:T(8,128)(2,1)}) custom-call(bf16[8192,2048]{1,0:T(8,128)(2,1)} %get-tuple-element.61.source, bf16[1024,3072]{1,0:T(8,128)(2,1)} %convolution_convert_fusion.q.k.v.refs_0_, f32[1024,128]{1,0:T(8,128)} %copy-done.1, ...), custom_call_target="tpu_custom_call" | custom-call | tf_op jit(solution)/shard_map/sum_output_left/pallas_call | solution.py:1120
  1020.4 90.7 %sum_output_right.1 = (f32[256,1024]{1,0:T(8,128)}, bf16[1024,2176]{1,0:T(8,128)(2,1)}) custom-call(bf16[8192,2048]{1,0:T(8,128)(2,1)} %get-tuple-element.61.source, bf16[1024,3072]{1,0:T(8,128)(2,1)} %get-tuple-element.65.refs_0_.refs_1_, bf16[2048,3072]{1,0:T(8,128)(2,1)} %get-tuple-element.47.refs_1_, f32[1024,128]{1,0:T(8,128)} %get-tuple-element.66.refs_2_), custom_call_target="tpu_custom_call" | custom-call | tf_op jit(solution)/shard_map/sum_output_right/pallas_call | solution.py:1120
  1111.1 106.0 %sum_attention_back.1 = (f32[256,2176]{1,0:T(8,128)}, bf16[256,2048]{1,0:T(8,128)(2,1)}, bf16[2048,3072]{1,0:T(8,128)(2,1)}) custom-call(bf16[1024,2176]{1,0:T(8,128)(2,1)} %get-tuple-element.68.source, bf16[2048,2048]{1,0:T(8,128)(2,1)} %get-tuple-element.69.out_grad, bf16[1024,2048]{1,0:T(8,128)(2,1)} %get-tuple-element.46.refs_0_, ...), custom_call_target="tpu_custom_call" | custom-call | tf_op jit(solution)/shard_map/sum_attention_back/pallas_call | solution.py:1189
  1219.3 4.9 fusion.10
  1226.0 4.8 fusion.9
  1230.8 173.5 %sum_weights.1 = (f32[256,2048]{1,0:T(8,128)}, f32[256,4096]{1,0:T(8,128)}, f32[256,2048]{1,0:T(8,128)}) custom-call(bf16[2048,3072]{1,0:T(8,128)(2,1)} %get-tuple-element.71.in_grad, bf16[256,2048]{1,0:T(8,128)(2,1)} %get-tuple-element.72.out_rows), custom_call_target="tpu_custom_call" | custom-call | tf_op jit(solution)/shard_map/sum_weights/pallas_call | solution.py:1301
  1407.1 4.9 copy.76
  1412.0 3.6 copy.77
  1416.9 2.9 copy.79
  1419.9 2.9 copy.80
  1423.8 2.5 copy.81
  (147 shorter events, 30.4 us)
Async XLA Ops:
  7.2 5.4 copy-start.19
  7.2 432.1 %all-gather.2.cloned.1.call-start = ((), (), s32[]{:S(2)}) async-start(), calls=%async_computation | async-start | bytes 12976128 | tf_op jit(solution)/shard_map/all_gather | solution.py:2150
  11.4 306.8 %copy-start.22 = (f32[256]{0:T(256)}, f32[256]{0:T(256)S(1)}, u32[]{:S(2)}) copy-start(f32[256]{0:T(256)S(1)} %add_rsqrt_fusion.1) | copy-start | bytes 3076
  13.9 305.2 %copy-start.25 = (s32[1,1024,2]{1,2,0:T(2,128)S(1)}, s32[1,1024,2]{1,2,0:T(2,128)}, u32[]{:S(2)}) copy-start(s32[1,1024,2]{1,2,0:T(2,128)} %param.16) | copy-start | bytes 24580
  318.3 524.7 %all-reduce.8.cloned.1.call-start = ((), (), s32[]{:S(2)}) async-start(), calls=%async_computation.2 | async-start | bytes 262144
  325.0 51.1 %slice-start.6 = ((s8[8388608]{0:T(1024)(128)(4,1)}), s8[4194304]{0:T(1024)(128)(4,1)S(1)}, s32[]{:S(2)}) async-start(s8[8388608]{0:T(1024)(128)(4,1)} %bitcast.116), calls=%async_computation.9 | async-start | bytes 8388608
  325.3 19.6 %copy-start.1 = (f32[1024,128]{1,0:T(8,128)}, f32[1024,128]{1,0:T(8,128)S(1)}, u32[]{:S(2)}) copy-start(f32[1024,128]{1,0:T(8,128)S(1)} %pad.8.side.refs_1_) | copy-start | bytes 1572868
  326.6 49.5 %slice-start.7 = ((s8[8388608]{0:T(1024)(128)(4,1)}), s8[4194304]{0:T(1024)(128)(4,1)S(1)}, s32[]{:S(2)}) async-start(s8[8388608]{0:T(1024)(128)(4,1)} %bitcast.116), calls=%async_computation.10 | async-start | bytes 8388608
  386.4 46.3 %copy-start.21 = (bf16[128,128]{1,0:T(8,128)(2,1)S(1)}, bf16[128,128]{1,0:T(8,128)(2,1)}, u32[]{:S(2)}) copy-start(bf16[128,128]{1,0:T(8,128)(2,1)} %get-tuple-element.53) | copy-start | bytes 98308
  685.5 718.8 %all-reduce.6.cloned.1.call-start = ((), (), s32[]{:S(2)}) async-start(), calls=%async_computation.1 | async-start | bytes 262144 | tf_op jit(solution)/shard_map/psum | solution.py:2284
  843.8 5.4 copy-start.5
  843.8 5.4 copy-start.13
  849.2 63.7 %slice-start.8 = ((s8[8388608]{0:T(1024)(128)(4,1)}), s8[4194304]{0:T(1024)(128)(4,1)S(1)}, s32[]{:S(2)}) async-start(s8[8388608]{0:T(1024)(128)(4,1)} %bitcast.118), calls=%async_computation.11 | async-start | bytes 8388608
  851.0 61.9 %slice-start.9 = ((s8[8388608]{0:T(1024)(128)(4,1)}), s8[4194304]{0:T(1024)(128)(4,1)S(1)}, s32[]{:S(2)}) async-start(s8[8388608]{0:T(1024)(128)(4,1)} %bitcast.118), calls=%async_computation.12 | async-start | bytes 8388608
  1111.1 106.0 %copy-start.16 = (f32[1024,2]{1,0:T(8,128)S(1)}, f32[1024,2]{1,0:T(8,128)}, u32[]{:S(2)}) copy-start(f32[1024,2]{1,0:T(8,128)} %copy-done.15) | copy-start | bytes 24580
  1111.1 108.2 %copy-start.20 = (f32[2048]{0:T(1024)S(1)}, f32[2048]{0:T(1024)}, u32[]{:S(2)}) copy-start(f32[2048]{0:T(1024)} %param.19) | copy-start | bytes 24580
  1111.1 108.2 %copy-start.23 = (f32[256]{0:T(256)S(1)}, f32[256]{0:T(256)}, u32[]{:S(2)}) copy-start(f32[256]{0:T(256)} %copy-done.22) | copy-start | bytes 3076
  1219.3 4.9 copy-start.14
  1219.3 5.5 copy-start.12
  1219.3 6.7 copy-start.8
  1407.1 9.8 slice-start.4
  1407.1 12.8 slice-start.2
  1412.0 4.9 slice-start.5
  1416.9 5.8 slice-start
  (16 other events, 42.8 us)
Sparse Core Ops, SparseCore 0:
  318.4 107.7 all-gather.1
  685.7 124.3 all-reduce.7
  1226.1 143.3 all-reduce.5
